TPU v7x, 32 devices: a whole 2x2x4 slice. The times are simulated.
32 devices in a mesh: fsdp: 8 (over z, core), tensor: 4 (over y, x).
Axes of the slice: x: 2, y: 2, z: 4, core: 2. Of those that a mesh axis runs over, the one named last changes fastest.
Arguments:
- inputs: bfloat16 [2, 4, 1024, 2048], P(None, 'tensor', 'fsdp'), may hold values from -6 to 6
- out_grads: bfloat16 [2, 4, 1024, 2048], P(None, 'tensor', 'fsdp'), may hold values from -6 to 6
- prefix_len: int32 [2, 4], replicated, may hold values from 102 to 512
- positions: int32 [2, 4, 1024], P(None, None, 'fsdp'), may hold values from 0 to 1535, as said below
- attn_gain: bfloat16 [2048], P('fsdp'), may hold values from 0.5 to 1.5
- w_query: bfloat16 [2048, 2048], P('fsdp', 'tensor'), may hold values from -0.1875 to 0.1875
- w_key: bfloat16 [2048, 2048], P('fsdp', 'tensor'), may hold values from -0.1875 to 0.1875
- w_value: bfloat16 [2048, 2048], P('fsdp', 'tensor'), may hold values from -0.125 to 0.125
- w_out: bfloat16 [2048, 2048], P('fsdp', 'tensor'), may hold values from -0.75 to 0.75
- mlp_gain: bfloat16 [2048], P('fsdp'), may hold values from 0.5 to 1.5
- w_gate: bfloat16 [2048, 8192], P('fsdp', 'tensor'), may hold values from -0.125 to 0.125
- w_up: bfloat16 [2048, 8192], P('fsdp', 'tensor'), may hold values from -0.125 to 0.125
- w_down: bfloat16 [2048, 8192], P('fsdp', 'tensor'), may hold values from -0.09375 to 0.09375
Outputs:
- output: bfloat16 [2, 4, 1024, 2048], P(None, 'tensor', 'fsdp')
- input_grad: float32 [2, 4, 1024, 2048], P(None, 'tensor', 'fsdp')
- attn_gain_grad: float32 [2048], P('fsdp')
- w_query_grad: float32 [2048, 2048], P('fsdp', 'tensor')
- w_key_grad: float32 [2048, 2048], P('fsdp', 'tensor')
- w_value_grad: float32 [2048, 2048], P('fsdp', 'tensor')
- w_out_grad: float32 [2048, 2048], P('fsdp', 'tensor')
- mlp_gain_grad: float32 [2048], P('fsdp')
- w_gate_grad: float32 [2048, 8192], P('fsdp', 'tensor')
- w_up_grad: float32 [2048, 8192], P('fsdp', 'tensor')
- w_down_grad: float32 [2048, 8192], P('fsdp', 'tensor')
- rms_stats: float32 [2, 4, 3], P(None, 'tensor')
Inputs may be any that keep to these rules, and one draw needn't show every extreme that they name: Within each sequence positions start at 0 and rise by 1 or 2 from token to token, by 2 at exactly 512 of the steps, so every sequence ends at the max.
All inputs are finite; a program needn't handle non-finite values.
Results may differ from a plain program's by a relative error of at most 0.023.
Values may be sent and summed in bfloat16 or wider, within the bound.
No kernel may reach another device: no remote copies, remote signals or barrier semaphores. Data moves between devices by JAX's collectives and lax.ppermute only.
A program may use at most 192 MiB of HBM per device.

v0:
```python
import math

import jax
import jax.numpy as jnp
from jax import lax
from jax.experimental import pallas as pl
from jax.experimental.pallas import tpu as pltpu
from jax.sharding import PartitionSpec as P

HEAD_DIM = 64

rope_base = 130000.0
norm_eps = 1e-05
stat_eps = 1e-06
LOG2E = math.log2(math.e)
MASKED = -1e30
PAIR = 2
BF16 = jnp.bfloat16
F32 = jnp.float32


def dot(left, right, left_dim, right_dim):
    return lax.dot_general(
        left, right, (((left_dim,), (right_dim,)), ((), ())), preferred_element_type=F32
    )


def normalize(values):
    row_scale = lax.rsqrt(jnp.mean(values * values, axis=-1, keepdims=True) + norm_eps)
    return (values * row_scale, row_scale)


def norm_back(grad_in, unit_rows, row_scale, gain):
    scaled = grad_in * gain
    inner_mean = jnp.mean(scaled * unit_rows, axis=-1, keepdims=True)
    return (
        row_scale * (scaled - unit_rows * inner_mean),
        jnp.sum(grad_in * unit_rows, axis=tuple(range(grad_in.ndim - 1))),
    )


def rotate(values, cos_tab, sin_tab, rot_sign):
    first_half = values[..., 0, :, :]
    second = values[..., 1, :, :]
    return jnp.stack(
        [
            first_half * cos_tab - rot_sign * second * sin_tab,
            second * cos_tab + rot_sign * first_half * sin_tab,
        ],
        axis=-3,
    )


def swap(value, axis, distance):
    count = lax.axis_size(axis)
    return lax.ppermute(value, axis, [(a, a ^ distance) for a in range(count)])


def after(value, *others):
    return lax.optimization_barrier((value, others))[0]


def spread(value, direct=True):
    count = lax.axis_size("tensor")
    if direct or count != 4:
        return [value] + [swap(value, "tensor", k) for k in range(1, count)]
    half = value.shape[0] // 2
    one = swap(value, "tensor", 1)
    two = swap(value, "tensor", 2)
    low = swap(two[:half], "tensor", 1)
    high = swap(one[half:], "tensor", 2)
    return [value, one, two, jnp.concatenate([low, high], axis=0)]


def collect(parts, direct=True, token=None):
    count = lax.axis_size("tensor")
    if direct or count != 4:
        blocks = [swap(parts[k].astype(BF16), "tensor", k) for k in range(1, count)]
        if token is not None:
            blocks = after(blocks, token)
        total = parts[0]
        for block in blocks:
            total = total + block.astype(F32)
        return total
    half = parts[0].shape[0] // 2
    far = parts[3].astype(BF16)
    low = swap(far[:half], "tensor", 1).astype(F32)
    high = swap(far[half:], "tensor", 2).astype(F32)
    one = jnp.concatenate([parts[1][:half], parts[1][half:] + high], axis=0)
    two = jnp.concatenate([parts[2][:half] + low, parts[2][half:]], axis=0)
    one = swap(one.astype(BF16), "tensor", 1).astype(F32)
    two = swap(two.astype(BF16), "tensor", 2).astype(F32)
    return parts[0] + one + two


def pair_join(value, micros):
    other = swap(value, "fsdp", PAIR)
    size = value.shape[0] // micros
    parts = [v[m * size : (m + 1) * size] for m in range(micros) for v in (value, other)]
    return jnp.concatenate(parts, axis=0)


def gather_rows(blocks, micros):
    size = blocks[0].shape[0] // micros
    return jnp.concatenate(
        [b[m * size : (m + 1) * size] for m in range(micros) for b in blocks], axis=0
    )


def peer_blocks(rows, micros, peers):
    size = rows.shape[0] // (micros * peers)
    return [
        jnp.concatenate(
            [rows[(m * peers + k) * size : (m * peers + k + 1) * size] for m in range(micros)],
            axis=0,
        )
        for k in range(peers)
    ]


def paired(values):
    count = lax.axis_size("fsdp")
    size = values.shape[-1] // count
    order = [(f & ~3) | ((f & 1) << 1) | ((f >> 1) & 1) for f in range(count)]
    parts = [lax.slice_in_dim(values, f * size, (f + 1) * size, axis=-1) for f in order]
    return jnp.concatenate(parts, axis=-1)


def pair_groups():
    count = lax.axis_size("fsdp")
    return [[f for f in range(count) if bool(f & PAIR) == side] for side in (False, True)]


def half_of(shards, side):
    half = shards[0].shape[1] // 2
    return jnp.concatenate(
        [lax.dynamic_slice_in_dim(s, side * half, half, 1) for s in shards], axis=1
    )


def order_pair(side, mine, other):
    return jnp.where(side == 0, mine, other), jnp.where(side == 0, other, mine)


def own_half(side, mine, other):
    return jnp.concatenate(order_pair(side, mine, other), axis=0)


def gather_half(shard):
    return lax.all_gather(
        shard,
        "fsdp",
        axis=0,
        tiled=True,
        axis_index_groups=pair_groups(),
    )


def scatter_half(grad):
    return lax.psum_scatter(
        grad, "fsdp", scatter_dimension=0, tiled=True, axis_index_groups=pair_groups()
    )


def settle_half(part, side, pieces, token):
    rows = part.shape[0] // 2
    mine = lax.dynamic_slice_in_dim(part, side * rows, rows, 0)
    other = swap(lax.dynamic_slice_in_dim(part, (1 - side) * rows, rows, 0), "fsdp", PAIR)
    low, high = order_pair(side, mine, after(other, token))
    half = part.shape[1] // pieces
    return [
        jnp.concatenate(
            [low[:, i * half : (i + 1) * half], high[:, i * half : (i + 1) * half]], axis=1
        ).astype(F32)
        for i in range(pieces)
    ]


def tree_sum(value, axis):
    step = 1
    while step < lax.axis_size(axis):
        value = value + swap(value, axis, step)
        step *= 2
    return value


def span_block(ref, first, count, lo, hi):
    return jnp.concatenate([ref[first + i, 0, lo:hi, :] for i in range(count)], axis=1)


def attn_blocks(spans, span_len):
    group = max(1, min(spans, 256 // span_len))
    while spans % group:
        group -= 1
    return group, spans // group


def key_count(q_block, block, prefix, blocks):
    return jnp.minimum(jnp.maximum(q_block + 1, (prefix + block - 1) // block), blocks)


def allowed_mask(k_block, q_block, block, prefix):
    key_id = k_block * block + lax.broadcasted_iota(jnp.int32, (block, block), 0)
    query_id = q_block * block + lax.broadcasted_iota(jnp.int32, (block, block), 1)
    return (key_id <= query_id) | (key_id < prefix)


def forward_kernel(prefix_ref, x_ref, out_ref, lse_ref, key_ref):
    spans, _, _, span_len = x_ref.shape
    group, blocks = attn_blocks(spans, span_len)
    block = group * span_len
    prefix = prefix_ref[pl.program_id(0)]
    coef = HEAD_DIM**-0.5 * LOG2E
    for kb in range(blocks):
        key_ref[pl.ds(kb * block, block), :] = span_block(
            x_ref, kb * group, group, HEAD_DIM, 2 * HEAD_DIM
        ).T
    for qb in range(blocks):
        q_t = span_block(x_ref, qb * group, group, 0, HEAD_DIM)

        def step(kb, carry):
            top, total, acc = carry
            keys = key_ref[pl.ds(pl.multiple_of(kb * block, block), block), :]
            scores = dot(keys, q_t, 1, 0) * coef
            scores = jnp.where(allowed_mask(kb, qb, block, prefix), scores, MASKED)
            new_top = jnp.maximum(top, jnp.max(scores, axis=0, keepdims=True))
            probs = jnp.exp2(scores - new_top)
            shrink = jnp.exp2(top - new_top)
            total = shrink * total + jnp.sum(probs, axis=0, keepdims=True)
            v_t = span_block(x_ref, kb * group, group, 2 * HEAD_DIM, 3 * HEAD_DIM)
            acc = shrink * acc + dot(v_t, probs.astype(BF16), 1, 0)
            return new_top, total, acc

        top, total, acc = lax.fori_loop(
            0,
            key_count(qb, block, prefix, blocks),
            step,
            (
                jnp.full((1, block), MASKED, F32),
                jnp.zeros((1, block), F32),
                jnp.zeros((HEAD_DIM, block), F32),
            ),
        )
        out = (acc / total).astype(BF16)
        for i in range(group):
            out_ref[qb * group + i, 0] = out[:, i * span_len : (i + 1) * span_len]
        lse_ref[0, :, qb * block : (qb + 1) * block] = top + jnp.log2(total)


def backward_kernel(
    prefix_ref, x_ref, o_ref, do_ref, lse_ref, dx_ref, key_ref, val_ref, dk_ref, dv_ref
):
    spans, _, _, span_len = x_ref.shape
    group, blocks = attn_blocks(spans, span_len)
    block = group * span_len
    prefix = prefix_ref[pl.program_id(0)]
    scale = HEAD_DIM**-0.5
    coef = scale * LOG2E
    for kb in range(blocks):
        rows = pl.ds(kb * block, block)
        key_ref[rows, :] = span_block(x_ref, kb * group, group, HEAD_DIM, 2 * HEAD_DIM).T
        val_ref[rows, :] = span_block(x_ref, kb * group, group, 2 * HEAD_DIM, 3 * HEAD_DIM).T
    dk_ref[...] = jnp.zeros_like(dk_ref)
    dv_ref[...] = jnp.zeros_like(dv_ref)
    for qb in range(blocks):
        q_t = span_block(x_ref, qb * group, group, 0, HEAD_DIM)
        do_t = span_block(do_ref, qb * group, group, 0, HEAD_DIM)
        o_t = span_block(o_ref, qb * group, group, 0, HEAD_DIM)
        delta = jnp.sum(do_t.astype(F32) * o_t.astype(F32), axis=0, keepdims=True)
        lse = lse_ref[0, :, qb * block : (qb + 1) * block]

        def step(kb, dq):
            rows = pl.ds(pl.multiple_of(kb * block, block), block)
            scores = dot(key_ref[rows, :], q_t, 1, 0) * coef
            scores = jnp.where(allowed_mask(kb, qb, block, prefix), scores, MASKED)
            probs = jnp.exp2(scores - lse)
            grad_probs = dot(val_ref[rows, :], do_t, 1, 0)
            grad_scores = (probs * (grad_probs - delta)).astype(BF16)
            dv_ref[kb] += dot(do_t, probs.astype(BF16), 1, 1)
            dk_ref[kb] += dot(q_t, grad_scores, 1, 1)
            k_t = span_block(x_ref, kb * group, group, HEAD_DIM, 2 * HEAD_DIM)
            return dq + dot(k_t, grad_scores, 1, 0)

        dq = lax.fori_loop(
            0,
            key_count(qb, block, prefix, blocks),
            step,
            jnp.zeros((HEAD_DIM, block), F32),
        )
        dq = (dq * scale).astype(BF16)
        for i in range(group):
            dx_ref[qb * group + i, 0, :HEAD_DIM, :] = dq[:, i * span_len : (i + 1) * span_len]
    for kb in range(blocks):
        dk = (dk_ref[kb] * scale).astype(BF16)
        dv = dv_ref[kb].astype(BF16)
        for i in range(group):
            cols = slice(i * span_len, (i + 1) * span_len)
            dx_ref[kb * group + i, 0, HEAD_DIM : 2 * HEAD_DIM, :] = dk[:, cols]
            dx_ref[kb * group + i, 0, 2 * HEAD_DIM :, :] = dv[:, cols]


def pair_spec(shape, first=0):
    return pl.BlockSpec((shape[0], 1) + shape[2:], lambda p, pre: (0, first + p, 0, 0))


def lse_spec(tokens):
    return pl.BlockSpec((1, 1, tokens), lambda p, pre: (p, 0, 0))


def attend_forward(prefix, packed, micro):
    spans, _, _, span_len = packed.shape
    pairs = prefix.shape[0]
    tokens = spans * span_len
    out_shape = (spans, pairs, HEAD_DIM, span_len)
    return pl.pallas_call(
        forward_kernel,
        out_shape=(
            jax.ShapeDtypeStruct(out_shape, BF16),
            jax.ShapeDtypeStruct((pairs, 1, tokens), F32),
        ),
        grid_spec=pltpu.PrefetchScalarGridSpec(
            num_scalar_prefetch=1,
            grid=(pairs,),
            in_specs=[pair_spec(packed.shape, micro * pairs)],
            out_specs=[pair_spec(out_shape), lse_spec(tokens)],
            scratch_shapes=[pltpu.VMEM((tokens, HEAD_DIM), BF16)],
        ),
        compiler_params=pltpu.CompilerParams(dimension_semantics=("arbitrary",)),
        name="attend_forward",
    )(prefix, packed)


def attend_back(prefix, packed, out, grad_out, lse, micro):
    spans, _, width, span_len = packed.shape
    pairs = prefix.shape[0]
    grad_shape = (spans, pairs, width, span_len)
    tokens = spans * span_len
    group, blocks = attn_blocks(spans, span_len)
    acc = pltpu.VMEM((blocks, HEAD_DIM, group * span_len), F32)
    return pl.pallas_call(
        backward_kernel,
        out_shape=jax.ShapeDtypeStruct(grad_shape, BF16),
        grid_spec=pltpu.PrefetchScalarGridSpec(
            num_scalar_prefetch=1,
            grid=(pairs,),
            in_specs=[
                pair_spec(packed.shape),
                pair_spec(out.shape),
                pair_spec(grad_out.shape, micro * pairs),
                lse_spec(tokens),
            ],
            out_specs=pair_spec(grad_shape),
            scratch_shapes=[
                pltpu.VMEM((tokens, HEAD_DIM), BF16),
                pltpu.VMEM((tokens, HEAD_DIM), BF16),
                acc,
                acc,
            ],
        ),
        compiler_params=pltpu.CompilerParams(dimension_semantics=("arbitrary",)),
        name="attend_back",
    )(prefix, packed, out, grad_out, lse)


class HeadSplit:
    def __init__(self, n_fsdp, head_count, seqs, span_len):
        self.head_groups = math.gcd(n_fsdp, head_count)
        self.seq_groups = n_fsdp // self.head_groups
        self.heads_per = head_count // self.head_groups
        self.seqs_per = seqs // self.seq_groups
        self.span_len = span_len

    def to_heads(self, stack):
        kinds = stack.shape[0]
        stack = stack.reshape(
            kinds,
            self.head_groups,
            self.heads_per,
            HEAD_DIM,
            -1,
            self.seq_groups,
            self.seqs_per,
            self.span_len,
        )
        stack = stack.transpose(5, 1, 4, 2, 6, 0, 3, 7)
        count = self.seq_groups * self.head_groups
        stack = stack.reshape(count, -1, kinds * HEAD_DIM, self.span_len)
        return lax.all_to_all(stack, "fsdp", split_axis=0, concat_axis=0, tiled=True)

    def to_spans(self, stack):
        kinds = stack.shape[2] // HEAD_DIM
        stack = lax.all_to_all(stack, "fsdp", split_axis=0, concat_axis=0, tiled=True)
        stack = stack.reshape(
            self.seq_groups,
            self.head_groups,
            -1,
            self.heads_per,
            self.seqs_per,
            kinds,
            HEAD_DIM,
            self.span_len,
        )
        stack = stack.transpose(5, 1, 3, 6, 2, 0, 4, 7)
        return stack.reshape(kinds, self.head_groups * self.heads_per * HEAD_DIM, -1)

    def pair_prefix(self, prefix, fsdp_index):
        mine = lax.dynamic_slice_in_dim(
            prefix, (fsdp_index // self.head_groups) * self.seqs_per, self.seqs_per, 0
        )
        return jnp.tile(mine, self.heads_per)


def layer(
    inputs,
    out_grads,
    prefix_len,
    positions,
    attn_gain,
    w_query,
    w_key,
    w_value,
    w_out,
    mlp_gain,
    w_gate,
    w_up,
    w_down,
):
    micro_count, seq_dev, span_len, model_width = inputs.shape
    n_tensor = lax.axis_size("tensor")
    n_fsdp = lax.axis_size("fsdp")
    seq_mb = seq_dev * n_tensor
    seq_len = span_len * n_fsdp
    row_count = seq_mb * span_len
    own_rows = seq_dev * span_len
    head_cols = w_query.shape[1]
    head_count = head_cols // HEAD_DIM
    ff_cols = w_gate.shape[1]
    fsdp_index = lax.axis_index("fsdp")
    tensor_index = lax.axis_index("tensor")
    query_index = fsdp_index * span_len + jnp.arange(span_len, dtype=jnp.int32)
    split = HeadSplit(n_fsdp, head_count, seq_mb, span_len)
    micros = range(micro_count)

    def gather(shard):
        return lax.all_gather(shard, "fsdp", axis=0, tiled=True)

    def scatter(grad):
        return lax.psum_scatter(grad, "fsdp", scatter_dimension=0, tiled=True).astype(F32)

    gains = lax.all_gather(jnp.stack([attn_gain, mlp_gain]), "fsdp", axis=1, tiled=True)
    gain_attn = gains[0].astype(F32)
    gain_mlp = gains[1].astype(F32)
    full_qkv = gather(jnp.concatenate([w_query, w_key, w_value], axis=1))
    full_out = gather(w_out)
    side = (fsdp_index // PAIR) % 2

    order = (
        ((tensor_index ^ jnp.arange(n_tensor, dtype=jnp.int32)) * seq_dev)[:, None]
        + jnp.arange(seq_dev, dtype=jnp.int32)
    ).reshape(-1)
    prefix_all = jnp.take(prefix_len, order, axis=1)
    own_prefix = prefix_all[:, :seq_dev]
    pos_all = jnp.take(positions, order, axis=1)
    half_dim = HEAD_DIM // 2
    ladder = jnp.arange(half_dim, dtype=F32) * (2.0 / HEAD_DIM)
    inverse = 1.0 / rope_base**ladder

    x_float = inputs.reshape(micro_count * own_rows, model_width).astype(F32)
    grad_own = out_grads.reshape(micro_count * own_rows, model_width)
    unit_attn, scale_attn = normalize(x_float)
    normed = (unit_attn * gain_attn).astype(BF16)
    normed_blocks = spread(normed)
    normed_rows = gather_rows(normed_blocks, micro_count)
    cos_tab, sin_tab, pair_prefix = [], [], []
    for m in micros:
        angles = inverse[:, None] * pos_all[m].astype(F32).reshape(-1)[None, :]
        cos_tab.append(jnp.cos(angles))
        sin_tab.append(jnp.sin(angles))
        pair_prefix.append(split.pair_prefix(prefix_all[m], fsdp_index))
    cos_all = jnp.concatenate(cos_tab, axis=1)
    sin_all = jnp.concatenate(sin_tab, axis=1)
    all_rows = micro_count * row_count
    half_cols = ff_cols // 2
    ffn_near = half_of([w_gate, w_up, w_down], side)
    ffn_far = half_of([w_gate, w_up, w_down], 1 - side)
    grad_pair = pair_join(after(paired(grad_own), full_qkv), micro_count)
    raw = dot(full_qkv, normed_rows, 0, 1).reshape(3, head_cols, all_rows)
    turned = rotate(
        raw[:2].reshape(2, head_count, 2, half_dim, all_rows), cos_all, sin_all, 1.0
    ).reshape(2, head_cols, all_rows)
    stack = jnp.concatenate([turned.astype(BF16), raw[2:].astype(BF16)], axis=0)
    packed = []
    for m in micros:
        packed.append(split.to_heads(stack[:, :, m * row_count : (m + 1) * row_count]))
    grad_pair = after(grad_pair, stack)
    grad_blocks = spread(grad_pair)
    ffn_other = swap(after(ffn_far, packed[-1]), "fsdp", PAIR)
    attn_out, attn_lse = [], []
    branch, resid, unit_mlp, scale_mlp, mlp_rows, normed_mlp = [], [], [], [], [], []
    for m in micros:
        out, lse = attend_forward(pair_prefix[m], packed[m], 0)
        attn_out.append(out)
        attn_lse.append(lse)
    mix_all = split.to_spans(jnp.concatenate(attn_out, axis=1))[0]
    ffn_other = after(ffn_other, attn_lse)
    shard_gu = own_half(side, ffn_near[:, : 2 * half_cols], ffn_other[:, : 2 * half_cols])
    shard_down = own_half(side, ffn_near[:, 2 * half_cols :], ffn_other[:, 2 * half_cols :])
    full_gu = gather_half(after(shard_gu, mix_all))
    full_down = gather_half(shard_down)
    for m in micros:
        mix = mix_all[:, m * row_count : (m + 1) * row_count]
        part = collect(peer_blocks(dot(mix, full_out, 0, 1), 1, n_tensor))
        res = x_float[m * own_rows : (m + 1) * own_rows] + part
        unit, scale = normalize(res)
        branch.append(part)
        resid.append(res)
        unit_mlp.append(unit)
        scale_mlp.append(scale)
        normed = paired((unit * gain_mlp).astype(BF16))
        normed_mlp.append(normed)
        mlp_rows.append(gather_rows(spread(pair_join(normed, 1), False), 1))

    grad_rows = gather_rows(after(grad_blocks, normed_mlp), micro_count)

    ffn_rows = 2 * row_count
    hidden, gate_val, up_val = [], [], []
    for m in micros:
        gate_up = dot(mlp_rows[m], full_gu, 1, 0)
        gate = gate_up[:, :half_cols]
        up = gate_up[:, half_cols:]
        gate_val.append(gate)
        up_val.append(up)
        hidden.append((gate * jax.nn.sigmoid(gate) * up).astype(BF16))
    hidden = jnp.concatenate(hidden, axis=0)
    down_grad = dot(grad_rows, hidden, 0, 0).astype(BF16)
    full_down = after(full_down, down_grad)
    part_down = scatter_half(down_grad)
    grad_gu = []
    for m in micros:
        rows = grad_rows[m * ffn_rows : (m + 1) * ffn_rows]
        grad_hidden = dot(rows, full_down, 1, 0)
        sig = jax.nn.sigmoid(gate_val[m])
        slope = sig * (1.0 + gate_val[m] * (1.0 - sig))
        grad_gu.append(
            jnp.concatenate(
                [
                    (grad_hidden * up_val[m] * slope).astype(BF16),
                    (grad_hidden * gate_val[m] * sig).astype(BF16),
                ],
                axis=1,
            )
        )
    normed_part = [dot(grad_gu[m], full_gu, 1, 1) for m in micros]
    gu_left = jnp.concatenate(after(mlp_rows, normed_part), axis=0)
    gu_right = jnp.concatenate(grad_gu, axis=0)
    gu_grad = dot(gu_left, gu_right, 0, 0).astype(BF16)
    part_gu = scatter_half(after(gu_grad, part_down))
    grad_resid, grad_mix, branch_rows = [], [], []
    mlp_gain_sum = jnp.zeros((model_width,), F32)
    for m in micros:
        total = collect(peer_blocks(normed_part[m], 1, n_tensor), False)
        grad_normed = total[:own_rows] + swap(
            total[own_rows:].astype(BF16), "fsdp", PAIR
        ).astype(F32)
        part, gain_part = norm_back(paired(grad_normed), unit_mlp[m], scale_mlp[m], gain_mlp)
        mlp_gain_sum = mlp_gain_sum + gain_part
        grad_res = grad_own[m * own_rows : (m + 1) * own_rows].astype(F32) + part
        grad_resid.append(grad_res)
        if m == 0:
            grad_res = after(grad_res, gu_grad)
        rows = gather_rows(spread(grad_res.astype(BF16)), 1)
        branch_rows.append(rows)
        grad_mix.append(dot(full_out, rows, 0, 1).astype(BF16))
    grad_out_all = split.to_heads(jnp.concatenate(grad_mix, axis=1)[None])
    out_grad = dot(
        jnp.concatenate(after(branch_rows, grad_mix), axis=0),
        mix_all,
        0,
        1,
    ).astype(BF16)

    mlp_rows_out = dot(after(hidden, out_grad), full_down, 1, 1)
    mlp_blocks = peer_blocks(mlp_rows_out, micro_count, n_tensor)
    own_out = scatter(after(out_grad, part_gu))

    grad_raw = []
    for m in micros:
        grad_out = after(grad_out_all, mlp_rows_out, part_down if m else own_out)
        packed_grad = attend_back(pair_prefix[m], packed[m], attn_out[m], grad_out, attn_lse[m], m)
        grad_raw.append(split.to_spans(packed_grad))

    raw = jnp.concatenate(grad_raw, axis=2)
    turned = rotate(
        raw[:2].reshape(2, head_count, 2, half_dim, all_rows).astype(F32), cos_all, sin_all, -1.0
    ).reshape(2, head_cols, all_rows)
    grad_qkv = jnp.concatenate([turned.astype(BF16), raw[2:]], axis=0).reshape(
        3 * head_cols, all_rows
    )
    qkv_grad = dot(normed_rows, grad_qkv, 0, 1).astype(BF16)
    own_down = settle_half(part_down, side, 1, qkv_grad)
    own_gu = settle_half(part_gu, side, 2, qkv_grad)
    part = dot(after(grad_qkv, qkv_grad), full_qkv, 0, 1)
    grad_normed = collect(peer_blocks(part, micro_count, n_tensor))
    mlp_part = collect(mlp_blocks, token=part)
    near = [mlp_part[2 * m * own_rows : (2 * m + 1) * own_rows] for m in micros]
    far = [mlp_part[(2 * m + 1) * own_rows : (2 * m + 2) * own_rows] for m in micros]
    far = swap(jnp.concatenate(far, axis=0).astype(BF16), "fsdp", PAIR).astype(F32)
    mlp_out = paired(jnp.concatenate(near, axis=0) + far)
    branch = jnp.concatenate(branch, axis=0)
    result = jnp.concatenate(resid, axis=0) + mlp_out
    output = result.astype(BF16).reshape(inputs.shape)
    valid = (query_index[None, None, :] >= own_prefix[:, :, None]).reshape(-1)
    stats = jnp.stack(
        [
            jnp.sum(
                jnp.where(valid, jnp.sum(part * part, axis=1), 0.0).reshape(
                    micro_count, seq_dev, span_len
                ),
                axis=2,
            )
            for part in (result, branch, mlp_out)
        ],
        axis=-1,
    )

    own_qkv = scatter(qkv_grad)
    part, attn_gain_sum = norm_back(grad_normed, unit_attn, scale_attn, gain_attn)
    input_grad = (jnp.concatenate(grad_resid, axis=0) + part).reshape(inputs.shape)

    stat_sum = tree_sum(stats, "fsdp")
    gain_sum = tree_sum(tree_sum(jnp.stack([attn_gain_sum, mlp_gain_sum]), "tensor"), "fsdp")
    row_share = model_width // n_fsdp
    own_gain = lax.dynamic_slice_in_dim(gain_sum, fsdp_index * row_share, row_share, 1)
    counts = ((seq_len - own_prefix) * model_width).astype(F32)
    rms_stats = jnp.sqrt(stat_sum / counts[..., None] + stat_eps)
    return (
        output,
        input_grad,
        own_gain[0],
        own_qkv[:, :head_cols],
        own_qkv[:, head_cols : 2 * head_cols],
        own_qkv[:, 2 * head_cols :],
        own_out,
        own_gain[1],
        own_gu[0],
        own_gu[1],
        own_down[0],
        rms_stats,
    )


def solution(mesh):
    in_specs = (
        P(None, "tensor", "fsdp", None),
        P(None, "tensor", "fsdp", None),
        P(),
        P(None, None, "fsdp"),
        P("fsdp"),
        P("fsdp", "tensor"),
        P("fsdp", "tensor"),
        P("fsdp", "tensor"),
        P("fsdp", "tensor"),
        P("fsdp"),
        P("fsdp", "tensor"),
        P("fsdp", "tensor"),
        P("fsdp", "tensor"),
    )
    out_specs = (
        P(None, "tensor", "fsdp", None),
        P(None, "tensor", "fsdp", None),
        P("fsdp"),
        P("fsdp", "tensor"),
        P("fsdp", "tensor"),
        P("fsdp", "tensor"),
        P("fsdp", "tensor"),
        P("fsdp"),
        P("fsdp", "tensor"),
        P("fsdp", "tensor"),
        P("fsdp", "tensor"),
        P(None, "tensor", None),
    )
    return jax.shard_map(layer, mesh=mesh, in_specs=in_specs, out_specs=out_specs, check_vma=False)
```

profile of v0, /device:TPU:0, one launch (start us, length us, event | category | flops | bytes accessed | tf_op | source)
XLA Modules:
  0.0 1092.7 jit_solution(6633767969920323350)
XLA Ops:
  33.6 19.8 %collective-permute-done = bf16[256,2048]{1,0:T(8,128)(2,1)S(1)} collective-permute-done((bf16[256,2048]{1,0:T(8,128)(2,1)S(1)}, bf16[256,2048]{1,0:T(8,128)(2,1)S(1)}, u32[]{:S(2)}, u32[]{:S(2)}) %collective-permute-start) | collective-permute-done | bytes 1048608 | tf_op jit(solution)/shard_map/ppermute | solution.py:56
  54.2 22.2 %collective-permute-done.1 = bf16[256,2048]{1,0:T(8,128)(2,1)S(1)} collective-permute-done((bf16[256,2048]{1,0:T(8,128)(2,1)S(1)}, bf16[256,2048]{1,0:T(8,128)(2,1)S(1)}, u32[]{:S(2)}, u32[]{:S(2)}) %collective-permute-start.1) | collective-permute-done | bytes 1048608 | tf_op jit(solution)/shard_map/ppermute | solution.py:56
  105.9 33.8 %all-to-all-done.1.x_ref = bf16[8,4,192,128]{3,2,1,0:T(8,128)(2,1)S(1)} async-done(((bf16[8,4,192,128]{3,2,1,0:T(8,128)(2,1)}), bf16[8,4,192,128]{3,2,1,0:T(8,128)(2,1)S(1)}, u32[]{:S(2)}, u32[]{:S(2)}) %all-to-all-start.1) | async-done | bytes 1572896 | tf_op jit(solution)/shard_map/all_to_all | solution.py:388
  152.4 19.3 %attend_forward.3 = (bf16[8,4,64,128]{3,2,1,0:T(8,128)(2,1)}, f32[4,1,1024]{2,1,0:T(1,128)}) custom-call(s32[4]{0:T(128)} %get-tuple-element.117.prefix_ref, bf16[8,4,192,128]{3,2,1,0:T(8,128)(2,1)} %copy-done.9), custom_call_target="tpu_custom_call" | custom-call | tf_op jit(solution)/shard_map/attend_forward/pallas_call | solution.py:315
  171.7 26.1 %all-to-all-done.x_ref = bf16[8,4,192,128]{3,2,1,0:T(8,128)(2,1)S(1)} async-done(((bf16[8,4,192,128]{3,2,1,0:T(8,128)(2,1)}), bf16[8,4,192,128]{3,2,1,0:T(8,128)(2,1)S(1)}, u32[]{:S(2)}, u32[]{:S(2)}) %all-to-all-start) | async-done | bytes 1572896 | tf_op jit(solution)/shard_map/all_to_all | solution.py:388
  199.0 20.1 %attend_forward.2 = (bf16[8,4,64,128]{3,2,1,0:T(8,128)(2,1)}, f32[4,1,1024]{2,1,0:T(1,128)}) custom-call(s32[4]{0:T(128)} %get-tuple-element.116.prefix_ref, bf16[8,4,192,128]{3,2,1,0:T(8,128)(2,1)} %copy-done.8), custom_call_target="tpu_custom_call" | custom-call | tf_op jit(solution)/shard_map/attend_forward/pallas_call | solution.py:315
  228.6 22.8 %all-to-all-done.2 = bf16[8,8,64,128]{3,2,1,0:T(8,128)(2,1)S(1)} async-done(((bf16[8,8,64,128]{3,2,1,0:T(8,128)(2,1)}), bf16[8,8,64,128]{3,2,1,0:T(8,128)(2,1)S(1)}, u32[]{:S(2)}, u32[]{:S(2)}) %all-to-all-start.2) | async-done | bytes 1048608 | tf_op jit(solution)/shard_map/all_to_all | solution.py:392
  257.0 37.3 %collective-permute-done.20 = bf16[256,2048]{1,0:T(8,128)(2,1)S(1)} collective-permute-done((bf16[256,2048]{1,0:T(8,128)(2,1)S(1)}, bf16[256,2048]{1,0:T(8,128)(2,1)S(1)}, u32[]{:S(2)}, u32[]{:S(2)}) %collective-permute-start.20) | collective-permute-done | bytes 1048608 | tf_op jit(solution)/shard_map/ppermute | solution.py:56
  359.4 35.5 %collective-permute-done.21 = bf16[512,2048]{1,0:T(8,128)(2,1)S(1)} collective-permute-done((bf16[512,2048]{1,0:T(8,128)(2,1)S(1)}, bf16[512,2048]{1,0:T(8,128)(2,1)S(1)}, u32[]{:S(2)}, u32[]{:S(2)}) %collective-permute-start.21) | collective-permute-done | bytes 2097184 | tf_op jit(solution)/shard_map/ppermute | solution.py:56
  394.9 43.2 %collective-permute-done.23 = bf16[512,2048]{1,0:T(8,128)(2,1)S(1)} collective-permute-done((bf16[512,2048]{1,0:T(8,128)(2,1)S(1)}, bf16[512,2048]{1,0:T(8,128)(2,1)S(1)}, u32[]{:S(2)}, u32[]{:S(2)}) %collective-permute-start.23) | collective-permute-done | bytes 2097184 | tf_op jit(solution)/shard_map/ppermute | solution.py:56
  454.1 21.0 %collective-permute-done.11 = bf16[256,2048]{1,0:T(8,128)(2,1)S(1)} collective-permute-done((bf16[256,2048]{1,0:T(8,128)(2,1)S(1)}, bf16[256,2048]{1,0:T(8,128)(2,1)S(1)}, u32[]{:S(2)}, u32[]{:S(2)}) %collective-permute-start.11) | collective-permute-done | bytes 1048608 | tf_op jit(solution)/shard_map/ppermute | solution.py:56
  477.1 20.4 %collective-permute-done.17 = bf16[256,2048]{1,0:T(8,128)(2,1)S(1)} collective-permute-done((bf16[256,2048]{1,0:T(8,128)(2,1)S(1)}, bf16[256,2048]{1,0:T(8,128)(2,1)S(1)}, u32[]{:S(2)}, u32[]{:S(2)}) %collective-permute-start.17) | collective-permute-done | bytes 1048608 | tf_op jit(solution)/shard_map/ppermute | solution.py:56
  591.2 14.8 %fusion.119 = (bf16[1024,2048]{1,0:T(8,128)(2,1)}, f32[1024,2048]{1,0:T(8,128)}) fusion(bf16[2048,2048]{1,0:T(8,128)(2,1)} %all-gather.9.cloned.1.call-done, bf16[1024,1024]{1,0:T(8,128)(2,1)S(1)} %get-tuple-element.137, bf16[1024,1024]{1,0:T(8,128)(2,1)S(1)} %get-tuple-element.136), kind=kOutput, calls=%fused_computation.346 | convolution fusion | flops 8600420352 | bytes 25165824 | tf_op jit(solution)/shard_map/dot_general | solution.py:23
  606.0 15.0 %fusion.118 = (bf16[1024,2048]{1,0:T(8,128)(2,1)}, f32[1024,2048]{1,0:T(8,128)}) fusion(bf16[2048,2048]{1,0:T(8,128)(2,1)} %all-gather.9.cloned.1.call-done, bf16[1024,1024]{1,0:T(8,128)(2,1)} %get-tuple-element.135, bf16[1024,1024]{1,0:T(8,128)(2,1)S(1)} %get-tuple-element.134), kind=kOutput, calls=%fused_computation.345 | convolution fusion | flops 8600420352 | bytes 25165824 | tf_op jit(solution)/shard_map/dot_general | solution.py:23
  621.1 26.2 %fusion.11 = bf16[2048,2048]{1,0:T(8,128)(2,1)} fusion(bf16[1024,1024]{1,0:T(8,128)(2,1)} %get-tuple-element.135, bf16[1024,1024]{1,0:T(8,128)(2,1)} %copy-done.76, bf16[1024,1024]{1,0:T(8,128)(2,1)} %copy-done.75, bf16[1024,1024]{1,0:T(8,128)(2,1)S(1)} %copy-done.74, bf16[1024,2048]{1,0:T(8,128)(2,1)} %constant_dynamic-update-slice_fusion.26, ...), kind=kOutput, calls=%fused_computation.13 | convolution fusion | flops 17234395136 | bytes 25165824 | tf_op jit(solution)/shard_map/dot_general | solution.py:23
  678.1 19.6 %collective-permute-done.25 = bf16[256,2048]{1,0:T(8,128)(2,1)S(1)} collective-permute-done((bf16[256,2048]{1,0:T(8,128)(2,1)S(1)}, bf16[256,2048]{1,0:T(8,128)(2,1)S(1)}, u32[]{:S(2)}, u32[]{:S(2)}) %collective-permute-start.25) | collective-permute-done | bytes 1048608 | tf_op jit(solution)/shard_map/ppermute | solution.py:56
  698.4 16.9 %collective-permute-done.33 = bf16[256,2048]{1,0:T(8,128)(2,1)S(1)} collective-permute-done((bf16[256,2048]{1,0:T(8,128)(2,1)S(1)}, bf16[256,2048]{1,0:T(8,128)(2,1)S(1)}, u32[]{:S(2)}, u32[]{:S(2)}) %collective-permute-start.33) | collective-permute-done | bytes 1048608 | tf_op jit(solution)/shard_map/ppermute | solution.py:56
  716.3 21.3 %collective-permute-done.36 = bf16[128,2048]{1,0:T(8,128)(2,1)S(1)} collective-permute-done((bf16[128,2048]{1,0:T(8,128)(2,1)S(1)}, bf16[128,2048]{1,0:T(8,128)(2,1)S(1)}, u32[]{:S(2)}, u32[]{:S(2)}) %collective-permute-start.36) | collective-permute-done | bytes 524320 | tf_op jit(solution)/shard_map/ppermute | solution.py:56
  810.4 16.7 %fusion.120 = (bf16[2048,2048]{1,0:T(8,128)(2,1)}, f32[2048,2048]{1,0:T(8,128)}) fusion(bf16[2048,1024]{1,0:T(8,128)(2,1)} %pad_maximum_fusion.1, bf16[2048,1024]{1,0:T(8,128)(2,1)} %all-gather.11.cloned.1.call-done), kind=kOutput, calls=%fused_computation.347 | convolution fusion | flops 8594128896 | bytes 33554432 | tf_op jit(solution)/shard_map/dot_general | solution.py:23
  838.6 20.3 %attend_back.3 = bf16[8,4,192,128]{3,2,1,0:T(8,128)(2,1)} custom-call(s32[4]{0:T(128)} %get-tuple-element.117.prefix_ref, bf16[8,4,192,128]{3,2,1,0:T(8,128)(2,1)} %copy-done.9, bf16[8,4,64,128]{3,2,1,0:T(8,128)(2,1)} %get-tuple-element.43.o_ref, bf16[8,8,64,128]{3,2,1,0:T(8,128)(2,1)} %all-to-all-done.3.do_ref, f32[4,1,1024]{2,1,0:T(1,128)} %get-tuple-element.46.lse_ref), custom_call_target="tpu_custom_call" | custom-call | tf_op jit(solution)/shard_map/attend_back/pallas_call | solution.py:340
  865.1 21.0 %attend_back.2 = bf16[8,4,192,128]{3,2,1,0:T(8,128)(2,1)} custom-call(s32[4]{0:T(128)} %get-tuple-element.116.prefix_ref, bf16[8,4,192,128]{3,2,1,0:T(8,128)(2,1)} %copy-done.8, bf16[8,4,64,128]{3,2,1,0:T(8,128)(2,1)} %get-tuple-element.42.o_ref, bf16[8,8,64,128]{3,2,1,0:T(8,128)(2,1)} %all-to-all-done.3.do_ref, f32[4,1,1024]{2,1,0:T(1,128)} %get-tuple-element.45.lse_ref), custom_call_target="tpu_custom_call" | custom-call | tf_op jit(solution)/shard_map/attend_back/pallas_call | solution.py:340
  886.1 14.9 %all-to-all-done.5 = bf16[8,4,192,128]{3,2,1,0:T(8,128)(2,1)} async-done(((bf16[8,4,192,128]{3,2,1,0:T(8,128)(2,1)}), bf16[8,4,192,128]{3,2,1,0:T(8,128)(2,1)}, u32[]{:S(2)}, u32[]{:S(2)}) %all-to-all-start.5) | async-done | bytes 1572896 | tf_op jit(solution)/shard_map/all_to_all | solution.py:392
  980.5 26.2 %collective-permute-done.41 = bf16[512,2048]{1,0:T(8,128)(2,1)} collective-permute-done((bf16[512,2048]{1,0:T(8,128)(2,1)}, bf16[512,2048]{1,0:T(8,128)(2,1)}, u32[]{:S(2)}, u32[]{:S(2)}) %collective-permute-start.41) | collective-permute-done | bytes 2097184 | tf_op jit(solution)/shard_map/ppermute | solution.py:56
  1027.6 29.2 %collective-permute-done.43 = bf16[256,2048]{1,0:T(8,128)(2,1)S(1)} collective-permute-done((bf16[256,2048]{1,0:T(8,128)(2,1)S(1)}, bf16[256,2048]{1,0:T(8,128)(2,1)S(1)}, u32[]{:S(2)}, u32[]{:S(2)}) %collective-permute-start.43) | collective-permute-done | bytes 1048608 | tf_op jit(solution)/shard_map/ppermute | solution.py:56
  (543 shorter events, 512.4 us)
Async XLA Ops:
  7.2 76.4 %all-gather.5.cloned.1.call-start = ((), (), s32[]{:S(2)}) async-start(), calls=%async_computation.10 | async-start | bytes 7077888 | tf_op jit(solution)/shard_map/all_gather | solution.py:445
  28.8 47.6 %collective-permute-start.1 = (bf16[256,2048]{1,0:T(8,128)(2,1)S(1)}, bf16[256,2048]{1,0:T(8,128)(2,1)S(1)}, u32[]{:S(2)}, u32[]{:S(2)}) collective-permute-start(bf16[256,2048]{1,0:T(8,128)(2,1)S(1)} %multiply_convert_fusion.6), channel_id=1, source_target_pairs={{0,2},{1,3},{2,0},{3,1},{4,6},{5,7},{6,4},{7,5},{8,10},{9,11},{10,... | collective-permute-start | bytes 3145736 | tf_op jit(solution)/shard_map/ppermute | solution.py:56
  30.3 47.0 %collective-permute-start.2 = (bf16[256,2048]{1,0:T(8,128)(2,1)S(1)}, bf16[256,2048]{1,0:T(8,128)(2,1)}, u32[]{:S(2)}, u32[]{:S(2)}) collective-permute-start(bf16[256,2048]{1,0:T(8,128)(2,1)S(1)} %multiply_convert_fusion.6), channel_id=1, source_target_pairs={{0,3},{1,2},{2,1},{3,0},{4,7},{5,6},{6,5},{7,4},{8,11},{9,10},{10,... | collective-permute-start | bytes 3145736 | tf_op jit(solution)/shard_map/ppermute | solution.py:56
  139.6 58.2 %all-to-all-start = ((bf16[8,4,192,128]{3,2,1,0:T(8,128)(2,1)}), bf16[8,4,192,128]{3,2,1,0:T(8,128)(2,1)S(1)}, u32[]{:S(2)}, u32[]{:S(2)}) async-start(bf16[8,4,192,128]{3,2,1,0:T(8,128)(2,1)} %bitcast.149), calls=%async_computation | async-start | bytes 3145728 | tf_op jit(solution)/shard_map/all_to_all | solution.py:388
  143.2 152.1 %all-gather.7.cloned.1.call-start = ((), (), s32[]{:S(2)}) async-start(), calls=%async_computation.11 | async-start | bytes 2359296 | tf_op jit(solution)/shard_map/all_gather | solution.py:445
  149.0 76.1 %collective-permute-start.14 = (bf16[256,3072]{1,0:T(8,128)(2,1)}, bf16[256,3072]{1,0:T(8,128)(2,1)}, u32[]{:S(2)}, u32[]{:S(2)}) collective-permute-start(bf16[256,3072]{1,0:T(8,128)(2,1)} %pad_maximum_fusion.13), channel_id=1, source_target_pairs={{0,8},{4,12},{8,0},{12,4},{16,24},{20,28},{24,16},{28,20},{1,9},{5... | collective-permute-start | bytes 4718600 | tf_op jit(solution)/shard_map/ppermute | solution.py:56
  224.9 292.3 %all-gather.9.cloned.1.call-start = ((), (), s32[]{:S(2)}) async-start(), calls=%async_computation.12 | async-start | bytes 10485760 | tf_op jit(solution)/shard_map/all_gather | solution.py:150
  255.0 308.8 %all-gather.11.cloned.1.call-start = ((), (), s32[]{:S(2)}) async-start(), calls=%async_computation.13 | async-start | bytes 5242880 | tf_op jit(solution)/shard_map/all_gather | solution.py:150
  319.8 327.5 %reduce-scatter.5.cloned.1.call-start = ((), (), s32[]{:S(2)}) async-start(), calls=%async_computation.14 | async-start | bytes 5242880 | tf_op jit(solution)/shard_map/reduce_scatter | solution.py:160
  326.8 68.0 %collective-permute-start.21 = (bf16[512,2048]{1,0:T(8,128)(2,1)S(1)}, bf16[512,2048]{1,0:T(8,128)(2,1)S(1)}, u32[]{:S(2)}, u32[]{:S(2)}) collective-permute-start(bf16[512,2048]{1,0:T(8,128)(2,1)S(1)} %pad_maximum_fusion.6), channel_id=1, source_target_pairs={{0,1},{1,0},{2,3},{3,2},{4,5},{5,4},{6,7},{7,6},{8,9},{9,8},{10,11... | collective-permute-start | bytes 6291464 | tf_op jit(solution)/shard_map/ppermute | solution.py:56
  329.7 65.2 %collective-permute-start.22 = (bf16[512,2048]{1,0:T(8,128)(2,1)S(1)}, bf16[512,2048]{1,0:T(8,128)(2,1)S(1)}, u32[]{:S(2)}, u32[]{:S(2)}) collective-permute-start(bf16[512,2048]{1,0:T(8,128)(2,1)S(1)} %pad_maximum_fusion.6), channel_id=1, source_target_pairs={{0,2},{1,3},{2,0},{3,1},{4,6},{5,7},{6,4},{7,5},{8,10},{9,11},{10,... | collective-permute-start | bytes 6291464 | tf_op jit(solution)/shard_map/ppermute | solution.py:56
  338.8 99.3 %collective-permute-start.23 = (bf16[512,2048]{1,0:T(8,128)(2,1)S(1)}, bf16[512,2048]{1,0:T(8,128)(2,1)S(1)}, u32[]{:S(2)}, u32[]{:S(2)}) collective-permute-start(bf16[512,2048]{1,0:T(8,128)(2,1)S(1)} %pad_maximum_fusion.6), channel_id=1, source_target_pairs={{0,3},{1,2},{2,1},{3,0},{4,7},{5,6},{6,5},{7,4},{8,11},{9,10},{10,... | collective-permute-start | bytes 6291464 | tf_op jit(solution)/shard_map/ppermute | solution.py:56
  356.4 91.6 %collective-permute-start.9 = (bf16[128,2048]{1,0:T(8,128)(2,1)S(1)}, bf16[128,2048]{1,0:T(8,128)(2,1)S(1)}, u32[]{:S(2)}, u32[]{:S(2)}) collective-permute-start(bf16[128,2048]{1,0:T(8,128)(2,1)S(1)} %get-tuple-element.229), channel_id=1, source_target_pairs={{0,8},{4,12},{8,0},{12,4},{16,24},{20,28},{24,16},{28,20},{1,9},{5... | collective-permute-start | bytes 1572872 | tf_op jit(solution)/shard_map/ppermute | solution.py:56
  359.3 91.3 %collective-permute-start.15 = (bf16[128,2048]{1,0:T(8,128)(2,1)S(1)}, bf16[128,2048]{1,0:T(8,128)(2,1)S(1)}, u32[]{:S(2)}, u32[]{:S(2)}) collective-permute-start(bf16[128,2048]{1,0:T(8,128)(2,1)S(1)} %get-tuple-element.231), channel_id=1, source_target_pairs={{0,8},{4,12},{8,0},{12,4},{16,24},{20,28},{24,16},{28,20},{1,9},{5... | collective-permute-start | bytes 1572872 | tf_op jit(solution)/shard_map/ppermute | solution.py:56
  450.7 48.1 %collective-permute-start.16 = (bf16[256,2048]{1,0:T(8,128)(2,1)S(1)}, bf16[256,2048]{1,0:T(8,128)(2,1)S(1)}, u32[]{:S(2)}, u32[]{:S(2)}) collective-permute-start(bf16[256,2048]{1,0:T(8,128)(2,1)S(1)} %pad_maximum_fusion.17), channel_id=1, source_target_pairs={{0,1},{1,0},{2,3},{3,2},{4,5},{5,4},{6,7},{7,6},{8,9},{9,8},{10,11... | collective-permute-start | bytes 3145736 | tf_op jit(solution)/shard_map/ppermute | solution.py:56
  563.8 246.6 %reduce-scatter.7.cloned.1.call-start = ((), (), s32[]{:S(2)}) async-start(), calls=%async_computation.15 | async-start | bytes 10485760 | tf_op jit(solution)/shard_map/reduce_scatter | solution.py:160
  804.1 59.2 %reduce-scatter.9.cloned.1.call-start = ((), (), s32[]{:S(2)}) async-start(), calls=%async_computation.16 | async-start | bytes 2359296 | tf_op jit(solution)/shard_map/reduce_scatter | solution.py:448
  905.3 177.8 %reduce-scatter.11.cloned.1.call-start = ((), (), s32[]{:S(2)}) async-start(), calls=%async_computation.17 | async-start | bytes 7077888 | tf_op jit(solution)/shard_map/reduce_scatter | solution.py:448
  912.8 67.8 %collective-permute-start.42 = (bf16[512,2048]{1,0:T(8,128)(2,1)}, bf16[512,2048]{1,0:T(8,128)(2,1)}, u32[]{:S(2)}, u32[]{:S(2)}) collective-permute-start(bf16[512,2048]{1,0:T(8,128)(2,1)} %pad_maximum_fusion.11), channel_id=1, source_target_pairs={{0,3},{1,2},{2,1},{3,0},{4,7},{5,6},{6,5},{7,4},{8,11},{9,10},{10,... | collective-permute-start | bytes 6291464 | tf_op jit(solution)/shard_map/ppermute | solution.py:56
  916.2 90.5 %collective-permute-start.41 = (bf16[512,2048]{1,0:T(8,128)(2,1)}, bf16[512,2048]{1,0:T(8,128)(2,1)}, u32[]{:S(2)}, u32[]{:S(2)}) collective-permute-start(bf16[512,2048]{1,0:T(8,128)(2,1)} %pad_maximum_fusion.10), channel_id=1, source_target_pairs={{0,2},{1,3},{2,0},{3,1},{4,6},{5,7},{6,4},{7,5},{8,10},{9,11},{10,... | collective-permute-start | bytes 6291464 | tf_op jit(solution)/shard_map/ppermute | solution.py:56
  918.4 88.3 %collective-permute-start.40 = (bf16[512,2048]{1,0:T(8,128)(2,1)}, bf16[512,2048]{1,0:T(8,128)(2,1)}, u32[]{:S(2)}, u32[]{:S(2)}) collective-permute-start(bf16[512,2048]{1,0:T(8,128)(2,1)} %pad_maximum_fusion.9), channel_id=1, source_target_pairs={{0,1},{1,0},{2,3},{3,2},{4,5},{5,4},{6,7},{7,6},{8,9},{9,8},{10,11... | collective-permute-start | bytes 6291464 | tf_op jit(solution)/shard_map/ppermute | solution.py:56
  924.7 88.7 %collective-permute-start.53 = (bf16[256,1024]{1,0:T(8,128)(2,1)}, bf16[256,1024]{1,0:T(8,128)(2,1)}, u32[]{:S(2)}, u32[]{:S(2)}) collective-permute-start(bf16[256,1024]{1,0:T(8,128)(2,1)} %constant_dynamic-slice_fusion.1), channel_id=1, source_target_pairs={{0,8},{4,12},{8,0},{12,4},{16,24},{20,28},{24,16},{28,20},{1,9},{5... | collective-permute-start | bytes 1572872 | tf_op jit(solution)/shard_map/ppermute | solution.py:56
  936.7 76.7 %collective-permute-start.52 = (bf16[256,2048]{1,0:T(8,128)(2,1)}, bf16[256,2048]{1,0:T(8,128)(2,1)}, u32[]{:S(2)}, u32[]{:S(2)}) collective-permute-start(bf16[256,2048]{1,0:T(8,128)(2,1)} %constant_dynamic-slice_fusion.2), channel_id=1, source_target_pairs={{0,8},{4,12},{8,0},{12,4},{16,24},{20,28},{24,16},{28,20},{1,9},{5... | collective-permute-start | bytes 3145736 | tf_op jit(solution)/shard_map/ppermute | solution.py:56
  1015.4 47.1 %collective-permute-start.45 = (bf16[256,2048]{1,0:T(8,128)(2,1)S(1)}, bf16[256,2048]{1,0:T(8,128)(2,1)S(1)}, u32[]{:S(2)}, u32[]{:S(2)}) collective-permute-start(bf16[256,2048]{1,0:T(8,128)(2,1)S(1)} %pad_maximum_fusion.26), channel_id=1, source_target_pairs={{0,2},{1,3},{2,0},{3,1},{4,6},{5,7},{6,4},{7,5},{8,10},{9,11},{10,... | collective-permute-start | bytes 3145736 | tf_op jit(solution)/shard_map/ppermute | solution.py:56
  (128 other events, 3099.9 us)
Sparse Core Ops, SparseCore 0:
  10.2 67.4 all-gather.4
  145.7 50.4 all-gather.6
  255.1 102.2 all-gather.8
  359.4 56.8 all-gather.10
  563.9 67.0 reduce-scatter.4
  647.4 115.6 reduce-scatter.6
  810.5 41.7 reduce-scatter.8
  968.4 86.8 reduce-scatter.10
where the time goes:
time: 1100 us; the launch traced here: 1090 us
  waiting for transfers between devices  534 us (49%)
  matrix products  182 us (17%)
  local copies, waits for them, and re-layouts  107 us (10%)
  starting transfers between devices  92.2 us (8%)
  Pallas kernels  80.8 us (7%)
  other arithmetic  66.3 us (6%)
  between operations  16.7 us (2%)
  blocking collectives  13.5 us (1%)
    ppermute x57, waiting for transfers between devices, swap(): return lax.ppermute(value, axis, [(a, a ^ distance) for a in range(count)])  417 us
    dot_general x17, matrix products, dot(): lax.dot_general(left, right, (((left_dim,), (right_dim,)), ((), ())), pre...  182 us
    all_to_all x3, waiting for transfers between devices, to_heads(): lax.all_to_all(stack, 'fsdp', split_axis=0, concat_axis=0, tiled=True)  71.4 us
    ppermute x57, starting transfers between devices, swap(): return lax.ppermute(value, axis, [(a, a ^ distance) for a in range(count)])  61.2 us
    all_to_all x3, waiting for transfers between devices, to_spans(): lax.all_to_all(stack, 'fsdp', split_axis=0, concat_axis=0, tiled=True)  44.1 us
    pallas_call x2, Pallas kernels, attend_back(): pl.pallas_call(backward_kernel, out_shape=jax.ShapeDtypeStruct(grad_shape...  41.4 us
    pallas_call x2, Pallas kernels, attend_forward(): pl.pallas_call(forward_kernel, out_shape=(jax.ShapeDtypeStruct(out_shape,...  39.4 us
    unnamed x237, local copies, waits for them, and re-layouts  31.7 us
  transfers between devices with their start and end apart: 71, of which 43 were waited for; matrix products, arithmetic and copies ran while one was open for 30% of the time, Pallas kernels for 7%

commit v1 on v0

--- a/solution.py
+++ b/solution.py
@@ -1,3 +1,4 @@
+import functools
 import math
 
 import jax
@@ -307,7 +308,7 @@
     return pl.BlockSpec((1, 1, tokens), lambda p, pre: (p, 0, 0))
 
 
-def attend_forward(prefix, packed, micro):
+def attend_forward(prefix, packed):
     spans, _, _, span_len = packed.shape
     pairs = prefix.shape[0]
     tokens = spans * span_len
@@ -321,7 +322,7 @@
         grid_spec=pltpu.PrefetchScalarGridSpec(
             num_scalar_prefetch=1,
             grid=(pairs,),
-            in_specs=[pair_spec(packed.shape, micro * pairs)],
+            in_specs=[pair_spec(packed.shape)],
             out_specs=[pair_spec(out_shape), lse_spec(tokens)],
             scratch_shapes=[pltpu.VMEM((tokens, HEAD_DIM), BF16)],
         ),
@@ -362,6 +363,107 @@
     )(prefix, packed, out, grad_out, lse)
 
 
+def tile_of(size):
+    return math.gcd(size, 256)
+
+
+def whole(shape):
+    return pl.BlockSpec(shape, lambda n: (0,) * len(shape), pipeline_mode=pl.Buffered(1))
+
+
+def col_tile(rows, tile):
+    return pl.BlockSpec((rows, tile), lambda n: (0, n))
+
+
+def ffn_forward_kernel(x_ref, wg_ref, wu_ref, g_ref, u_ref, h_ref):
+    x = x_ref[...]
+    gate = dot(x, wg_ref[...], 1, 0)
+    up = dot(x, wu_ref[...], 1, 0)
+    g_ref[...] = gate
+    u_ref[...] = up
+    h_ref[...] = (gate * jax.nn.sigmoid(gate) * up).astype(BF16)
+
+
+def ffn_forward(rows, w_gate, w_up):
+    count, width = rows.shape
+    units = w_gate.shape[1]
+    tile = tile_of(units)
+    return pl.pallas_call(
+        ffn_forward_kernel,
+        grid=(units // tile,),
+        in_specs=[whole(rows.shape), col_tile(width, tile), col_tile(width, tile)],
+        out_specs=[col_tile(count, tile)] * 3,
+        out_shape=[
+            jax.ShapeDtypeStruct((count, units), F32),
+            jax.ShapeDtypeStruct((count, units), F32),
+            jax.ShapeDtypeStruct((count, units), BF16),
+        ],
+        name="ffn_forward",
+    )(rows, w_gate, w_up)
+
+
+def ffn_back_kernel(dy_ref, wd_ref, g_ref, u_ref, dg_ref, du_ref):
+    grad_hidden = dot(dy_ref[...], wd_ref[...], 1, 0)
+    gate = g_ref[...]
+    sig = jax.nn.sigmoid(gate)
+    slope = sig * (1.0 + gate * (1.0 - sig))
+    dg_ref[...] = (grad_hidden * u_ref[...] * slope).astype(BF16)
+    du_ref[...] = (grad_hidden * (gate * sig)).astype(BF16)
+
+
+def ffn_back(grad_rows, micro, w_down, gate, up):
+    count, units = gate.shape
+    width = w_down.shape[0]
+    tile = tile_of(units)
+    return pl.pallas_call(
+        ffn_back_kernel,
+        grid=(units // tile,),
+        in_specs=[
+            pl.BlockSpec((count, width), lambda n: (micro, 0), pipeline_mode=pl.Buffered(1)),
+            col_tile(width, tile),
+            col_tile(count, tile),
+            col_tile(count, tile),
+        ],
+        out_specs=[col_tile(count, tile)] * 2,
+        out_shape=[jax.ShapeDtypeStruct((count, units), BF16)] * 2,
+        name="ffn_back",
+    )(grad_rows, w_down, gate, up)
+
+
+def to_peers_kernel(terms, micros, *refs):
+    left = [r[...] for r in refs[:terms]]
+    right = [r[...] for r in refs[terms : 2 * terms]]
+    outs = refs[2 * terms :]
+    total = None
+    for a, b in zip(left, right):
+        part = dot(a, b, 1, 1)
+        total = part if total is None else total + part
+    size = outs[0].shape[0] // micros
+    for m in range(micros):
+        for k, out in enumerate(outs):
+            first = (m * len(outs) + k) * size
+            out[m * size : (m + 1) * size, :] = total[first : first + size].astype(out.dtype)
+
+
+def to_peers(lefts, rights, micros, peers):
+    count, units = lefts[0].shape
+    width = rights[0].shape[0]
+    tile = tile_of(width)
+    terms = len(lefts)
+    rows = count // peers
+    return pl.pallas_call(
+        functools.partial(to_peers_kernel, terms, micros),
+        grid=(width // tile,),
+        in_specs=[whole(left.shape) for left in lefts]
+        + [pl.BlockSpec((tile, units), lambda n: (n, 0))] * terms,
+        out_specs=[col_tile(rows, tile)] * peers,
+        out_shape=[
+            jax.ShapeDtypeStruct((rows, width), BF16 if k else F32) for k in range(peers)
+        ],
+        name="to_peers",
+    )(*lefts, *rights)
+
+
 class HeadSplit:
     def __init__(self, n_fsdp, head_count, seqs, span_len):
         self.head_groups = math.gcd(n_fsdp, head_count)
@@ -469,7 +571,7 @@
     grad_own = out_grads.reshape(micro_count * own_rows, model_width)
     unit_attn, scale_attn = normalize(x_float)
     normed = (unit_attn * gain_attn).astype(BF16)
-    normed_blocks = spread(normed)
+    normed_blocks = spread(normed, False)
     normed_rows = gather_rows(normed_blocks, micro_count)
     cos_tab, sin_tab, pair_prefix = [], [], []
     for m in micros:
@@ -495,21 +597,29 @@
     grad_pair = after(grad_pair, stack)
     grad_blocks = spread(grad_pair)
     ffn_other = swap(after(ffn_far, packed[-1]), "fsdp", PAIR)
-    attn_out, attn_lse = [], []
-    branch, resid, unit_mlp, scale_mlp, mlp_rows, normed_mlp = [], [], [], [], [], []
-    for m in micros:
-        out, lse = attend_forward(pair_prefix[m], packed[m], 0)
-        attn_out.append(out)
-        attn_lse.append(lse)
+    attn_out, attn_lse = [None] * micro_count, [None] * micro_count
+    done = full_out
+    for m in reversed(micros):
+        attn_out[m], attn_lse[m] = attend_forward(pair_prefix[m], after(packed[m], done))
+        done = attn_lse[m]
     mix_all = split.to_spans(jnp.concatenate(attn_out, axis=1))[0]
     ffn_other = after(ffn_other, attn_lse)
-    shard_gu = own_half(side, ffn_near[:, : 2 * half_cols], ffn_other[:, : 2 * half_cols])
-    shard_down = own_half(side, ffn_near[:, 2 * half_cols :], ffn_other[:, 2 * half_cols :])
-    full_gu = gather_half(after(shard_gu, mix_all))
-    full_down = gather_half(shard_down)
+    shards = [
+        own_half(
+            side,
+            ffn_near[:, i * half_cols : (i + 1) * half_cols],
+            ffn_other[:, i * half_cols : (i + 1) * half_cols],
+        )
+        for i in range(3)
+    ]
+    full_gate = gather_half(after(shards[0], mix_all))
+    branch, resid, unit_mlp, scale_mlp, joined = [], [], [], [], []
+    parts = []
     for m in micros:
         mix = mix_all[:, m * row_count : (m + 1) * row_count]
-        part = collect(peer_blocks(dot(mix, full_out, 0, 1), 1, n_tensor))
+        parts.append(dot(after(mix, parts) if parts else mix, full_out, 0, 1))
+    for m in micros:
+        part = collect(peer_blocks(parts[m], 1, n_tensor))
         res = x_float[m * own_rows : (m + 1) * own_rows] + part
         unit, scale = normalize(res)
         branch.append(part)
@@ -517,48 +627,39 @@
         unit_mlp.append(unit)
         scale_mlp.append(scale)
         normed = paired((unit * gain_mlp).astype(BF16))
-        normed_mlp.append(normed)
-        mlp_rows.append(gather_rows(spread(pair_join(normed, 1), False), 1))
-
-    grad_rows = gather_rows(after(grad_blocks, normed_mlp), micro_count)
-
-    ffn_rows = 2 * row_count
+        joined.append(pair_join(normed, 1))
+    full_up = gather_half(after(shards[1], joined))
+    full_down = gather_half(shards[2])
+    mlp_rows, first = [], None
+    for m in micros:
+        blocks = spread(joined[m] if first is None else after(joined[m], first), False)
+        if first is None:
+            first = blocks[1:3]
+            grad_rows = gather_rows(after(grad_blocks, first), micro_count)
+        mlp_rows.append(gather_rows(blocks, 1))
+
     hidden, gate_val, up_val = [], [], []
     for m in micros:
-        gate_up = dot(mlp_rows[m], full_gu, 1, 0)
-        gate = gate_up[:, :half_cols]
-        up = gate_up[:, half_cols:]
+        gate, up, hid = ffn_forward(mlp_rows[m], full_gate, full_up)
         gate_val.append(gate)
         up_val.append(up)
-        hidden.append((gate * jax.nn.sigmoid(gate) * up).astype(BF16))
+        hidden.append(hid)
     hidden = jnp.concatenate(hidden, axis=0)
     down_grad = dot(grad_rows, hidden, 0, 0).astype(BF16)
     full_down = after(full_down, down_grad)
     part_down = scatter_half(down_grad)
-    grad_gu = []
-    for m in micros:
-        rows = grad_rows[m * ffn_rows : (m + 1) * ffn_rows]
-        grad_hidden = dot(rows, full_down, 1, 0)
-        sig = jax.nn.sigmoid(gate_val[m])
-        slope = sig * (1.0 + gate_val[m] * (1.0 - sig))
-        grad_gu.append(
-            jnp.concatenate(
-                [
-                    (grad_hidden * up_val[m] * slope).astype(BF16),
-                    (grad_hidden * gate_val[m] * sig).astype(BF16),
-                ],
-                axis=1,
-            )
-        )
-    normed_part = [dot(grad_gu[m], full_gu, 1, 1) for m in micros]
-    gu_left = jnp.concatenate(after(mlp_rows, normed_part), axis=0)
-    gu_right = jnp.concatenate(grad_gu, axis=0)
-    gu_grad = dot(gu_left, gu_right, 0, 0).astype(BF16)
+    grad_gu, normed_part = [], []
+    for m in micros:
+        gate, up = ffn_back(grad_rows, m, full_down, gate_val[m], up_val[m])
+        grad_gu.append(jnp.concatenate([gate, up], axis=1))
+        normed_part.append(to_peers([gate, up], [full_gate, full_up], 1, n_tensor))
+    all_mlp_rows = jnp.concatenate(after(mlp_rows, normed_part), axis=0)
+    gu_grad = dot(all_mlp_rows, jnp.concatenate(grad_gu, axis=0), 0, 0).astype(BF16)
     part_gu = scatter_half(after(gu_grad, part_down))
     grad_resid, grad_mix, branch_rows = [], [], []
     mlp_gain_sum = jnp.zeros((model_width,), F32)
     for m in micros:
-        total = collect(peer_blocks(normed_part[m], 1, n_tensor), False)
+        total = collect(normed_part[m])
         grad_normed = total[:own_rows] + swap(
             total[own_rows:].astype(BF16), "fsdp", PAIR
         ).astype(F32)
@@ -579,13 +680,12 @@
         1,
     ).astype(BF16)
 
-    mlp_rows_out = dot(after(hidden, out_grad), full_down, 1, 1)
-    mlp_blocks = peer_blocks(mlp_rows_out, micro_count, n_tensor)
+    mlp_blocks = to_peers([after(hidden, out_grad)], [full_down], micro_count, n_tensor)
     own_out = scatter(after(out_grad, part_gu))
 
     grad_raw = []
     for m in micros:
-        grad_out = after(grad_out_all, mlp_rows_out, part_down if m else own_out)
+        grad_out = after(grad_out_all, mlp_blocks, part_down if m else own_out)
         packed_grad = attend_back(pair_prefix[m], packed[m], attn_out[m], grad_out, attn_lse[m], m)
         grad_raw.append(split.to_spans(packed_grad))
 
@@ -597,8 +697,8 @@
         3 * head_cols, all_rows
     )
     qkv_grad = dot(normed_rows, grad_qkv, 0, 1).astype(BF16)
-    own_down = settle_half(part_down, side, 1, qkv_grad)
-    own_gu = settle_half(part_gu, side, 2, qkv_grad)
+    own_gate, own_up = settle_half(part_gu, side, 2, qkv_grad)
+    (own_down,) = settle_half(part_down, side, 1, qkv_grad)
     part = dot(after(grad_qkv, qkv_grad), full_qkv, 0, 1)
     grad_normed = collect(peer_blocks(part, micro_count, n_tensor))
     mlp_part = collect(mlp_blocks, token=part)
@@ -642,9 +742,9 @@
         own_qkv[:, 2 * head_cols :],
         own_out,
         own_gain[1],
-        own_gu[0],
-        own_gu[1],
-        own_down[0],
+        own_gate,
+        own_up,
+        own_down,
         rms_stats,
     )
 

time: 1100 us -> 1160 us (1.055)
  matrix products: 182 us -> 83.7 us
  Pallas kernels: 80.8 us -> 174 us
  waiting for transfers between devices: 534 us -> 596 us
    dot_general x17 -> x10, matrix products: 182 us -> 83.7 us  [dot(): lax.dot_general(left, right, (((left_dim,), (right_dim,)), ((), ())), pre...]
    pallas_call x0 -> x7, Pallas kernels: none -> 93.1 us  [the longest x3 41.7 us: to_peers(): pl.pallas_call(functools.partial(to_peers_kernel, terms, micros), grid=(w...]
    ppermute x57 -> x56, waiting for transfers between devices: 417 us -> 466 us  [swap(): return lax.ppermute(value, axis, [(a, a ^ distance) for a in range(count)])]
    unnamed x237 -> x146, local copies, waits for them, and re-layouts: 31.7 us -> 52.2 us
    ppermute x57 -> x56, starting transfers between devices: 61.2 us -> 63.3 us  [swap(): return lax.ppermute(value, axis, [(a, a ^ distance) for a in range(count)])]
  transfers between devices with their start and end apart: 71 -> 71, of which waited for: 43 -> 41; matrix products, arithmetic and copies ran while one was open for 30% -> 20% of each run, Pallas kernels for 7% -> 15%
where the time goes in v1:
time: 1160 us; the launch traced here: 1140 us
  waiting for transfers between devices  596 us (51%)
  Pallas kernels  174 us (15%)
  local copies, waits for them, and re-layouts  113 us (10%)
  starting transfers between devices  88.9 us (8%)
  matrix products  83.7 us (7%)
  other arithmetic  59.6 us (5%)
  between operations  15.7 us (1%)
  blocking collectives  13.5 us (1%)
    ppermute x56, waiting for transfers between devices, swap(): return lax.ppermute(value, axis, [(a, a ^ distance) for a in range(count)])  466 us
    dot_general x10, matrix products, dot(): lax.dot_general(left, right, (((left_dim,), (right_dim,)), ((), ())), pre...  83.7 us
    all_to_all x3, waiting for transfers between devices, to_heads(): lax.all_to_all(stack, 'fsdp', split_axis=0, concat_axis=0, tiled=True)  73.1 us
    ppermute x56, starting transfers between devices, swap(): return lax.ppermute(value, axis, [(a, a ^ distance) for a in range(count)])  63.3 us
    all_to_all x3, waiting for transfers between devices, to_spans(): lax.all_to_all(stack, 'fsdp', split_axis=0, concat_axis=0, tiled=True)  55.3 us
    unnamed x146, local copies, waits for them, and re-layouts  52.2 us
    pallas_call x3, Pallas kernels, to_peers(): pl.pallas_call(functools.partial(to_peers_kernel, terms, micros), grid=(w...  41.7 us
    pallas_call x2, Pallas kernels, attend_back(): pl.pallas_call(backward_kernel, out_shape=jax.ShapeDtypeStruct(grad_shape...  41.4 us
  transfers between devices with their start and end apart: 71, of which 41 were waited for; matrix products, arithmetic and copies ran while one was open for 20% of the time, Pallas kernels for 15%

profile of v1, /device:TPU:0, one launch (start us, length us, event | category | flops | bytes accessed | tf_op | source)
XLA Modules:
  0.0 1144.2 jit_solution(13656293970575469112)
XLA Ops:
  28.8 22.2 %collective-permute-done = bf16[256,2048]{1,0:T(8,128)(2,1)} collective-permute-done((bf16[256,2048]{1,0:T(8,128)(2,1)S(1)}, bf16[256,2048]{1,0:T(8,128)(2,1)}, u32[]{:S(2)}, u32[]{:S(2)}) %collective-permute-start) | collective-permute-done | bytes 1048608 | tf_op jit(solution)/shard_map/ppermute | solution.py:57
  111.7 47.4 %all-to-all-done.1.x_ref = bf16[8,4,192,128]{3,2,1,0:T(8,128)(2,1)S(1)} async-done(((bf16[8,4,192,128]{3,2,1,0:T(8,128)(2,1)}), bf16[8,4,192,128]{3,2,1,0:T(8,128)(2,1)S(1)}, u32[]{:S(2)}, u32[]{:S(2)}) %all-to-all-start.1) | async-done | bytes 1572896 | tf_op jit(solution)/shard_map/all_to_all | solution.py:490
  170.3 19.3 %attend_forward.2 = (bf16[8,4,64,128]{3,2,1,0:T(8,128)(2,1)}, f32[4,1,1024]{2,1,0:T(1,128)}) custom-call(s32[4]{0:T(128)} %get-tuple-element.171.prefix_ref, bf16[8,4,192,128]{3,2,1,0:T(8,128)(2,1)} %copy-done.5), custom_call_target="tpu_custom_call" | custom-call | tf_op jit(solution)/shard_map/attend_forward/pallas_call | solution.py:316
  201.3 20.1 %attend_forward.3 = (bf16[8,4,64,128]{3,2,1,0:T(8,128)(2,1)}, f32[4,1,1024]{2,1,0:T(1,128)}) custom-call(s32[4]{0:T(128)} %get-tuple-element.170.prefix_ref, bf16[8,4,192,128]{3,2,1,0:T(8,128)(2,1)} %all-to-all-done.x_ref), custom_call_target="tpu_custom_call" | custom-call | tf_op jit(solution)/shard_map/attend_forward/pallas_call | solution.py:316
  232.3 21.4 %all-to-all-done.2 = bf16[8,8,64,128]{3,2,1,0:T(8,128)(2,1)S(1)} async-done(((bf16[8,8,64,128]{3,2,1,0:T(8,128)(2,1)}), bf16[8,8,64,128]{3,2,1,0:T(8,128)(2,1)S(1)}, u32[]{:S(2)}, u32[]{:S(2)}) %all-to-all-start.2) | async-done | bytes 1048608 | tf_op jit(solution)/shard_map/all_to_all | solution.py:494
  348.1 41.5 %collective-permute-done.21 = bf16[256,2048]{1,0:T(8,128)(2,1)S(1)} collective-permute-done((bf16[256,2048]{1,0:T(8,128)(2,1)S(1)}, bf16[256,2048]{1,0:T(8,128)(2,1)S(1)}, u32[]{:S(2)}, u32[]{:S(2)}) %collective-permute-start.21) | collective-permute-done | bytes 1048608 | tf_op jit(solution)/shard_map/ppermute | solution.py:57
  403.7 92.5 %collective-permute-done.12 = bf16[256,2048]{1,0:T(8,128)(2,1)S(1)} collective-permute-done((bf16[256,2048]{1,0:T(8,128)(2,1)}, bf16[256,2048]{1,0:T(8,128)(2,1)S(1)}, u32[]{:S(2)}, u32[]{:S(2)}) %collective-permute-start.12) | collective-permute-done | bytes 1048608 | tf_op jit(solution)/shard_map/ppermute | solution.py:57
  515.1 19.0 %collective-permute-done.13 = bf16[128,2048]{1,0:T(8,128)(2,1)S(1)} collective-permute-done((bf16[128,2048]{1,0:T(8,128)(2,1)S(1)}, bf16[128,2048]{1,0:T(8,128)(2,1)S(1)}, u32[]{:S(2)}, u32[]{:S(2)}) %collective-permute-start.13) | collective-permute-done | bytes 524320 | tf_op jit(solution)/shard_map/ppermute | solution.py:57
  549.5 13.9 %ffn_forward.3 = (f32[1024,1024]{1,0:T(8,128)}, f32[1024,1024]{1,0:T(8,128)}, bf16[1024,1024]{1,0:T(8,128)(2,1)}) custom-call(bf16[1024,2048]{1,0:T(8,128)(2,1)} %constant_dynamic-update-slice_fusion.30.x_ref, bf16[2048,1024]{1,0:T(8,128)(2,1)} %all-gather.10.cloned.1.call-done.wg_ref.refs_2_, bf16[2048,1024]{1,0:T(8,128)(2,1)} %all-gather.12.cloned.1.call-done.wu_ref.refs_3_), custom_call_target="tpu_custom_call" | custom-call | tf_op jit(solution)/shard_map/ffn_forward/pallas_call | solution.py:391
  563.5 13.9 %ffn_forward.2 = (f32[1024,1024]{1,0:T(8,128)}, f32[1024,1024]{1,0:T(8,128)}, bf16[1024,1024]{1,0:T(8,128)(2,1)}) custom-call(bf16[1024,2048]{1,0:T(8,128)(2,1)} %constant_dynamic-update-slice_fusion.11.x_ref, bf16[2048,1024]{1,0:T(8,128)(2,1)} %all-gather.10.cloned.1.call-done.wg_ref.refs_2_, bf16[2048,1024]{1,0:T(8,128)(2,1)} %all-gather.12.cloned.1.call-done.wu_ref.refs_3_), custom_call_target="tpu_custom_call" | custom-call | tf_op jit(solution)/shard_map/ffn_forward/pallas_call | solution.py:391
  646.5 24.9 %fusion.11 = bf16[2048,2048]{1,0:T(8,128)(2,1)} fusion(bf16[1024,1024]{1,0:T(8,128)(2,1)} %get-tuple-element.101.refs_1_, bf16[1024,1024]{1,0:T(8,128)(2,1)} %get-tuple-element.100.refs_0_, bf16[1024,1024]{1,0:T(8,128)(2,1)} %get-tuple-element.93.refs_1_, bf16[1024,1024]{1,0:T(8,128)(2,1)} %get-tuple-element.92.refs_0_, ...), kind=kOutput, calls=%fused_computation.13 | convolution fusion | flops 17234395136 | bytes 25165824 | tf_op jit(solution)/shard_map/dot_general | solution.py:24
  676.7 21.0 %collective-permute-done.32 = bf16[256,2048]{1,0:T(8,128)(2,1)S(1)} collective-permute-done((bf16[256,2048]{1,0:T(8,128)(2,1)}, bf16[256,2048]{1,0:T(8,128)(2,1)S(1)}, u32[]{:S(2)}, u32[]{:S(2)}) %collective-permute-start.32) | collective-permute-done | bytes 1048608 | tf_op jit(solution)/shard_map/ppermute | solution.py:57
  698.8 23.1 %collective-permute-done.33 = bf16[256,2048]{1,0:T(8,128)(2,1)S(1)} collective-permute-done((bf16[256,2048]{1,0:T(8,128)(2,1)}, bf16[256,2048]{1,0:T(8,128)(2,1)S(1)}, u32[]{:S(2)}, u32[]{:S(2)}) %collective-permute-start.33) | collective-permute-done | bytes 1048608 | tf_op jit(solution)/shard_map/ppermute | solution.py:57
  725.9 16.9 %collective-permute-done.25 = bf16[256,2048]{1,0:T(8,128)(2,1)S(1)} collective-permute-done((bf16[256,2048]{1,0:T(8,128)(2,1)}, bf16[256,2048]{1,0:T(8,128)(2,1)S(1)}, u32[]{:S(2)}, u32[]{:S(2)}) %collective-permute-start.25) | collective-permute-done | bytes 1048608 | tf_op jit(solution)/shard_map/ppermute | solution.py:57
  742.7 20.4 %collective-permute-done.26 = bf16[256,2048]{1,0:T(8,128)(2,1)S(1)} collective-permute-done((bf16[256,2048]{1,0:T(8,128)(2,1)}, bf16[256,2048]{1,0:T(8,128)(2,1)S(1)}, u32[]{:S(2)}, u32[]{:S(2)}) %collective-permute-start.26) | collective-permute-done | bytes 1048608 | tf_op jit(solution)/shard_map/ppermute | solution.py:57
  765.2 28.8 %collective-permute-done.28 = bf16[128,2048]{1,0:T(8,128)(2,1)S(1)} collective-permute-done((bf16[128,2048]{1,0:T(8,128)(2,1)S(1)}, bf16[128,2048]{1,0:T(8,128)(2,1)S(1)}, u32[]{:S(2)}, u32[]{:S(2)}) %collective-permute-start.28) | collective-permute-done | bytes 524320 | tf_op jit(solution)/shard_map/ppermute | solution.py:57
  866.5 14.0 %to_peers.5 = (f32[512,2048]{1,0:T(8,128)}, bf16[512,2048]{1,0:T(8,128)(2,1)}, bf16[512,2048]{1,0:T(8,128)(2,1)}, bf16[512,2048]{1,0:T(8,128)(2,1)}) custom-call(bf16[2048,1024]{1,0:T(8,128)(2,1)} %copy-done.6, bf16[2048,1024]{1,0:T(8,128)(2,1)} %all-gather.14.cloned.1.call-done.wd_ref.refs_1_), custom_call_target="tpu_custom_call" | custom-call | tf_op jit(solution)/shard_map/to_peers/pallas_call | solution.py:454
  880.4 14.1 %all-to-all-done.3.do_ref = bf16[8,8,64,128]{3,2,1,0:T(8,128)(2,1)} async-done(((bf16[8,8,64,128]{3,2,1,0:T(8,128)(2,1)}), bf16[8,8,64,128]{3,2,1,0:T(8,128)(2,1)}, u32[]{:S(2)}, u32[]{:S(2)}) %all-to-all-start.3) | async-done | bytes 1048608 | tf_op jit(solution)/shard_map/all_to_all | solution.py:490
  894.6 20.4 %attend_back.3 = bf16[8,4,192,128]{3,2,1,0:T(8,128)(2,1)} custom-call(s32[4]{0:T(128)} %get-tuple-element.171.prefix_ref, bf16[8,4,192,128]{3,2,1,0:T(8,128)(2,1)} %copy-done.5, bf16[8,4,64,128]{3,2,1,0:T(8,128)(2,1)} %get-tuple-element.73.o_ref, bf16[8,8,64,128]{3,2,1,0:T(8,128)(2,1)} %all-to-all-done.3.do_ref, f32[4,1,1024]{2,1,0:T(1,128)} %get-tuple-element.70.lse_ref), custom_call_target="tpu_custom_call" | custom-call | tf_op jit(solution)/shard_map/attend_back/pallas_call | solution.py:341
  921.3 21.0 %attend_back.2 = bf16[8,4,192,128]{3,2,1,0:T(8,128)(2,1)} custom-call(s32[4]{0:T(128)} %get-tuple-element.170.prefix_ref, bf16[8,4,192,128]{3,2,1,0:T(8,128)(2,1)} %all-to-all-done.x_ref, bf16[8,4,64,128]{3,2,1,0:T(8,128)(2,1)} %get-tuple-element.72.o_ref, bf16[8,8,64,128]{3,2,1,0:T(8,128)(2,1)} %all-to-all-done.3.do_ref, ...), custom_call_target="tpu_custom_call" | custom-call | tf_op jit(solution)/shard_map/attend_back/pallas_call | solution.py:341
  942.4 14.9 %all-to-all-done.5 = bf16[8,4,192,128]{3,2,1,0:T(8,128)(2,1)} async-done(((bf16[8,4,192,128]{3,2,1,0:T(8,128)(2,1)}), bf16[8,4,192,128]{3,2,1,0:T(8,128)(2,1)}, u32[]{:S(2)}, u32[]{:S(2)}) %all-to-all-start.5) | async-done | bytes 1572896 | tf_op jit(solution)/shard_map/all_to_all | solution.py:494
  980.6 18.9 %all-to-all-done.4 = bf16[8,4,192,128]{3,2,1,0:T(8,128)(2,1)} async-done(((bf16[8,4,192,128]{3,2,1,0:T(8,128)(2,1)}), bf16[8,4,192,128]{3,2,1,0:T(8,128)(2,1)}, u32[]{:S(2)}, u32[]{:S(2)}) %all-to-all-start.4) | async-done | bytes 1572896 | tf_op jit(solution)/shard_map/all_to_all | solution.py:494
  1037.1 21.6 %collective-permute-done.40 = bf16[512,2048]{1,0:T(8,128)(2,1)} collective-permute-done((bf16[512,2048]{1,0:T(8,128)(2,1)}, bf16[512,2048]{1,0:T(8,128)(2,1)}, u32[]{:S(2)}, u32[]{:S(2)}) %collective-permute-start.40) | collective-permute-done | bytes 2097184 | tf_op jit(solution)/shard_map/ppermute | solution.py:57
  1080.0 32.9 %collective-permute-done.42 = bf16[256,2048]{1,0:T(8,128)(2,1)S(1)} collective-permute-done((bf16[256,2048]{1,0:T(8,128)(2,1)S(1)}, bf16[256,2048]{1,0:T(8,128)(2,1)S(1)}, u32[]{:S(2)}, u32[]{:S(2)}) %collective-permute-start.42) | collective-permute-done | bytes 1048608 | tf_op jit(solution)/shard_map/ppermute | solution.py:57
  (436 shorter events, 524.3 us)
Async XLA Ops:
  7.2 76.4 %all-gather.6.cloned.1.call-start = ((), (), s32[]{:S(2)}) async-start(), calls=%async_computation.10 | async-start | bytes 7077888 | tf_op jit(solution)/shard_map/all_gather | solution.py:547
  100.9 58.2 %all-to-all-start.1 = ((bf16[8,4,192,128]{3,2,1,0:T(8,128)(2,1)}), bf16[8,4,192,128]{3,2,1,0:T(8,128)(2,1)S(1)}, u32[]{:S(2)}, u32[]{:S(2)}) async-start(bf16[8,4,192,128]{3,2,1,0:T(8,128)(2,1)} %bitcast.142), calls=%async_computation.1 | async-start | bytes 3145728 | tf_op jit(solution)/shard_map/all_to_all | solution.py:490
  104.5 65.8 %all-gather.8.cloned.1.call-start = ((), (), s32[]{:S(2)}) async-start(), calls=%async_computation.11 | async-start | bytes 2359296 | tf_op jit(solution)/shard_map/all_gather | solution.py:547
  167.8 59.8 %collective-permute-start.15 = (bf16[256,3072]{1,0:T(8,128)(2,1)}, bf16[256,3072]{1,0:T(8,128)(2,1)}, u32[]{:S(2)}, u32[]{:S(2)}) collective-permute-start(bf16[256,3072]{1,0:T(8,128)(2,1)} %pad_maximum_fusion.8), channel_id=1, source_target_pairs={{0,8},{4,12},{8,0},{12,4},{16,24},{20,28},{24,16},{28,20},{1,9},{5... | collective-permute-start | bytes 4718600 | tf_op jit(solution)/shard_map/ppermute | solution.py:57
  227.3 322.3 %all-gather.10.cloned.1.call-start = ((), (), s32[]{:S(2)}) async-start(), calls=%async_computation.12 | async-start | bytes 5242880 | tf_op jit(solution)/shard_map/all_gather | solution.py:151
  258.3 291.2 %all-gather.12.cloned.1.call-start = ((), (), s32[]{:S(2)}) async-start(), calls=%async_computation.13 | async-start | bytes 5242880 | tf_op jit(solution)/shard_map/all_gather | solution.py:151
  341.1 254.1 %all-gather.14.cloned.1.call-start = ((), (), s32[]{:S(2)}) async-start(), calls=%async_computation.14 | async-start | bytes 5242880 | tf_op jit(solution)/shard_map/all_gather | solution.py:151
  391.2 107.4 %collective-permute-start.24 = (bf16[512,2048]{1,0:T(8,128)(2,1)}, bf16[512,2048]{1,0:T(8,128)(2,1)}, u32[]{:S(2)}, u32[]{:S(2)}) collective-permute-start(bf16[512,2048]{1,0:T(8,128)(2,1)} %pad_maximum_fusion.4), channel_id=1, source_target_pairs={{0,3},{1,2},{2,1},{3,0},{4,7},{5,6},{6,5},{7,4},{8,11},{9,10},{10,... | collective-permute-start | bytes 6291464 | tf_op jit(solution)/shard_map/ppermute | solution.py:57
  393.5 106.5 %collective-permute-start.23 = (bf16[512,2048]{1,0:T(8,128)(2,1)}, bf16[512,2048]{1,0:T(8,128)(2,1)}, u32[]{:S(2)}, u32[]{:S(2)}) collective-permute-start(bf16[512,2048]{1,0:T(8,128)(2,1)} %pad_maximum_fusion.4), channel_id=1, source_target_pairs={{0,2},{1,3},{2,0},{3,1},{4,6},{5,7},{6,4},{7,5},{8,10},{9,11},{10,... | collective-permute-start | bytes 6291464 | tf_op jit(solution)/shard_map/ppermute | solution.py:57
  393.9 106.0 %collective-permute-start.22 = (bf16[512,2048]{1,0:T(8,128)(2,1)}, bf16[512,2048]{1,0:T(8,128)(2,1)}, u32[]{:S(2)}, u32[]{:S(2)}) collective-permute-start(bf16[512,2048]{1,0:T(8,128)(2,1)} %pad_maximum_fusion.4), channel_id=1, source_target_pairs={{0,1},{1,0},{2,3},{3,2},{4,5},{5,4},{6,7},{7,6},{8,9},{9,8},{10,11... | collective-permute-start | bytes 6291464 | tf_op jit(solution)/shard_map/ppermute | solution.py:57
  395.9 275.6 %reduce-scatter.5.cloned.1.call-start = ((), (), s32[]{:S(2)}) async-start(), calls=%async_computation.15 | async-start | bytes 5242880 | tf_op jit(solution)/shard_map/reduce_scatter | solution.py:161
  397.4 98.8 %collective-permute-start.12 = (bf16[256,2048]{1,0:T(8,128)(2,1)}, bf16[256,2048]{1,0:T(8,128)(2,1)S(1)}, u32[]{:S(2)}, u32[]{:S(2)}) collective-permute-start(bf16[256,2048]{1,0:T(8,128)(2,1)} %pad_maximum_fusion.10), channel_id=1, source_target_pairs={{0,2},{1,3},{2,0},{3,1},{4,6},{5,7},{6,4},{7,5},{8,10},{9,11},{10,... | collective-permute-start | bytes 3145736 | tf_op jit(solution)/shard_map/ppermute | solution.py:57
  398.7 97.7 %collective-permute-start.11 = (bf16[256,2048]{1,0:T(8,128)(2,1)}, bf16[256,2048]{1,0:T(8,128)(2,1)S(1)}, u32[]{:S(2)}, u32[]{:S(2)}) collective-permute-start(bf16[256,2048]{1,0:T(8,128)(2,1)} %pad_maximum_fusion.10), channel_id=1, source_target_pairs={{0,1},{1,0},{2,3},{3,2},{4,5},{5,4},{6,7},{7,6},{8,9},{9,8},{10,11... | collective-permute-start | bytes 3145736 | tf_op jit(solution)/shard_map/ppermute | solution.py:57
  594.7 271.7 %reduce-scatter.7.cloned.1.call-start = ((), (), s32[]{:S(2)}) async-start(), calls=%async_computation.16 | async-start | bytes 10485760 | tf_op jit(solution)/shard_map/reduce_scatter | solution.py:161
  675.0 67.7 %collective-permute-start.25 = (bf16[256,2048]{1,0:T(8,128)(2,1)}, bf16[256,2048]{1,0:T(8,128)(2,1)S(1)}, u32[]{:S(2)}, u32[]{:S(2)}) collective-permute-start(bf16[256,2048]{1,0:T(8,128)(2,1)} %get-tuple-element.95), channel_id=1, source_target_pairs={{0,1},{1,0},{2,3},{3,2},{4,5},{5,4},{6,7},{7,6},{8,9},{9,8},{10,11... | collective-permute-start | bytes 3145736 | tf_op jit(solution)/shard_map/ppermute | solution.py:57
  676.7 86.4 %collective-permute-start.26 = (bf16[256,2048]{1,0:T(8,128)(2,1)}, bf16[256,2048]{1,0:T(8,128)(2,1)S(1)}, u32[]{:S(2)}, u32[]{:S(2)}) collective-permute-start(bf16[256,2048]{1,0:T(8,128)(2,1)} %get-tuple-element.96), channel_id=1, source_target_pairs={{0,2},{1,3},{2,0},{3,1},{4,6},{5,7},{6,4},{7,5},{8,10},{9,11},{10,... | collective-permute-start | bytes 3145736 | tf_op jit(solution)/shard_map/ppermute | solution.py:57
  697.7 65.4 %collective-permute-start.27 = (bf16[256,2048]{1,0:T(8,128)(2,1)S(1)}, bf16[256,2048]{1,0:T(8,128)(2,1)S(1)}, u32[]{:S(2)}, u32[]{:S(2)}) collective-permute-start(bf16[256,2048]{1,0:T(8,128)(2,1)S(1)} %copy-done.34), channel_id=1, source_target_pairs={{0,3},{1,2},{2,1},{3,0},{4,7},{5,6},{6,5},{7,4},{8,11},{9,10},{10,... | collective-permute-start | bytes 3145736 | tf_op jit(solution)/shard_map/ppermute | solution.py:57
  860.2 59.3 %reduce-scatter.9.cloned.1.call-start = ((), (), s32[]{:S(2)}) async-start(), calls=%async_computation.17 | async-start | bytes 2359296 | tf_op jit(solution)/shard_map/reduce_scatter | solution.py:550
  961.6 173.4 %reduce-scatter.11.cloned.1.call-start = ((), (), s32[]{:S(2)}) async-start(), calls=%async_computation.18 | async-start | bytes 7077888 | tf_op jit(solution)/shard_map/reduce_scatter | solution.py:550
  964.2 72.9 %collective-permute-start.39 = (bf16[512,2048]{1,0:T(8,128)(2,1)}, bf16[512,2048]{1,0:T(8,128)(2,1)}, u32[]{:S(2)}, u32[]{:S(2)}) collective-permute-start(bf16[512,2048]{1,0:T(8,128)(2,1)} %get-tuple-element.113), channel_id=1, source_target_pairs={{0,1},{1,0},{2,3},{3,2},{4,5},{5,4},{6,7},{7,6},{8,9},{9,8},{10,11... | collective-permute-start | bytes 6291464 | tf_op jit(solution)/shard_map/ppermute | solution.py:57
  965.8 92.8 %collective-permute-start.40 = (bf16[512,2048]{1,0:T(8,128)(2,1)}, bf16[512,2048]{1,0:T(8,128)(2,1)}, u32[]{:S(2)}, u32[]{:S(2)}) collective-permute-start(bf16[512,2048]{1,0:T(8,128)(2,1)} %get-tuple-element.114), channel_id=1, source_target_pairs={{0,2},{1,3},{2,0},{3,1},{4,6},{5,7},{6,4},{7,5},{8,10},{9,11},{10,... | collective-permute-start | bytes 6291464 | tf_op jit(solution)/shard_map/ppermute | solution.py:57
  966.7 92.0 %collective-permute-start.41 = (bf16[512,2048]{1,0:T(8,128)(2,1)}, bf16[512,2048]{1,0:T(8,128)(2,1)}, u32[]{:S(2)}, u32[]{:S(2)}) collective-permute-start(bf16[512,2048]{1,0:T(8,128)(2,1)} %get-tuple-element.115), channel_id=1, source_target_pairs={{0,3},{1,2},{2,1},{3,0},{4,7},{5,6},{6,5},{7,4},{8,11},{9,10},{10,... | collective-permute-start | bytes 6291464 | tf_op jit(solution)/shard_map/ppermute | solution.py:57
  968.6 56.0 %collective-permute-start.52 = (bf16[256,1024]{1,0:T(8,128)(2,1)}, bf16[256,1024]{1,0:T(8,128)(2,1)}, u32[]{:S(2)}, u32[]{:S(2)}) collective-permute-start(bf16[256,1024]{1,0:T(8,128)(2,1)} %constant_dynamic-slice_fusion.1), channel_id=1, source_target_pairs={{0,8},{4,12},{8,0},{12,4},{16,24},{20,28},{24,16},{28,20},{1,9},{5... | collective-permute-start | bytes 1572872 | tf_op jit(solution)/shard_map/ppermute | solution.py:57
  1058.7 55.6 %collective-permute-start.44 = (bf16[256,2048]{1,0:T(8,128)(2,1)S(1)}, bf16[256,2048]{1,0:T(8,128)(2,1)S(1)}, u32[]{:S(2)}, u32[]{:S(2)}) collective-permute-start(bf16[256,2048]{1,0:T(8,128)(2,1)S(1)} %pad_maximum_fusion.18), channel_id=1, source_target_pairs={{0,2},{1,3},{2,0},{3,1},{4,6},{5,7},{6,4},{7,5},{8,10},{9,11},{10,... | collective-permute-start | bytes 3145736 | tf_op jit(solution)/shard_map/ppermute | solution.py:57
  (85 other events, 1630.7 us)
Sparse Core Ops, SparseCore 0:
  10.2 67.4 all-gather.5
  106.9 50.4 all-gather.7
  258.4 55.8 all-gather.9
  341.2 57.8 all-gather.11
  400.5 56.8 all-gather.13
  594.8 68.8 reduce-scatter.4
  671.6 118.2 reduce-scatter.6
  866.6 41.6 reduce-scatter.8
  1024.7 89.5 reduce-scatter.10

commit v2 on v1

--- a/solution.py
+++ b/solution.py
@@ -40,18 +40,6 @@
     )
 
 
-def rotate(values, cos_tab, sin_tab, rot_sign):
-    first_half = values[..., 0, :, :]
-    second = values[..., 1, :, :]
-    return jnp.stack(
-        [
-            first_half * cos_tab - rot_sign * second * sin_tab,
-            second * cos_tab + rot_sign * first_half * sin_tab,
-        ],
-        axis=-3,
-    )
-
-
 def swap(value, axis, distance):
     count = lax.axis_size(axis)
     return lax.ppermute(value, axis, [(a, a ^ distance) for a in range(count)])
@@ -61,7 +49,7 @@
     return lax.optimization_barrier((value, others))[0]
 
 
-def spread(value, direct=True):
+def spread_pieces(value, direct=True):
     count = lax.axis_size("tensor")
     if direct or count != 4:
         return [value] + [swap(value, "tensor", k) for k in range(1, count)]
@@ -70,7 +58,19 @@
     two = swap(value, "tensor", 2)
     low = swap(two[:half], "tensor", 1)
     high = swap(one[half:], "tensor", 2)
-    return [value, one, two, jnp.concatenate([low, high], axis=0)]
+    return [value, one, two, low, high]
+
+
+def whole_blocks(pieces):
+    rows = pieces[0].shape[0]
+    far = [p for p in pieces if p.shape[0] < rows]
+    return [p for p in pieces if p.shape[0] == rows] + (
+        [jnp.concatenate(far, axis=0)] if far else []
+    )
+
+
+def spread(value, direct=True):
+    return whole_blocks(spread_pieces(value, direct))
 
 
 def collect(parts, direct=True, token=None):
@@ -106,17 +106,6 @@
     return jnp.concatenate(
         [b[m * size : (m + 1) * size] for m in range(micros) for b in blocks], axis=0
     )
-
-
-def peer_blocks(rows, micros, peers):
-    size = rows.shape[0] // (micros * peers)
-    return [
-        jnp.concatenate(
-            [rows[(m * peers + k) * size : (m * peers + k + 1) * size] for m in range(micros)],
-            axis=0,
-        )
-        for k in range(peers)
-    ]
 
 
 def paired(values):
@@ -464,46 +453,178 @@
     )(*lefts, *rights)
 
 
+def turn(values, cos_tab, sin_tab):
+    half = HEAD_DIM // 2
+    first, second = values[:half], values[half:]
+    return jnp.concatenate(
+        [first * cos_tab - second * sin_tab, second * cos_tab + first * sin_tab], axis=0
+    )
+
+
+def project_kernel(labels, *refs):
+    count = len(labels)
+    wq_ref, wk_ref, wv_ref, cos_ref, sin_ref = refs[count : count + 5]
+    outs = refs[count + 5 :]
+    span = outs[0].shape[3]
+    weights = jnp.concatenate([wq_ref[...], wk_ref[...], wv_ref[...]], axis=1)
+    for ref, places in zip(refs, labels):
+        cols_all = dot(ref[...], weights, 1, 0).T
+        for i, (m, k) in enumerate(places):
+            cols = cols_all[:, i * span : (i + 1) * span]
+            cos_tab = cos_ref[m, :, k * span : (k + 1) * span]
+            sin_tab = sin_ref[m, :, k * span : (k + 1) * span]
+            for h in range(2):
+                for kind in range(3):
+                    first = (2 * kind + h) * HEAD_DIM
+                    value = cols[first : first + HEAD_DIM]
+                    if kind < 2:
+                        value = turn(value, cos_tab, sin_tab)
+                    outs[m][h, k, kind * HEAD_DIM : (kind + 1) * HEAD_DIM, :] = value.astype(BF16)
+
+
+def project(pieces, labels, weights, cos_tab, sin_tab, span):
+    micros, _, tokens = cos_tab.shape
+    width = weights.shape[0]
+    cols = weights.shape[1] // 3
+    blocks = cols // (2 * HEAD_DIM)
+    seqs = tokens // span
+    out = (cols // HEAD_DIM, seqs, 3 * HEAD_DIM, span)
+    return pl.pallas_call(
+        functools.partial(project_kernel, labels),
+        grid=(blocks,),
+        in_specs=[whole(p.shape) for p in pieces]
+        + [
+            pl.BlockSpec((width, 2 * HEAD_DIM), lambda n, kind=kind: (0, kind * blocks + n))
+            for kind in range(3)
+        ]
+        + [whole(cos_tab.shape)] * 2,
+        out_specs=[pl.BlockSpec((2,) + out[1:], lambda n: (n, 0, 0, 0))] * micros,
+        out_shape=[jax.ShapeDtypeStruct(out, BF16)] * micros,
+        name="project",
+    )(*pieces, weights, weights, weights, cos_tab, sin_tab)
+
+
+def mix_out_kernel(micros, x_ref, w_ref, mix_ref, *outs):
+    heads, seqs, _, span = x_ref.shape
+    peers = len(outs) // micros
+    own = seqs // (micros * peers)
+
+    @pl.when(pl.program_id(0) == 0)
+    def _():
+        for q in range(seqs):
+            mix = x_ref[:, q].reshape(heads * HEAD_DIM, span)
+            mix_ref[q * span : (q + 1) * span, :] = mix.T
+
+    total = dot(mix_ref[...], w_ref[...], 1, 1)
+    size = own * span
+    for i, out in enumerate(outs):
+        out[...] = total[i * size : (i + 1) * size].astype(out.dtype)
+
+
+def mix_out(packed, weights, micros, peers):
+    _, seqs, _, span = packed.shape
+    width, cols = weights.shape
+    tile = tile_of(width)
+    rows = seqs * span // (micros * peers)
+    kinds = [BF16 if k else F32 for _ in range(micros) for k in range(peers)]
+    return pl.pallas_call(
+        functools.partial(mix_out_kernel, micros),
+        grid=(width // tile,),
+        in_specs=[whole(packed.shape), pl.BlockSpec((tile, cols), lambda n: (n, 0))],
+        out_specs=[pl.BlockSpec((seqs * span, cols), lambda n: (0, 0))]
+        + [col_tile(rows, tile)] * len(kinds),
+        out_shape=[jax.ShapeDtypeStruct((seqs * span, cols), BF16)]
+        + [jax.ShapeDtypeStruct((rows, width), kind) for kind in kinds],
+        name="mix_out",
+    )(packed, weights)
+
+
+def mix_back_kernel(*refs):
+    pieces, (w_ref, out_ref) = refs[:-2], refs[-2:]
+    heads, _, _, span = out_ref.shape
+    q = 0
+    for ref in pieces:
+        cols = dot(ref[...], w_ref[...], 1, 0).T.astype(BF16)
+        for i in range(ref.shape[0] // span):
+            for h in range(heads):
+                out_ref[h, q] = cols[
+                    h * HEAD_DIM : (h + 1) * HEAD_DIM, i * span : (i + 1) * span
+                ]
+            q += 1
+
+
+def mix_back(pieces, weights, span):
+    width, cols = weights.shape
+    tile = tile_of(cols)
+    seqs = sum(p.shape[0] for p in pieces) // span
+    heads = cols // HEAD_DIM
+    return pl.pallas_call(
+        mix_back_kernel,
+        grid=(cols // tile,),
+        in_specs=[whole(p.shape) for p in pieces] + [col_tile(width, tile)],
+        out_specs=pl.BlockSpec((tile // HEAD_DIM, seqs, HEAD_DIM, span), lambda n: (n, 0, 0, 0)),
+        out_shape=jax.ShapeDtypeStruct((heads, seqs, HEAD_DIM, span), BF16),
+        name="mix_back",
+    )(*pieces, weights)
+
+
+def unturn_kernel(blocks, *refs):
+    packed, (cos_ref, sin_ref, out_ref) = refs[:-3], refs[-3:]
+    _, seqs, _, span = packed[0].shape
+    plain = pl.program_id(0) >= 2 * blocks
+    for m, ref in enumerate(packed):
+        for k in range(seqs):
+            cos_tab = jnp.where(plain, 1.0, cos_ref[m, :, k * span : (k + 1) * span])
+            sin_tab = jnp.where(plain, 0.0, -sin_ref[m, :, k * span : (k + 1) * span])
+            pair = jnp.concatenate(
+                [turn(ref[h, k].astype(F32), cos_tab, sin_tab) for h in range(2)], axis=0
+            )
+            first = (m * seqs + k) * span
+            out_ref[first : first + span, :] = pair.T.astype(BF16)
+
+
+def unturn(packed, cos_tab, sin_tab):
+    heads, seqs, _, span = packed[0].shape
+    blocks = heads // 2
+    rows = len(packed) * seqs * span
+    return pl.pallas_call(
+        functools.partial(unturn_kernel, blocks),
+        grid=(3 * blocks,),
+        in_specs=[
+            pl.BlockSpec(
+                (2, seqs, HEAD_DIM, span), lambda n: (n % blocks, 0, n // blocks, 0)
+            )
+        ]
+        * len(packed)
+        + [whole(cos_tab.shape)] * 2,
+        out_specs=col_tile(rows, 2 * HEAD_DIM),
+        out_shape=jax.ShapeDtypeStruct((rows, 3 * heads * HEAD_DIM), BF16),
+        name="unturn",
+    )(*packed, cos_tab, sin_tab)
+
+
 class HeadSplit:
-    def __init__(self, n_fsdp, head_count, seqs, span_len):
+    def __init__(self, n_fsdp, head_count, seqs):
         self.head_groups = math.gcd(n_fsdp, head_count)
         self.seq_groups = n_fsdp // self.head_groups
         self.heads_per = head_count // self.head_groups
         self.seqs_per = seqs // self.seq_groups
-        self.span_len = span_len
-
-    def to_heads(self, stack):
-        kinds = stack.shape[0]
-        stack = stack.reshape(
-            kinds,
-            self.head_groups,
-            self.heads_per,
-            HEAD_DIM,
-            -1,
-            self.seq_groups,
-            self.seqs_per,
-            self.span_len,
-        )
-        stack = stack.transpose(5, 1, 4, 2, 6, 0, 3, 7)
-        count = self.seq_groups * self.head_groups
-        stack = stack.reshape(count, -1, kinds * HEAD_DIM, self.span_len)
-        return lax.all_to_all(stack, "fsdp", split_axis=0, concat_axis=0, tiled=True)
-
-    def to_spans(self, stack):
-        kinds = stack.shape[2] // HEAD_DIM
-        stack = lax.all_to_all(stack, "fsdp", split_axis=0, concat_axis=0, tiled=True)
-        stack = stack.reshape(
-            self.seq_groups,
-            self.head_groups,
-            -1,
-            self.heads_per,
-            self.seqs_per,
-            kinds,
-            HEAD_DIM,
-            self.span_len,
-        )
-        stack = stack.transpose(5, 1, 3, 6, 2, 0, 4, 7)
-        return stack.reshape(kinds, self.head_groups * self.heads_per * HEAD_DIM, -1)
+
+    def to_heads(self, packed):
+        width, span = packed.shape[2:]
+        packed = packed.reshape(
+            self.head_groups, self.heads_per, -1, self.seq_groups, self.seqs_per, width, span
+        ).transpose(3, 0, 2, 1, 4, 5, 6)
+        packed = packed.reshape(self.seq_groups * self.head_groups, -1, width, span)
+        return lax.all_to_all(packed, "fsdp", split_axis=0, concat_axis=0, tiled=True)
+
+    def to_spans(self, packed):
+        width, span = packed.shape[2:]
+        packed = lax.all_to_all(packed, "fsdp", split_axis=0, concat_axis=0, tiled=True)
+        packed = packed.reshape(
+            self.seq_groups, self.head_groups, -1, self.heads_per, self.seqs_per, width, span
+        ).transpose(1, 3, 2, 0, 4, 5, 6)
+        return packed.reshape(self.head_groups * self.heads_per, -1, width, span)
 
     def pair_prefix(self, prefix, fsdp_index):
         mine = lax.dynamic_slice_in_dim(
@@ -532,7 +653,6 @@
     n_fsdp = lax.axis_size("fsdp")
     seq_mb = seq_dev * n_tensor
     seq_len = span_len * n_fsdp
-    row_count = seq_mb * span_len
     own_rows = seq_dev * span_len
     head_cols = w_query.shape[1]
     head_count = head_cols // HEAD_DIM
@@ -540,7 +660,7 @@
     fsdp_index = lax.axis_index("fsdp")
     tensor_index = lax.axis_index("tensor")
     query_index = fsdp_index * span_len + jnp.arange(span_len, dtype=jnp.int32)
-    split = HeadSplit(n_fsdp, head_count, seq_mb, span_len)
+    split = HeadSplit(n_fsdp, head_count, seq_mb)
     micros = range(micro_count)
 
     def gather(shard):
@@ -571,29 +691,36 @@
     grad_own = out_grads.reshape(micro_count * own_rows, model_width)
     unit_attn, scale_attn = normalize(x_float)
     normed = (unit_attn * gain_attn).astype(BF16)
-    normed_blocks = spread(normed, False)
-    normed_rows = gather_rows(normed_blocks, micro_count)
+    normed_pieces = spread_pieces(normed, False)
     cos_tab, sin_tab, pair_prefix = [], [], []
     for m in micros:
         angles = inverse[:, None] * pos_all[m].astype(F32).reshape(-1)[None, :]
         cos_tab.append(jnp.cos(angles))
         sin_tab.append(jnp.sin(angles))
         pair_prefix.append(split.pair_prefix(prefix_all[m], fsdp_index))
-    cos_all = jnp.concatenate(cos_tab, axis=1)
-    sin_all = jnp.concatenate(sin_tab, axis=1)
-    all_rows = micro_count * row_count
+    cos_all = jnp.stack(cos_tab)
+    sin_all = jnp.stack(sin_tab)
     half_cols = ff_cols // 2
     ffn_near = half_of([w_gate, w_up, w_down], side)
     ffn_far = half_of([w_gate, w_up, w_down], 1 - side)
     grad_pair = pair_join(after(paired(grad_own), full_qkv), micro_count)
-    raw = dot(full_qkv, normed_rows, 0, 1).reshape(3, head_cols, all_rows)
-    turned = rotate(
-        raw[:2].reshape(2, head_count, 2, half_dim, all_rows), cos_all, sin_all, 1.0
-    ).reshape(2, head_cols, all_rows)
-    stack = jnp.concatenate([turned.astype(BF16), raw[2:].astype(BF16)], axis=0)
+    labels, taken = [], [0] * n_tensor
+    spans_of = [(m, r) for m in micros for r in range(seq_dev)]
+    peer = 0
+    for piece in normed_pieces:
+        size = piece.shape[0] // span_len
+        start = taken[peer]
+        labels.append(
+            tuple((m, peer * seq_dev + r) for m, r in spans_of[start : start + size])
+        )
+        taken[peer] += size
+        if taken[peer] == len(spans_of):
+            peer += 1
+    stack = project(normed_pieces, tuple(labels), full_qkv, cos_all, sin_all, span_len)
     packed = []
     for m in micros:
-        packed.append(split.to_heads(stack[:, :, m * row_count : (m + 1) * row_count]))
+        packed.append(split.to_heads(stack[m]))
+    normed_rows = gather_rows(whole_blocks(after(normed_pieces, stack)), micro_count)
     grad_pair = after(grad_pair, stack)
     grad_blocks = spread(grad_pair)
     ffn_other = swap(after(ffn_far, packed[-1]), "fsdp", PAIR)
@@ -602,7 +729,7 @@
     for m in reversed(micros):
         attn_out[m], attn_lse[m] = attend_forward(pair_prefix[m], after(packed[m], done))
         done = attn_lse[m]
-    mix_all = split.to_spans(jnp.concatenate(attn_out, axis=1))[0]
+    mix_packed = split.to_spans(jnp.concatenate(attn_out, axis=1))
     ffn_other = after(ffn_other, attn_lse)
     shards = [
         own_half(
@@ -612,14 +739,11 @@
         )
         for i in range(3)
     ]
-    full_gate = gather_half(after(shards[0], mix_all))
+    full_gate = gather_half(after(shards[0], mix_packed))
     branch, resid, unit_mlp, scale_mlp, joined = [], [], [], [], []
-    parts = []
+    mix_rows, *parts = mix_out(mix_packed, full_out, micro_count, n_tensor)
     for m in micros:
-        mix = mix_all[:, m * row_count : (m + 1) * row_count]
-        parts.append(dot(after(mix, parts) if parts else mix, full_out, 0, 1))
-    for m in micros:
-        part = collect(peer_blocks(parts[m], 1, n_tensor))
+        part = collect(parts[m * n_tensor : (m + 1) * n_tensor])
         res = x_float[m * own_rows : (m + 1) * own_rows] + part
         unit, scale = normalize(res)
         branch.append(part)
@@ -656,7 +780,7 @@
     all_mlp_rows = jnp.concatenate(after(mlp_rows, normed_part), axis=0)
     gu_grad = dot(all_mlp_rows, jnp.concatenate(grad_gu, axis=0), 0, 0).astype(BF16)
     part_gu = scatter_half(after(gu_grad, part_down))
-    grad_resid, grad_mix, branch_rows = [], [], []
+    grad_resid, branch_rows = [], []
     mlp_gain_sum = jnp.zeros((model_width,), F32)
     for m in micros:
         total = collect(normed_part[m])
@@ -669,15 +793,11 @@
         grad_resid.append(grad_res)
         if m == 0:
             grad_res = after(grad_res, gu_grad)
-        rows = gather_rows(spread(grad_res.astype(BF16)), 1)
-        branch_rows.append(rows)
-        grad_mix.append(dot(full_out, rows, 0, 1).astype(BF16))
-    grad_out_all = split.to_heads(jnp.concatenate(grad_mix, axis=1)[None])
+        branch_rows += spread(grad_res.astype(BF16))
+    grad_mix = mix_back(branch_rows, full_out, span_len)
+    grad_out_all = split.to_heads(grad_mix)
     out_grad = dot(
-        jnp.concatenate(after(branch_rows, grad_mix), axis=0),
-        mix_all,
-        0,
-        1,
+        jnp.concatenate(after(branch_rows, grad_mix), axis=0), mix_rows, 0, 0
     ).astype(BF16)
 
     mlp_blocks = to_peers([after(hidden, out_grad)], [full_down], micro_count, n_tensor)
@@ -689,18 +809,12 @@
         packed_grad = attend_back(pair_prefix[m], packed[m], attn_out[m], grad_out, attn_lse[m], m)
         grad_raw.append(split.to_spans(packed_grad))
 
-    raw = jnp.concatenate(grad_raw, axis=2)
-    turned = rotate(
-        raw[:2].reshape(2, head_count, 2, half_dim, all_rows).astype(F32), cos_all, sin_all, -1.0
-    ).reshape(2, head_cols, all_rows)
-    grad_qkv = jnp.concatenate([turned.astype(BF16), raw[2:]], axis=0).reshape(
-        3 * head_cols, all_rows
-    )
-    qkv_grad = dot(normed_rows, grad_qkv, 0, 1).astype(BF16)
+    grad_qkv = unturn(grad_raw, cos_all, sin_all)
+    qkv_grad = dot(normed_rows, grad_qkv, 0, 0).astype(BF16)
     own_gate, own_up = settle_half(part_gu, side, 2, qkv_grad)
     (own_down,) = settle_half(part_down, side, 1, qkv_grad)
-    part = dot(after(grad_qkv, qkv_grad), full_qkv, 0, 1)
-    grad_normed = collect(peer_blocks(part, micro_count, n_tensor))
+    part = to_peers([after(grad_qkv, qkv_grad)], [full_qkv], micro_count, n_tensor)
+    grad_normed = collect(part)
     mlp_part = collect(mlp_blocks, token=part)
     near = [mlp_part[2 * m * own_rows : (2 * m + 1) * own_rows] for m in micros]
     far = [mlp_part[(2 * m + 1) * own_rows : (2 * m + 2) * own_rows] for m in micros]

time: 1160 us -> 1190 us (1.026)
  Pallas kernels: 174 us -> 223 us
  waiting for transfers between devices: 596 us -> 638 us
  matrix products: 83.7 us -> 53 us
  local copies, waits for them, and re-layouts: 113 us -> 83.6 us
    ppermute x56, waiting for transfers between devices: 466 us -> 513 us  [swap(): return lax.ppermute(value, axis, [(a, a ^ distance) for a in range(count)])]
    pallas_call x0 -> x4, Pallas kernels: none -> 37.4 us  [the longest x1 13.7 us: project(): pl.pallas_call(functools.partial(project_kernel, labels), grid=(blocks,),...]
    dot_general x10 -> x4, matrix products: 83.7 us -> 53 us  [dot(): lax.dot_general(left, right, (((left_dim,), (right_dim,)), ((), ())), pre...]
    reshape x7 -> x0, local copies, waits for them, and re-layouts: 22.9 us -> none  [the longest x3 9.78 us: to_spans(): stack.reshape(self.seq_groups, self.head_groups, -1, self.heads_per, self...]
    all_to_all x6, waiting for transfers between devices: 128 us -> 113 us  [the longest x3 79.7 us: to_heads(): lax.all_to_all(packed, 'fsdp', split_axis=0, concat_axis=0, tiled=True)]
    pallas_call x3 -> x4, Pallas kernels: 41.7 us -> 53.9 us  [to_peers(): pl.pallas_call(functools.partial(to_peers_kernel, terms, micros), grid=(w...]
    all_gather x2, waiting for transfers between devices: 0.01 us -> 12 us  [gather(): return lax.all_gather(shard, 'fsdp', axis=0, tiled=True)]
    unnamed x146 -> x184, local copies, waits for them, and re-layouts: 52.2 us -> 62.5 us
  transfers between devices with their start and end apart: 71 -> 71, of which waited for: 41 -> 46; matrix products, arithmetic and copies ran while one was open for 20% -> 15% of each run, Pallas kernels for 15% -> 15%
where the time goes in v2:
time: 1190 us; the launch traced here: 1170 us
  waiting for transfers between devices  638 us (54%)
  Pallas kernels  223 us (19%)
  starting transfers between devices  92.5 us (8%)
  local copies, waits for them, and re-layouts  83.6 us (7%)
  other arithmetic  53.7 us (5%)
  matrix products  53 us (4%)
  between operations  15.5 us (1%)
  blocking collectives  13.5 us (1%)
    ppermute x56, waiting for transfers between devices, swap(): return lax.ppermute(value, axis, [(a, a ^ distance) for a in range(count)])  513 us
    all_to_all x3, waiting for transfers between devices, to_heads(): lax.all_to_all(packed, 'fsdp', split_axis=0, concat_axis=0, tiled=True)  79.7 us
    ppermute x56, starting transfers between devices, swap(): return lax.ppermute(value, axis, [(a, a ^ distance) for a in range(count)])  67.7 us
    unnamed x184, local copies, waits for them, and re-layouts  62.5 us
    pallas_call x4, Pallas kernels, to_peers(): pl.pallas_call(functools.partial(to_peers_kernel, terms, micros), grid=(w...  53.9 us
    dot_general x4, matrix products, dot(): lax.dot_general(left, right, (((left_dim,), (right_dim,)), ((), ())), pre...  53 us
    pallas_call x2, Pallas kernels, attend_back(): pl.pallas_call(backward_kernel, out_shape=jax.ShapeDtypeStruct(grad_shape...  41.4 us
    pallas_call x2, Pallas kernels, attend_forward(): pl.pallas_call(forward_kernel, out_shape=(jax.ShapeDtypeStruct(out_shape,...  39.4 us
  transfers between devices with their start and end apart: 71, of which 46 were waited for; matrix products, arithmetic and copies ran while one was open for 15% of the time, Pallas kernels for 15%

profile of v2, /device:TPU:0, one launch (start us, length us, event | category | flops | bytes accessed | tf_op | source)
XLA Modules:
  0.0 1173.6 jit_solution(2472079869970665385)
XLA Ops:
  27.9 21.7 %collective-permute-done.1.refs_2_ = bf16[256,2048]{1,0:T(8,128)(2,1)S(1)} collective-permute-done((bf16[256,2048]{1,0:T(8,128)(2,1)S(1)}, bf16[256,2048]{1,0:T(8,128)(2,1)S(1)}, u32[]{:S(2)}, u32[]{:S(2)}) %collective-permute-start.1) | collective-permute-done | bytes 1048608 | tf_op jit(solution)/shard_map/ppermute | solution.py:45
  95.8 53.8 %all-to-all-done.1.x_ref = bf16[8,4,192,128]{3,2,1,0:T(8,128)(2,1)S(1)} async-done(((bf16[8,4,192,128]{3,2,1,0:T(8,128)(2,1)}), bf16[8,4,192,128]{3,2,1,0:T(8,128)(2,1)S(1)}, u32[]{:S(2)}, u32[]{:S(2)}) %all-to-all-start.1) | async-done | bytes 1572896 | tf_op jit(solution)/shard_map/all_to_all | solution.py:619
  159.7 19.3 %attend_forward.2 = (bf16[8,4,64,128]{3,2,1,0:T(8,128)(2,1)}, f32[4,1,1024]{2,1,0:T(1,128)}) custom-call(s32[4]{0:T(128)} %get-tuple-element.221.prefix_ref, bf16[8,4,192,128]{3,2,1,0:T(8,128)(2,1)} %copy-done.6), custom_call_target="tpu_custom_call" | custom-call | tf_op jit(solution)/shard_map/attend_forward/pallas_call | solution.py:305
  193.2 20.1 %attend_forward.3 = (bf16[8,4,64,128]{3,2,1,0:T(8,128)(2,1)}, f32[4,1,1024]{2,1,0:T(1,128)}) custom-call(s32[4]{0:T(128)} %get-tuple-element.220.prefix_ref, bf16[8,4,192,128]{3,2,1,0:T(8,128)(2,1)} %copy-done.5), custom_call_target="tpu_custom_call" | custom-call | tf_op jit(solution)/shard_map/attend_forward/pallas_call | solution.py:305
  223.4 49.5 %collective-permute-done.15 = bf16[256,3072]{1,0:T(8,128)(2,1)} collective-permute-done((bf16[256,3072]{1,0:T(8,128)(2,1)}, bf16[256,3072]{1,0:T(8,128)(2,1)}, u32[]{:S(2)}, u32[]{:S(2)}) %collective-permute-start.15) | collective-permute-done | bytes 1572896 | tf_op jit(solution)/shard_map/ppermute | solution.py:45
  300.1 15.0 %collective-permute-done.5 = bf16[128,2048]{1,0:T(8,128)(2,1)S(1)} collective-permute-done((bf16[128,2048]{1,0:T(8,128)(2,1)}, bf16[128,2048]{1,0:T(8,128)(2,1)S(1)}, u32[]{:S(2)}, u32[]{:S(2)}) %collective-permute-start.5) | collective-permute-done | bytes 524320 | tf_op jit(solution)/shard_map/ppermute | solution.py:45
  320.0 15.9 %collective-permute-done.8 = bf16[128,2048]{1,0:T(8,128)(2,1)S(1)} collective-permute-done((bf16[128,2048]{1,0:T(8,128)(2,1)}, bf16[128,2048]{1,0:T(8,128)(2,1)S(1)}, u32[]{:S(2)}, u32[]{:S(2)}) %collective-permute-start.8) | collective-permute-done | bytes 524320 | tf_op jit(solution)/shard_map/ppermute | solution.py:45
  378.1 42.9 %collective-permute-done.21 = bf16[256,2048]{1,0:T(8,128)(2,1)S(1)} collective-permute-done((bf16[256,2048]{1,0:T(8,128)(2,1)S(1)}, bf16[256,2048]{1,0:T(8,128)(2,1)S(1)}, u32[]{:S(2)}, u32[]{:S(2)}) %collective-permute-start.21) | collective-permute-done | bytes 1048608 | tf_op jit(solution)/shard_map/ppermute | solution.py:45
  433.7 97.3 %collective-permute-done.12 = bf16[256,2048]{1,0:T(8,128)(2,1)S(1)} collective-permute-done((bf16[256,2048]{1,0:T(8,128)(2,1)}, bf16[256,2048]{1,0:T(8,128)(2,1)S(1)}, u32[]{:S(2)}, u32[]{:S(2)}) %collective-permute-start.12) | collective-permute-done | bytes 1048608 | tf_op jit(solution)/shard_map/ppermute | solution.py:45
  550.0 17.3 %collective-permute-done.13 = bf16[128,2048]{1,0:T(8,128)(2,1)S(1)} collective-permute-done((bf16[128,2048]{1,0:T(8,128)(2,1)S(1)}, bf16[128,2048]{1,0:T(8,128)(2,1)S(1)}, u32[]{:S(2)}, u32[]{:S(2)}) %collective-permute-start.13) | collective-permute-done | bytes 524320 | tf_op jit(solution)/shard_map/ppermute | solution.py:45
  584.2 13.9 %ffn_forward.3 = (f32[1024,1024]{1,0:T(8,128)}, f32[1024,1024]{1,0:T(8,128)}, bf16[1024,1024]{1,0:T(8,128)(2,1)}) custom-call(bf16[1024,2048]{1,0:T(8,128)(2,1)} %constant_dynamic-update-slice_fusion.26.x_ref, bf16[2048,1024]{1,0:T(8,128)(2,1)} %all-gather.10.cloned.1.call-done.wg_ref.refs_2_, bf16[2048,1024]{1,0:T(8,128)(2,1)} %all-gather.12.cloned.1.call-done.wu_ref.refs_3_), custom_call_target="tpu_custom_call" | custom-call | tf_op jit(solution)/shard_map/ffn_forward/pallas_call | solution.py:380
  598.1 13.9 %ffn_forward.2 = (f32[1024,1024]{1,0:T(8,128)}, f32[1024,1024]{1,0:T(8,128)}, bf16[1024,1024]{1,0:T(8,128)(2,1)}) custom-call(bf16[1024,2048]{1,0:T(8,128)(2,1)} %constant_dynamic-update-slice_fusion.7.x_ref, bf16[2048,1024]{1,0:T(8,128)(2,1)} %all-gather.10.cloned.1.call-done.wg_ref.refs_2_, bf16[2048,1024]{1,0:T(8,128)(2,1)} %all-gather.12.cloned.1.call-done.wu_ref.refs_3_), custom_call_target="tpu_custom_call" | custom-call | tf_op jit(solution)/shard_map/ffn_forward/pallas_call | solution.py:380
  680.9 24.9 %fusion.11 = bf16[2048,2048]{1,0:T(8,128)(2,1)} fusion(bf16[1024,1024]{1,0:T(8,128)(2,1)} %get-tuple-element.135.refs_1_, bf16[1024,1024]{1,0:T(8,128)(2,1)} %get-tuple-element.134.refs_0_, bf16[1024,1024]{1,0:T(8,128)(2,1)} %get-tuple-element.127.refs_1_, bf16[1024,1024]{1,0:T(8,128)(2,1)} %get-tuple-element.126.refs_0_, ...), kind=kOutput, calls=%fused_computation.13 | convolution fusion | flops 17234395136 | bytes 25165824 | tf_op jit(solution)/shard_map/dot_general | solution.py:24
  710.7 21.6 %collective-permute-done.32 = bf16[256,2048]{1,0:T(8,128)(2,1)S(1)} collective-permute-done((bf16[256,2048]{1,0:T(8,128)(2,1)}, bf16[256,2048]{1,0:T(8,128)(2,1)S(1)}, u32[]{:S(2)}, u32[]{:S(2)}) %collective-permute-start.32) | collective-permute-done | bytes 1048608 | tf_op jit(solution)/shard_map/ppermute | solution.py:45
  732.8 21.5 %collective-permute-done.33 = bf16[256,2048]{1,0:T(8,128)(2,1)S(1)} collective-permute-done((bf16[256,2048]{1,0:T(8,128)(2,1)}, bf16[256,2048]{1,0:T(8,128)(2,1)S(1)}, u32[]{:S(2)}, u32[]{:S(2)}) %collective-permute-start.33) | collective-permute-done | bytes 1048608 | tf_op jit(solution)/shard_map/ppermute | solution.py:45
  760.5 16.7 %collective-permute-done.25 = bf16[256,2048]{1,0:T(8,128)(2,1)S(1)} collective-permute-done((bf16[256,2048]{1,0:T(8,128)(2,1)}, bf16[256,2048]{1,0:T(8,128)(2,1)S(1)}, u32[]{:S(2)}, u32[]{:S(2)}) %collective-permute-start.25) | collective-permute-done | bytes 1048608 | tf_op jit(solution)/shard_map/ppermute | solution.py:45
  777.7 19.1 %collective-permute-done.27 = bf16[256,2048]{1,0:T(8,128)(2,1)S(1)} collective-permute-done((bf16[256,2048]{1,0:T(8,128)(2,1)S(1)}, bf16[256,2048]{1,0:T(8,128)(2,1)S(1)}, u32[]{:S(2)}, u32[]{:S(2)}) %collective-permute-start.27) | collective-permute-done | bytes 1048608 | tf_op jit(solution)/shard_map/ppermute | solution.py:45
  800.3 28.2 %collective-permute-done.28 = bf16[128,2048]{1,0:T(8,128)(2,1)S(1)} collective-permute-done((bf16[128,2048]{1,0:T(8,128)(2,1)S(1)}, bf16[128,2048]{1,0:T(8,128)(2,1)S(1)}, u32[]{:S(2)}, u32[]{:S(2)}) %collective-permute-start.28) | collective-permute-done | bytes 524320 | tf_op jit(solution)/shard_map/ppermute | solution.py:45
  896.6 14.0 %to_peers.6 = (f32[512,2048]{1,0:T(8,128)}, bf16[512,2048]{1,0:T(8,128)(2,1)}, bf16[512,2048]{1,0:T(8,128)(2,1)}, bf16[512,2048]{1,0:T(8,128)(2,1)}) custom-call(bf16[2048,1024]{1,0:T(8,128)(2,1)} %copy-done.9, bf16[2048,1024]{1,0:T(8,128)(2,1)} %all-gather.14.cloned.1.call-done.wd_ref.refs_1_), custom_call_target="tpu_custom_call" | custom-call | tf_op jit(solution)/shard_map/to_peers/pallas_call | solution.py:443
  923.4 20.4 %attend_back.3 = bf16[8,4,192,128]{3,2,1,0:T(8,128)(2,1)} custom-call(s32[4]{0:T(128)} %get-tuple-element.221.prefix_ref, bf16[8,4,192,128]{3,2,1,0:T(8,128)(2,1)} %copy-done.6, bf16[8,4,64,128]{3,2,1,0:T(8,128)(2,1)} %get-tuple-element.100.o_ref, bf16[8,8,64,128]{3,2,1,0:T(8,128)(2,1)} %all-to-all-done.3.do_ref, f32[4,1,1024]{2,1,0:T(1,128)} %get-tuple-element.97.lse_ref), custom_call_target="tpu_custom_call" | custom-call | tf_op jit(solution)/shard_map/attend_back/pallas_call | solution.py:330
  951.8 21.0 %attend_back.2 = bf16[8,4,192,128]{3,2,1,0:T(8,128)(2,1)} custom-call(s32[4]{0:T(128)} %get-tuple-element.220.prefix_ref, bf16[8,4,192,128]{3,2,1,0:T(8,128)(2,1)} %copy-done.5, bf16[8,4,64,128]{3,2,1,0:T(8,128)(2,1)} %get-tuple-element.99.o_ref, bf16[8,8,64,128]{3,2,1,0:T(8,128)(2,1)} %all-to-all-done.3.do_ref, f32[4,1,1024]{2,1,0:T(1,128)} %get-tuple-element.110.lse_ref), custom_call_target="tpu_custom_call" | custom-call | tf_op jit(solution)/shard_map/attend_back/pallas_call | solution.py:330
  1008.3 20.0 %all-to-all-done.4.refs_0_ = bf16[8,4,192,128]{3,2,1,0:T(8,128)(2,1)} async-done(((bf16[8,4,192,128]{3,2,1,0:T(8,128)(2,1)}), bf16[8,4,192,128]{3,2,1,0:T(8,128)(2,1)}, u32[]{:S(2)}, u32[]{:S(2)}) %all-to-all-start.4) | async-done | bytes 1572896 | tf_op jit(solution)/shard_map/all_to_all | solution.py:623
  1052.6 21.9 %collective-permute-done.52 = bf16[256,1024]{1,0:T(8,128)(2,1)} collective-permute-done((bf16[256,1024]{1,0:T(8,128)(2,1)}, bf16[256,1024]{1,0:T(8,128)(2,1)}, u32[]{:S(2)}, u32[]{:S(2)}) %collective-permute-start.52) | collective-permute-done | bytes 524320 | tf_op jit(solution)/shard_map/ppermute | solution.py:45
  1118.0 21.7 %collective-permute-done.44 = bf16[256,2048]{1,0:T(8,128)(2,1)S(1)} collective-permute-done((bf16[256,2048]{1,0:T(8,128)(2,1)}, bf16[256,2048]{1,0:T(8,128)(2,1)S(1)}, u32[]{:S(2)}, u32[]{:S(2)}) %collective-permute-start.44) | collective-permute-done | bytes 1048608 | tf_op jit(solution)/shard_map/ppermute | solution.py:45
  (437 shorter events, 526.4 us)
Async XLA Ops:
  7.2 70.5 %all-gather.6.cloned.1.call-start = ((), (), s32[]{:S(2)}) async-start(), calls=%async_computation.10 | async-start | bytes 7077888 | tf_op jit(solution)/shard_map/all_gather | solution.py:667
  91.4 58.2 %all-to-all-start.1 = ((bf16[8,4,192,128]{3,2,1,0:T(8,128)(2,1)}), bf16[8,4,192,128]{3,2,1,0:T(8,128)(2,1)S(1)}, u32[]{:S(2)}, u32[]{:S(2)}) async-start(bf16[8,4,192,128]{3,2,1,0:T(8,128)(2,1)} %get-tuple-element.95), calls=%async_computation.1 | async-start | bytes 3145728 | tf_op jit(solution)/shard_map/all_to_all | solution.py:619
  95.0 64.7 %all-gather.8.cloned.1.call-start = ((), (), s32[]{:S(2)}) async-start(), calls=%async_computation.11 | async-start | bytes 2359296 | tf_op jit(solution)/shard_map/all_gather | solution.py:667
  215.6 57.3 %all-to-all-start.2 = ((bf16[8,8,64,128]{3,2,1,0:T(8,128)(2,1)}), bf16[8,8,64,128]{3,2,1,0:T(8,128)(2,1)S(1)}, u32[]{:S(2)}, u32[]{:S(2)}) async-start(bf16[8,8,64,128]{3,2,1,0:T(8,128)(2,1)} %pad_maximum_fusion.3), calls=%async_computation.2 | async-start | bytes 2097152 | tf_op jit(solution)/shard_map/all_to_all | solution.py:623
  219.2 365.0 %all-gather.10.cloned.1.call-start = ((), (), s32[]{:S(2)}) async-start(), calls=%async_computation.12 | async-start | bytes 5242880 | tf_op jit(solution)/shard_map/all_gather | solution.py:140
  288.7 295.4 %all-gather.12.cloned.1.call-start = ((), (), s32[]{:S(2)}) async-start(), calls=%async_computation.13 | async-start | bytes 5242880 | tf_op jit(solution)/shard_map/all_gather | solution.py:140
  370.1 259.8 %all-gather.14.cloned.1.call-start = ((), (), s32[]{:S(2)}) async-start(), calls=%async_computation.14 | async-start | bytes 5242880 | tf_op jit(solution)/shard_map/all_gather | solution.py:140
  422.6 110.3 %collective-permute-start.24 = (bf16[512,2048]{1,0:T(8,128)(2,1)}, bf16[512,2048]{1,0:T(8,128)(2,1)}, u32[]{:S(2)}, u32[]{:S(2)}) collective-permute-start(bf16[512,2048]{1,0:T(8,128)(2,1)} %pad_maximum_fusion.1), channel_id=1, source_target_pairs={{0,3},{1,2},{2,1},{3,0},{4,7},{5,6},{6,5},{7,4},{8,11},{9,10},{10,... | collective-permute-start | bytes 6291464 | tf_op jit(solution)/shard_map/ppermute | solution.py:45
  423.8 110.9 %collective-permute-start.23 = (bf16[512,2048]{1,0:T(8,128)(2,1)}, bf16[512,2048]{1,0:T(8,128)(2,1)}, u32[]{:S(2)}, u32[]{:S(2)}) collective-permute-start(bf16[512,2048]{1,0:T(8,128)(2,1)} %pad_maximum_fusion.1), channel_id=1, source_target_pairs={{0,2},{1,3},{2,0},{3,1},{4,6},{5,7},{6,4},{7,5},{8,10},{9,11},{10,... | collective-permute-start | bytes 6291464 | tf_op jit(solution)/shard_map/ppermute | solution.py:45
  424.3 110.4 %collective-permute-start.22 = (bf16[512,2048]{1,0:T(8,128)(2,1)}, bf16[512,2048]{1,0:T(8,128)(2,1)}, u32[]{:S(2)}, u32[]{:S(2)}) collective-permute-start(bf16[512,2048]{1,0:T(8,128)(2,1)} %pad_maximum_fusion.1), channel_id=1, source_target_pairs={{0,1},{1,0},{2,3},{3,2},{4,5},{5,4},{6,7},{7,6},{8,9},{9,8},{10,11... | collective-permute-start | bytes 6291464 | tf_op jit(solution)/shard_map/ppermute | solution.py:45
  427.1 278.7 %reduce-scatter.5.cloned.1.call-start = ((), (), s32[]{:S(2)}) async-start(), calls=%async_computation.15 | async-start | bytes 5242880 | tf_op jit(solution)/shard_map/reduce_scatter | solution.py:150
  428.5 102.5 %collective-permute-start.12 = (bf16[256,2048]{1,0:T(8,128)(2,1)}, bf16[256,2048]{1,0:T(8,128)(2,1)S(1)}, u32[]{:S(2)}, u32[]{:S(2)}) collective-permute-start(bf16[256,2048]{1,0:T(8,128)(2,1)} %pad_maximum_fusion.4), channel_id=1, source_target_pairs={{0,2},{1,3},{2,0},{3,1},{4,6},{5,7},{6,4},{7,5},{8,10},{9,11},{10,... | collective-permute-start | bytes 3145736 | tf_op jit(solution)/shard_map/ppermute | solution.py:45
  430.0 101.3 %collective-permute-start.11 = (bf16[256,2048]{1,0:T(8,128)(2,1)}, bf16[256,2048]{1,0:T(8,128)(2,1)S(1)}, u32[]{:S(2)}, u32[]{:S(2)}) collective-permute-start(bf16[256,2048]{1,0:T(8,128)(2,1)} %pad_maximum_fusion.4), channel_id=1, source_target_pairs={{0,1},{1,0},{2,3},{3,2},{4,5},{5,4},{6,7},{7,6},{8,9},{9,8},{10,11... | collective-permute-start | bytes 3145736 | tf_op jit(solution)/shard_map/ppermute | solution.py:45
  629.4 267.2 %reduce-scatter.7.cloned.1.call-start = ((), (), s32[]{:S(2)}) async-start(), calls=%async_computation.16 | async-start | bytes 10485760 | tf_op jit(solution)/shard_map/reduce_scatter | solution.py:150
  709.5 67.7 %collective-permute-start.25 = (bf16[256,2048]{1,0:T(8,128)(2,1)}, bf16[256,2048]{1,0:T(8,128)(2,1)S(1)}, u32[]{:S(2)}, u32[]{:S(2)}) collective-permute-start(bf16[256,2048]{1,0:T(8,128)(2,1)} %get-tuple-element.129), channel_id=1, source_target_pairs={{0,1},{1,0},{2,3},{3,2},{4,5},{5,4},{6,7},{7,6},{8,9},{9,8},{10,11... | collective-permute-start | bytes 3145736 | tf_op jit(solution)/shard_map/ppermute | solution.py:45
  709.5 68.2 %collective-permute-start.26 = (bf16[256,2048]{1,0:T(8,128)(2,1)}, bf16[256,2048]{1,0:T(8,128)(2,1)S(1)}, u32[]{:S(2)}, u32[]{:S(2)}) collective-permute-start(bf16[256,2048]{1,0:T(8,128)(2,1)} %get-tuple-element.130), channel_id=1, source_target_pairs={{0,2},{1,3},{2,0},{3,1},{4,6},{5,7},{6,4},{7,5},{8,10},{9,11},{10,... | collective-permute-start | bytes 3145736 | tf_op jit(solution)/shard_map/ppermute | solution.py:45
  732.2 64.6 %collective-permute-start.27 = (bf16[256,2048]{1,0:T(8,128)(2,1)S(1)}, bf16[256,2048]{1,0:T(8,128)(2,1)S(1)}, u32[]{:S(2)}, u32[]{:S(2)}) collective-permute-start(bf16[256,2048]{1,0:T(8,128)(2,1)S(1)} %copy-done.48), channel_id=1, source_target_pairs={{0,3},{1,2},{2,1},{3,0},{4,7},{5,6},{6,5},{7,4},{8,11},{9,10},{10,... | collective-permute-start | bytes 3145736 | tf_op jit(solution)/shard_map/ppermute | solution.py:45
  888.7 61.3 %reduce-scatter.9.cloned.1.call-start = ((), (), s32[]{:S(2)}) async-start(), calls=%async_computation.17 | async-start | bytes 2359296 | tf_op jit(solution)/shard_map/reduce_scatter | solution.py:670
  990.4 173.9 %reduce-scatter.11.cloned.1.call-start = ((), (), s32[]{:S(2)}) async-start(), calls=%async_computation.18 | async-start | bytes 7077888 | tf_op jit(solution)/shard_map/reduce_scatter | solution.py:670
  1001.8 86.7 %collective-permute-start.39 = (bf16[512,2048]{1,0:T(8,128)(2,1)}, bf16[512,2048]{1,0:T(8,128)(2,1)}, u32[]{:S(2)}, u32[]{:S(2)}) collective-permute-start(bf16[512,2048]{1,0:T(8,128)(2,1)} %get-tuple-element.154), channel_id=1, source_target_pairs={{0,1},{1,0},{2,3},{3,2},{4,5},{5,4},{6,7},{7,6},{8,9},{9,8},{10,11... | collective-permute-start | bytes 6291464 | tf_op jit(solution)/shard_map/ppermute | solution.py:45
  1002.9 92.2 %collective-permute-start.40 = (bf16[512,2048]{1,0:T(8,128)(2,1)}, bf16[512,2048]{1,0:T(8,128)(2,1)}, u32[]{:S(2)}, u32[]{:S(2)}) collective-permute-start(bf16[512,2048]{1,0:T(8,128)(2,1)} %get-tuple-element.155), channel_id=1, source_target_pairs={{0,2},{1,3},{2,0},{3,1},{4,6},{5,7},{6,4},{7,5},{8,10},{9,11},{10,... | collective-permute-start | bytes 6291464 | tf_op jit(solution)/shard_map/ppermute | solution.py:45
  1004.2 92.3 %collective-permute-start.41 = (bf16[512,2048]{1,0:T(8,128)(2,1)}, bf16[512,2048]{1,0:T(8,128)(2,1)}, u32[]{:S(2)}, u32[]{:S(2)}) collective-permute-start(bf16[512,2048]{1,0:T(8,128)(2,1)} %get-tuple-element.156), channel_id=1, source_target_pairs={{0,3},{1,2},{2,1},{3,0},{4,7},{5,6},{6,5},{7,4},{8,11},{9,10},{10,... | collective-permute-start | bytes 6291464 | tf_op jit(solution)/shard_map/ppermute | solution.py:45
  1006.4 68.2 %collective-permute-start.51 = (bf16[256,2048]{1,0:T(8,128)(2,1)}, bf16[256,2048]{1,0:T(8,128)(2,1)}, u32[]{:S(2)}, u32[]{:S(2)}) collective-permute-start(bf16[256,2048]{1,0:T(8,128)(2,1)} %constant_dynamic-slice_fusion.2), channel_id=1, source_target_pairs={{0,8},{4,12},{8,0},{12,4},{16,24},{20,28},{24,16},{28,20},{1,9},{5... | collective-permute-start | bytes 3145736 | tf_op jit(solution)/shard_map/ppermute | solution.py:45
  1087.3 52.3 %collective-permute-start.44 = (bf16[256,2048]{1,0:T(8,128)(2,1)}, bf16[256,2048]{1,0:T(8,128)(2,1)S(1)}, u32[]{:S(2)}, u32[]{:S(2)}) collective-permute-start(bf16[256,2048]{1,0:T(8,128)(2,1)} %get-tuple-element.169), channel_id=1, source_target_pairs={{0,2},{1,3},{2,0},{3,1},{4,6},{5,7},{6,4},{7,5},{8,10},{9,11},{10,... | collective-permute-start | bytes 3145736 | tf_op jit(solution)/shard_map/ppermute | solution.py:45
  (99 other events, 2056.0 us)
Sparse Core Ops, SparseCore 0:
  10.2 67.4 all-gather.5
  97.5 50.8 all-gather.7
  288.9 57.0 all-gather.9
  370.2 57.5 all-gather.11
  429.2 56.8 all-gather.13
  629.5 68.5 reduce-scatter.4
  706.0 118.1 reduce-scatter.6
  896.7 40.3 reduce-scatter.8
  1049.1 92.0 reduce-scatter.10

commit v3 on v2

--- a/solution.py
+++ b/solution.py
@@ -94,6 +94,10 @@
     return parts[0] + one + two
 
 
+def peer_swaps(parts):
+    return [swap(part, "tensor", k) for k, part in enumerate(parts) if k]
+
+
 def pair_join(value, micros):
     other = swap(value, "fsdp", PAIR)
     size = value.shape[0] // micros
@@ -108,10 +112,14 @@
     )
 
 
+def paired_order(count):
+    return [(f & ~3) | ((f & 1) << 1) | ((f >> 1) & 1) for f in range(count)]
+
+
 def paired(values):
     count = lax.axis_size("fsdp")
     size = values.shape[-1] // count
-    order = [(f & ~3) | ((f & 1) << 1) | ((f >> 1) & 1) for f in range(count)]
+    order = paired_order(count)
     parts = [lax.slice_in_dim(values, f * size, (f + 1) * size, axis=-1) for f in order]
     return jnp.concatenate(parts, axis=-1)
 
@@ -451,6 +459,105 @@
         ],
         name="to_peers",
     )(*lefts, *rights)
+
+
+def row_tile(rows):
+    return math.gcd(rows, 64)
+
+
+def row_block(tile, width, first=0):
+    return pl.BlockSpec((tile, width), lambda n: (first + n, 0))
+
+
+def paired_store(ref, values, parts):
+    size = values.shape[1] // parts
+    for i, f in enumerate(paired_order(parts)):
+        ref[:, i * size : (i + 1) * size] = values[:, f * size : (f + 1) * size]
+
+
+def norm_rows_kernel(parts, x_ref, gain_ref, own_ref, *refs):
+    blocks, (branch_ref, res_ref, normed_ref) = refs[:-3], refs[-3:]
+    branch = own_ref[...]
+    for ref in blocks:
+        branch = branch + ref[...].astype(F32)
+    res = x_ref[...].astype(F32) + branch
+    unit, _ = normalize(res)
+    branch_ref[...] = branch
+    res_ref[...] = res
+    paired_store(normed_ref, (unit * gain_ref[...]).astype(BF16), parts)
+
+
+def norm_rows(inputs, micro, gain, own, blocks, parts):
+    rows, width = own.shape
+    tile = row_tile(rows)
+    return pl.pallas_call(
+        functools.partial(norm_rows_kernel, parts),
+        grid=(rows // tile,),
+        in_specs=[row_block(tile, width, micro * (rows // tile)), whole(gain.shape)]
+        + [row_block(tile, width)] * (1 + len(blocks)),
+        out_specs=[row_block(tile, width)] * 3,
+        out_shape=[jax.ShapeDtypeStruct((rows, width), kind) for kind in (F32, F32, BF16)],
+        name="norm_rows",
+    )(inputs, gain, own, *blocks)
+
+
+def peer_sum_kernel(*refs):
+    count = (len(refs) - 2) // 2
+    for pieces, out in ((refs[:count], refs[-2]), (refs[count:-2], refs[-1])):
+        total = pieces[0][...]
+        for ref in pieces[1:]:
+            total = total + ref[...].astype(F32)
+        out[...] = total.astype(out.dtype)
+
+
+def peer_sum(own, blocks):
+    rows, width = own.shape[0] // 2, own.shape[1]
+    tile = row_tile(rows)
+    pieces = [own] + list(blocks)
+    return pl.pallas_call(
+        peer_sum_kernel,
+        grid=(rows // tile,),
+        in_specs=[
+            row_block(tile, width, half * (rows // tile)) for half in range(2) for _ in pieces
+        ],
+        out_specs=[row_block(tile, width)] * 2,
+        out_shape=[jax.ShapeDtypeStruct((rows, width), kind) for kind in (F32, BF16)],
+        name="peer_sum",
+    )(*pieces, *pieces)
+
+
+def norm_grad_kernel(parts, dy_ref, gain_ref, near_ref, far_ref, res_ref, grad_ref, low_ref, sum_ref, dn_ref):
+    paired_store(dn_ref, near_ref[...] + far_ref[...].astype(F32), parts)
+    unit, scale = normalize(res_ref[...])
+    part, gain_part = norm_back(dn_ref[...], unit, scale, gain_ref[...])
+    grad = dy_ref[...].astype(F32) + part
+    grad_ref[...] = grad
+    low_ref[...] = grad.astype(BF16)
+
+    @pl.when(pl.program_id(0) == 0)
+    def _():
+        sum_ref[...] = jnp.zeros_like(sum_ref)
+
+    sum_ref[...] += gain_part[None]
+
+
+def norm_grad(grads, micro, gain, near, far, res, parts):
+    rows, width = near.shape
+    tile = row_tile(rows)
+    return pl.pallas_call(
+        functools.partial(norm_grad_kernel, parts),
+        grid=(rows // tile,),
+        in_specs=[row_block(tile, width, micro * (rows // tile)), whole(gain.shape)]
+        + [row_block(tile, width)] * 3,
+        out_specs=[row_block(tile, width)] * 2 + [pl.BlockSpec((1, width), lambda n: (0, 0))],
+        out_shape=[
+            jax.ShapeDtypeStruct((rows, width), F32),
+            jax.ShapeDtypeStruct((rows, width), BF16),
+            jax.ShapeDtypeStruct((1, width), F32),
+        ],
+        scratch_shapes=[pltpu.VMEM((tile, width), F32)],
+        name="norm_grad",
+    )(grads, gain, near, far, res)
 
 
 def turn(values, cos_tab, sin_tab):
@@ -740,18 +847,23 @@
         for i in range(3)
     ]
     full_gate = gather_half(after(shards[0], mix_packed))
-    branch, resid, unit_mlp, scale_mlp, joined = [], [], [], [], []
+    branch, resid, others, normed_mlp, joined = [], [], [], [], []
+    flat_inputs = inputs.reshape(micro_count * own_rows, model_width)
+    gain_rows = gain_mlp[None]
     mix_rows, *parts = mix_out(mix_packed, full_out, micro_count, n_tensor)
     for m in micros:
-        part = collect(parts[m * n_tensor : (m + 1) * n_tensor])
-        res = x_float[m * own_rows : (m + 1) * own_rows] + part
-        unit, scale = normalize(res)
+        own, *sent = parts[m * n_tensor : (m + 1) * n_tensor]
+        blocks = peer_swaps([own] + sent)
+        if m:
+            blocks = after(blocks, normed_mlp)
+        part, res, normed = norm_rows(flat_inputs, m, gain_rows, own, blocks, n_fsdp)
         branch.append(part)
         resid.append(res)
-        unit_mlp.append(unit)
-        scale_mlp.append(scale)
-        normed = paired((unit * gain_mlp).astype(BF16))
-        joined.append(pair_join(normed, 1))
+        normed_mlp.append(normed)
+        others.append(swap(normed, "fsdp", PAIR))
+    for m in micros:
+        other = after(others[m], joined) if m else others[m]
+        joined.append(jnp.concatenate([normed_mlp[m], other], axis=0))
     full_up = gather_half(after(shards[1], joined))
     full_down = gather_half(shards[2])
     mlp_rows, first = [], None
@@ -774,26 +886,29 @@
     part_down = scatter_half(down_grad)
     grad_gu, normed_part = [], []
     for m in micros:
-        gate, up = ffn_back(grad_rows, m, full_down, gate_val[m], up_val[m])
+        gate_in = after(gate_val[m], normed_part) if m else gate_val[m]
+        gate, up = ffn_back(grad_rows, m, full_down, gate_in, up_val[m])
         grad_gu.append(jnp.concatenate([gate, up], axis=1))
         normed_part.append(to_peers([gate, up], [full_gate, full_up], 1, n_tensor))
     all_mlp_rows = jnp.concatenate(after(mlp_rows, normed_part), axis=0)
     gu_grad = dot(all_mlp_rows, jnp.concatenate(grad_gu, axis=0), 0, 0).astype(BF16)
     part_gu = scatter_half(after(gu_grad, part_down))
-    grad_resid, branch_rows = [], []
-    mlp_gain_sum = jnp.zeros((model_width,), F32)
+    grad_resid, branch_rows, near_far, mlp_gain_parts = [], [], [], []
     for m in micros:
-        total = collect(normed_part[m])
-        grad_normed = total[:own_rows] + swap(
-            total[own_rows:].astype(BF16), "fsdp", PAIR
-        ).astype(F32)
-        part, gain_part = norm_back(paired(grad_normed), unit_mlp[m], scale_mlp[m], gain_mlp)
-        mlp_gain_sum = mlp_gain_sum + gain_part
-        grad_res = grad_own[m * own_rows : (m + 1) * own_rows].astype(F32) + part
+        blocks = peer_swaps(normed_part[m])
+        blocks = after(blocks, near_far[-1][0] if m else gu_grad)
+        near, far = peer_sum(normed_part[m][0], blocks)
+        near_far.append((near, swap(far, "fsdp", PAIR)))
+    low = None
+    for m in micros:
+        near, far = near_far[m]
+        if m:
+            far = after(far, low)
+        grad_res, low, gain_part = norm_grad(grad_own, m, gain_rows, near, far, resid[m], n_fsdp)
+        mlp_gain_parts.append(gain_part[0])
         grad_resid.append(grad_res)
-        if m == 0:
-            grad_res = after(grad_res, gu_grad)
-        branch_rows += spread(grad_res.astype(BF16))
+        branch_rows += spread(low)
+    mlp_gain_sum = sum(mlp_gain_parts)
     grad_mix = mix_back(branch_rows, full_out, span_len)
     grad_out_all = split.to_heads(grad_mix)
     out_grad = dot(
@@ -801,24 +916,27 @@
     ).astype(BF16)
 
     mlp_blocks = to_peers([after(hidden, out_grad)], [full_down], micro_count, n_tensor)
-    own_out = scatter(after(out_grad, part_gu))
+    own_out = scatter(after(out_grad, part_gu, mlp_blocks))
 
     grad_raw = []
+    packed_grads = []
     for m in micros:
         grad_out = after(grad_out_all, mlp_blocks, part_down if m else own_out)
         packed_grad = attend_back(pair_prefix[m], packed[m], attn_out[m], grad_out, attn_lse[m], m)
+        packed_grads.append(packed_grad)
         grad_raw.append(split.to_spans(packed_grad))
 
+    mlp_part = collect(mlp_blocks, token=packed_grads[0])
+    near = [mlp_part[2 * m * own_rows : (2 * m + 1) * own_rows] for m in micros]
+    far = [mlp_part[(2 * m + 1) * own_rows : (2 * m + 2) * own_rows] for m in micros]
+    far = swap(jnp.concatenate(far, axis=0).astype(BF16), "fsdp", PAIR)
     grad_qkv = unturn(grad_raw, cos_all, sin_all)
     qkv_grad = dot(normed_rows, grad_qkv, 0, 0).astype(BF16)
     own_gate, own_up = settle_half(part_gu, side, 2, qkv_grad)
     (own_down,) = settle_half(part_down, side, 1, qkv_grad)
     part = to_peers([after(grad_qkv, qkv_grad)], [full_qkv], micro_count, n_tensor)
     grad_normed = collect(part)
-    mlp_part = collect(mlp_blocks, token=part)
-    near = [mlp_part[2 * m * own_rows : (2 * m + 1) * own_rows] for m in micros]
-    far = [mlp_part[(2 * m + 1) * own_rows : (2 * m + 2) * own_rows] for m in micros]
-    far = swap(jnp.concatenate(far, axis=0).astype(BF16), "fsdp", PAIR).astype(F32)
+    far = after(far, part).astype(F32)
     mlp_out = paired(jnp.concatenate(near, axis=0) + far)
     branch = jnp.concatenate(branch, axis=0)
     result = jnp.concatenate(resid, axis=0) + mlp_out

time: 1190 us -> 1230 us (1.034)
  waiting for transfers between devices: 638 us -> 699 us
  Pallas kernels: 223 us -> 244 us
  local copies, waits for them, and re-layouts: 83.6 us -> 65.9 us
  other arithmetic: 53.7 us -> 38.1 us
    ppermute x56, waiting for transfers between devices: 513 us -> 551 us  [swap(): return lax.ppermute(value, axis, [(a, a ^ distance) for a in range(count)])]
    all_to_all x3, waiting for transfers between devices: 33.1 us -> 57.8 us  [to_spans(): lax.all_to_all(packed, 'fsdp', split_axis=0, concat_axis=0, tiled=True)]
    pallas_call x0 -> x6, Pallas kernels: none -> 19.9 us  [the longest x2 6.99 us: peer_sum(): pl.pallas_call(peer_sum_kernel, grid=(rows // tile,), in_specs=[row_block...]
    unnamed x184 -> x182, local copies, waits for them, and re-layouts: 62.5 us -> 48.6 us
  transfers between devices with their start and end apart: 71 -> 71, of which waited for: 46 -> 42; matrix products, arithmetic and copies ran while one was open for 15% -> 12% of each run, Pallas kernels for 15% -> 19%
where the time goes in v3:
time: 1230 us; the launch traced here: 1220 us
  waiting for transfers between devices  699 us (57%)
  Pallas kernels  244 us (20%)
  starting transfers between devices  83 us (7%)
  local copies, waits for them, and re-layouts  65.9 us (5%)
  matrix products  62.7 us (5%)
  other arithmetic  38.1 us (3%)
  between operations  15.6 us (1%)
  blocking collectives  13.5 us (1%)
    ppermute x56, waiting for transfers between devices, swap(): return lax.ppermute(value, axis, [(a, a ^ distance) for a in range(count)])  551 us
    all_to_all x3, waiting for transfers between devices, to_heads(): lax.all_to_all(packed, 'fsdp', split_axis=0, concat_axis=0, tiled=True)  72.3 us
    dot_general x4, matrix products, dot(): lax.dot_general(left, right, (((left_dim,), (right_dim,)), ((), ())), pre...  62.7 us
    ppermute x56, starting transfers between devices, swap(): return lax.ppermute(value, axis, [(a, a ^ distance) for a in range(count)])  59.3 us
    all_to_all x3, waiting for transfers between devices, to_spans(): lax.all_to_all(packed, 'fsdp', split_axis=0, concat_axis=0, tiled=True)  57.8 us
    pallas_call x4, Pallas kernels, to_peers(): pl.pallas_call(functools.partial(to_peers_kernel, terms, micros), grid=(w...  54.4 us
    unnamed x182, local copies, waits for them, and re-layouts  48.6 us
    pallas_call x2, Pallas kernels, attend_back(): pl.pallas_call(backward_kernel, out_shape=jax.ShapeDtypeStruct(grad_shape...  41.4 us
  transfers between devices with their start and end apart: 71, of which 42 were waited for; matrix products, arithmetic and copies ran while one was open for 12% of the time, Pallas kernels for 19%

profile of v3, /device:TPU:0, one launch (start us, length us, event | category | flops | bytes accessed | tf_op | source)
XLA Modules:
  0.0 1221.6 jit_solution(10100872657595455909)
XLA Ops:
  28.2 21.7 %collective-permute-done.1.refs_2_ = bf16[256,2048]{1,0:T(8,128)(2,1)S(1)} collective-permute-done((bf16[256,2048]{1,0:T(8,128)(2,1)S(1)}, bf16[256,2048]{1,0:T(8,128)(2,1)S(1)}, u32[]{:S(2)}, u32[]{:S(2)}) %collective-permute-start.1) | collective-permute-done | bytes 1048608 | tf_op jit(solution)/shard_map/ppermute | solution.py:45
  95.8 53.8 %all-to-all-done.1.x_ref = bf16[8,4,192,128]{3,2,1,0:T(8,128)(2,1)S(1)} async-done(((bf16[8,4,192,128]{3,2,1,0:T(8,128)(2,1)}), bf16[8,4,192,128]{3,2,1,0:T(8,128)(2,1)S(1)}, u32[]{:S(2)}, u32[]{:S(2)}) %all-to-all-start.1) | async-done | bytes 1572896 | tf_op jit(solution)/shard_map/all_to_all | solution.py:726
  159.1 19.3 %attend_forward.2 = (bf16[8,4,64,128]{3,2,1,0:T(8,128)(2,1)}, f32[4,1,1024]{2,1,0:T(1,128)}) custom-call(s32[4]{0:T(128)} %get-tuple-element.273.prefix_ref, bf16[8,4,192,128]{3,2,1,0:T(8,128)(2,1)} %copy-done.6), custom_call_target="tpu_custom_call" | custom-call | tf_op jit(solution)/shard_map/attend_forward/pallas_call | solution.py:313
  192.2 20.1 %attend_forward.3 = (bf16[8,4,64,128]{3,2,1,0:T(8,128)(2,1)}, f32[4,1,1024]{2,1,0:T(1,128)}) custom-call(s32[4]{0:T(128)} %get-tuple-element.272.prefix_ref, bf16[8,4,192,128]{3,2,1,0:T(8,128)(2,1)} %copy-done.5), custom_call_target="tpu_custom_call" | custom-call | tf_op jit(solution)/shard_map/attend_forward/pallas_call | solution.py:313
  222.9 21.7 %all-to-all-done.2.x_ref = bf16[8,8,64,128]{3,2,1,0:T(8,128)(2,1)S(1)} async-done(((bf16[8,8,64,128]{3,2,1,0:T(8,128)(2,1)}), bf16[8,8,64,128]{3,2,1,0:T(8,128)(2,1)S(1)}, u32[]{:S(2)}, u32[]{:S(2)}) %all-to-all-start.2) | async-done | bytes 1048608 | tf_op jit(solution)/shard_map/all_to_all | solution.py:730
  323.9 39.6 %collective-permute-done.21 = bf16[256,2048]{1,0:T(8,128)(2,1)S(1)} collective-permute-done((bf16[256,2048]{1,0:T(8,128)(2,1)S(1)}, bf16[256,2048]{1,0:T(8,128)(2,1)S(1)}, u32[]{:S(2)}, u32[]{:S(2)}) %collective-permute-start.21) | collective-permute-done | bytes 1048608 | tf_op jit(solution)/shard_map/ppermute | solution.py:45
  371.6 107.2 %collective-permute-done.12 = bf16[256,2048]{1,0:T(8,128)(2,1)S(1)} collective-permute-done((bf16[256,2048]{1,0:T(8,128)(2,1)}, bf16[256,2048]{1,0:T(8,128)(2,1)S(1)}, u32[]{:S(2)}, u32[]{:S(2)}) %collective-permute-start.12) | collective-permute-done | bytes 1048608 | tf_op jit(solution)/shard_map/ppermute | solution.py:45
  499.5 17.2 %collective-permute-done.13 = bf16[128,2048]{1,0:T(8,128)(2,1)S(1)} collective-permute-done((bf16[128,2048]{1,0:T(8,128)(2,1)S(1)}, bf16[128,2048]{1,0:T(8,128)(2,1)S(1)}, u32[]{:S(2)}, u32[]{:S(2)}) %collective-permute-start.13) | collective-permute-done | bytes 524320 | tf_op jit(solution)/shard_map/ppermute | solution.py:45
  532.2 13.9 %ffn_forward.3 = (f32[1024,1024]{1,0:T(8,128)}, f32[1024,1024]{1,0:T(8,128)}, bf16[1024,1024]{1,0:T(8,128)(2,1)}) custom-call(bf16[1024,2048]{1,0:T(8,128)(2,1)} %constant_dynamic-update-slice_fusion.12.x_ref, bf16[2048,1024]{1,0:T(8,128)(2,1)} %all-gather.10.cloned.1.call-done.wg_ref.refs_2_, bf16[2048,1024]{1,0:T(8,128)(2,1)} %all-gather.12.cloned.1.call-done.wu_ref.refs_3_), custom_call_target="tpu_custom_call" | custom-call | tf_op jit(solution)/shard_map/ffn_forward/pallas_call | solution.py:388
  546.1 13.9 %ffn_forward.2 = (f32[1024,1024]{1,0:T(8,128)}, f32[1024,1024]{1,0:T(8,128)}, bf16[1024,1024]{1,0:T(8,128)(2,1)}) custom-call(bf16[1024,2048]{1,0:T(8,128)(2,1)} %constant_dynamic-update-slice_fusion.4.x_ref, bf16[2048,1024]{1,0:T(8,128)(2,1)} %all-gather.10.cloned.1.call-done.wg_ref.refs_2_, bf16[2048,1024]{1,0:T(8,128)(2,1)} %all-gather.12.cloned.1.call-done.wu_ref.refs_3_), custom_call_target="tpu_custom_call" | custom-call | tf_op jit(solution)/shard_map/ffn_forward/pallas_call | solution.py:388
  589.5 14.1 %to_peers.4 = (f32[256,2048]{1,0:T(8,128)}, bf16[256,2048]{1,0:T(8,128)(2,1)}, bf16[256,2048]{1,0:T(8,128)(2,1)}, bf16[256,2048]{1,0:T(8,128)(2,1)}) custom-call(bf16[1024,1024]{1,0:T(8,128)(2,1)} %get-tuple-element.162.refs_0_, bf16[1024,1024]{1,0:T(8,128)(2,1)} %get-tuple-element.163.refs_1_, ...), custom_call_target="tpu_custom_call" | custom-call | tf_op jit(solution)/shard_map/to_peers/pallas_call | solution.py:451
  628.7 34.6 %fusion.11 = bf16[2048,2048]{1,0:T(8,128)(2,1)} fusion(bf16[1024,1024]{1,0:T(8,128)(2,1)} %get-tuple-element.172.refs_1_, bf16[1024,1024]{1,0:T(8,128)(2,1)} %get-tuple-element.171.refs_0_, bf16[1024,1024]{1,0:T(8,128)(2,1)} %get-tuple-element.163.refs_1_, bf16[1024,1024]{1,0:T(8,128)(2,1)S(1)} %copy-done.39, ...), kind=kOutput, calls=%fused_computation.13 | convolution fusion | flops 17234395136 | bytes 25165824 | tf_op jit(solution)/shard_map/dot_general | solution.py:24
  670.0 20.6 %collective-permute-done.25.refs_1_.refs_5_ = bf16[256,2048]{1,0:T(8,128)(2,1)} collective-permute-done((bf16[256,2048]{1,0:T(8,128)(2,1)S(1)}, bf16[256,2048]{1,0:T(8,128)(2,1)}, u32[]{:S(2)}, u32[]{:S(2)}) %collective-permute-start.25) | collective-permute-done | bytes 1048608 | tf_op jit(solution)/shard_map/ppermute | solution.py:45
  692.1 22.9 %collective-permute-done.26.refs_2_.refs_6_ = bf16[256,2048]{1,0:T(8,128)(2,1)} collective-permute-done((bf16[256,2048]{1,0:T(8,128)(2,1)}, bf16[256,2048]{1,0:T(8,128)(2,1)}, u32[]{:S(2)}, u32[]{:S(2)}) %collective-permute-start.26) | collective-permute-done | bytes 1048608 | tf_op jit(solution)/shard_map/ppermute | solution.py:45
  718.6 17.0 %collective-permute-done.32.refs_1_.refs_5_ = bf16[256,2048]{1,0:T(8,128)(2,1)S(1)} collective-permute-done((bf16[256,2048]{1,0:T(8,128)(2,1)}, bf16[256,2048]{1,0:T(8,128)(2,1)S(1)}, u32[]{:S(2)}, u32[]{:S(2)}) %collective-permute-start.32) | collective-permute-done | bytes 1048608 | tf_op jit(solution)/shard_map/ppermute | solution.py:45
  735.6 20.6 %collective-permute-done.33.refs_2_.refs_6_ = bf16[256,2048]{1,0:T(8,128)(2,1)S(1)} collective-permute-done((bf16[256,2048]{1,0:T(8,128)(2,1)}, bf16[256,2048]{1,0:T(8,128)(2,1)S(1)}, u32[]{:S(2)}, u32[]{:S(2)}) %collective-permute-start.33) | collective-permute-done | bytes 1048608 | tf_op jit(solution)/shard_map/ppermute | solution.py:45
  762.0 27.0 %collective-permute-done.28.far_ref = bf16[128,2048]{1,0:T(8,128)(2,1)} collective-permute-done((bf16[128,2048]{1,0:T(8,128)(2,1)}, bf16[128,2048]{1,0:T(8,128)(2,1)}, u32[]{:S(2)}, u32[]{:S(2)}) %collective-permute-start.28) | collective-permute-done | bytes 524320 | tf_op jit(solution)/shard_map/ppermute | solution.py:45
  864.5 13.9 %to_peers.6 = (f32[512,2048]{1,0:T(8,128)}, bf16[512,2048]{1,0:T(8,128)(2,1)}, bf16[512,2048]{1,0:T(8,128)(2,1)}, bf16[512,2048]{1,0:T(8,128)(2,1)}) custom-call(bf16[2048,1024]{1,0:T(8,128)(2,1)} %copy-done.11, bf16[2048,1024]{1,0:T(8,128)(2,1)} %all-gather.14.cloned.1.call-done.wd_ref.refs_1_), custom_call_target="tpu_custom_call" | custom-call | tf_op jit(solution)/shard_map/to_peers/pallas_call | solution.py:451
  885.2 20.4 %attend_back.3 = bf16[8,4,192,128]{3,2,1,0:T(8,128)(2,1)} custom-call(s32[4]{0:T(128)} %get-tuple-element.273.prefix_ref, bf16[8,4,192,128]{3,2,1,0:T(8,128)(2,1)} %copy-done.6, bf16[8,4,64,128]{3,2,1,0:T(8,128)(2,1)} %get-tuple-element.128.o_ref, bf16[8,8,64,128]{3,2,1,0:T(8,128)(2,1)} %copy-done.8, f32[4,1,1024]{2,1,0:T(1,128)} %get-tuple-element.125.lse_ref), custom_call_target="tpu_custom_call" | custom-call | tf_op jit(solution)/shard_map/attend_back/pallas_call | solution.py:338
  916.9 21.1 %attend_back.2 = bf16[8,4,192,128]{3,2,1,0:T(8,128)(2,1)} custom-call(s32[4]{0:T(128)} %get-tuple-element.272.prefix_ref, bf16[8,4,192,128]{3,2,1,0:T(8,128)(2,1)} %copy-done.5, bf16[8,4,64,128]{3,2,1,0:T(8,128)(2,1)} %get-tuple-element.127.o_ref, bf16[8,8,64,128]{3,2,1,0:T(8,128)(2,1)} %copy-done.8, f32[4,1,1024]{2,1,0:T(1,128)} %get-tuple-element.144.lse_ref), custom_call_target="tpu_custom_call" | custom-call | tf_op jit(solution)/shard_map/attend_back/pallas_call | solution.py:338
  963.7 26.3 %all-to-all-done.4.refs_0_ = bf16[8,4,192,128]{3,2,1,0:T(8,128)(2,1)} async-done(((bf16[8,4,192,128]{3,2,1,0:T(8,128)(2,1)}), bf16[8,4,192,128]{3,2,1,0:T(8,128)(2,1)}, u32[]{:S(2)}, u32[]{:S(2)}) %all-to-all-start.4) | async-done | bytes 1572896 | tf_op jit(solution)/shard_map/all_to_all | solution.py:730
  1012.6 41.3 %collective-permute-done.40 = bf16[512,2048]{1,0:T(8,128)(2,1)} collective-permute-done((bf16[512,2048]{1,0:T(8,128)(2,1)}, bf16[512,2048]{1,0:T(8,128)(2,1)}, u32[]{:S(2)}, u32[]{:S(2)}) %collective-permute-start.40) | collective-permute-done | bytes 2097184 | tf_op jit(solution)/shard_map/ppermute | solution.py:45
  1066.1 63.7 %collective-permute-done.52 = bf16[256,1024]{1,0:T(8,128)(2,1)S(1)} collective-permute-done((bf16[256,1024]{1,0:T(8,128)(2,1)S(1)}, bf16[256,1024]{1,0:T(8,128)(2,1)S(1)}, u32[]{:S(2)}, u32[]{:S(2)}) %collective-permute-start.52) | collective-permute-done | bytes 524320 | tf_op jit(solution)/shard_map/ppermute | solution.py:45
  1169.3 21.8 %collective-permute-done.44 = bf16[256,2048]{1,0:T(8,128)(2,1)S(1)} collective-permute-done((bf16[256,2048]{1,0:T(8,128)(2,1)}, bf16[256,2048]{1,0:T(8,128)(2,1)S(1)}, u32[]{:S(2)}, u32[]{:S(2)}) %collective-permute-start.44) | collective-permute-done | bytes 1048608 | tf_op jit(solution)/shard_map/ppermute | solution.py:45
  (422 shorter events, 512.1 us)
Async XLA Ops:
  7.2 70.5 %all-gather.6.cloned.1.call-start = ((), (), s32[]{:S(2)}) async-start(), calls=%async_computation.10 | async-start | bytes 7077888 | tf_op jit(solution)/shard_map/all_gather | solution.py:774
  91.4 58.2 %all-to-all-start.1 = ((bf16[8,4,192,128]{3,2,1,0:T(8,128)(2,1)}), bf16[8,4,192,128]{3,2,1,0:T(8,128)(2,1)S(1)}, u32[]{:S(2)}, u32[]{:S(2)}) async-start(bf16[8,4,192,128]{3,2,1,0:T(8,128)(2,1)} %get-tuple-element.123), calls=%async_computation.1 | async-start | bytes 3145728 | tf_op jit(solution)/shard_map/all_to_all | solution.py:726
  95.0 64.1 %all-gather.8.cloned.1.call-start = ((), (), s32[]{:S(2)}) async-start(), calls=%async_computation.11 | async-start | bytes 2359296 | tf_op jit(solution)/shard_map/all_gather | solution.py:774
  156.5 61.7 %collective-permute-start.15 = (bf16[256,3072]{1,0:T(8,128)(2,1)S(1)}, bf16[256,3072]{1,0:T(8,128)(2,1)}, u32[]{:S(2)}, u32[]{:S(2)}) collective-permute-start(bf16[256,3072]{1,0:T(8,128)(2,1)S(1)} %pad_maximum_fusion.1), channel_id=1, source_target_pairs={{0,8},{4,12},{8,0},{12,4},{16,24},{20,28},{24,16},{28,20},{1,9},{5... | collective-permute-start | bytes 4718600 | tf_op jit(solution)/shard_map/ppermute | solution.py:45
  218.1 314.0 %all-gather.10.cloned.1.call-start = ((), (), s32[]{:S(2)}) async-start(), calls=%async_computation.12 | async-start | bytes 5242880 | tf_op jit(solution)/shard_map/all_gather | solution.py:148
  244.6 287.5 %all-gather.12.cloned.1.call-start = ((), (), s32[]{:S(2)}) async-start(), calls=%async_computation.13 | async-start | bytes 5242880 | tf_op jit(solution)/shard_map/all_gather | solution.py:148
  323.2 254.2 %all-gather.14.cloned.1.call-start = ((), (), s32[]{:S(2)}) async-start(), calls=%async_computation.14 | async-start | bytes 5242880 | tf_op jit(solution)/shard_map/all_gather | solution.py:148
  363.7 117.5 %collective-permute-start.24 = (bf16[512,2048]{1,0:T(8,128)(2,1)S(1)}, bf16[512,2048]{1,0:T(8,128)(2,1)}, u32[]{:S(2)}, u32[]{:S(2)}) collective-permute-start(bf16[512,2048]{1,0:T(8,128)(2,1)S(1)} %pad_maximum_fusion), channel_id=1, source_target_pairs={{0,3},{1,2},{2,1},{3,0},{4,7},{5,6},{6,5},{7,4},{8,11},{9,10},{10,... | collective-permute-start | bytes 6291464 | tf_op jit(solution)/shard_map/ppermute | solution.py:45
  366.4 116.2 %collective-permute-start.23 = (bf16[512,2048]{1,0:T(8,128)(2,1)S(1)}, bf16[512,2048]{1,0:T(8,128)(2,1)}, u32[]{:S(2)}, u32[]{:S(2)}) collective-permute-start(bf16[512,2048]{1,0:T(8,128)(2,1)S(1)} %pad_maximum_fusion), channel_id=1, source_target_pairs={{0,2},{1,3},{2,0},{3,1},{4,6},{5,7},{6,4},{7,5},{8,10},{9,11},{10,... | collective-permute-start | bytes 6291464 | tf_op jit(solution)/shard_map/ppermute | solution.py:45
  367.0 115.6 %collective-permute-start.22 = (bf16[512,2048]{1,0:T(8,128)(2,1)S(1)}, bf16[512,2048]{1,0:T(8,128)(2,1)}, u32[]{:S(2)}, u32[]{:S(2)}) collective-permute-start(bf16[512,2048]{1,0:T(8,128)(2,1)S(1)} %pad_maximum_fusion), channel_id=1, source_target_pairs={{0,1},{1,0},{2,3},{3,2},{4,5},{5,4},{6,7},{7,6},{8,9},{9,8},{10,11... | collective-permute-start | bytes 6291464 | tf_op jit(solution)/shard_map/ppermute | solution.py:45
  367.3 111.6 %collective-permute-start.12 = (bf16[256,2048]{1,0:T(8,128)(2,1)}, bf16[256,2048]{1,0:T(8,128)(2,1)S(1)}, u32[]{:S(2)}, u32[]{:S(2)}) collective-permute-start(bf16[256,2048]{1,0:T(8,128)(2,1)} %get-tuple-element.318), channel_id=1, source_target_pairs={{0,2},{1,3},{2,0},{3,1},{4,6},{5,7},{6,4},{7,5},{8,10},{9,11},{10,... | collective-permute-start | bytes 3145736 | tf_op jit(solution)/shard_map/ppermute | solution.py:45
  369.0 110.1 %collective-permute-start.11 = (bf16[256,2048]{1,0:T(8,128)(2,1)}, bf16[256,2048]{1,0:T(8,128)(2,1)}, u32[]{:S(2)}, u32[]{:S(2)}) collective-permute-start(bf16[256,2048]{1,0:T(8,128)(2,1)} %get-tuple-element.318), channel_id=1, source_target_pairs={{0,1},{1,0},{2,3},{3,2},{4,5},{5,4},{6,7},{7,6},{8,9},{9,8},{10,11... | collective-permute-start | bytes 3145736 | tf_op jit(solution)/shard_map/ppermute | solution.py:45
  371.5 291.8 %reduce-scatter.5.cloned.1.call-start = ((), (), s32[]{:S(2)}) async-start(), calls=%async_computation.15 | async-start | bytes 5242880 | tf_op jit(solution)/shard_map/reduce_scatter | solution.py:158
  577.4 301.0 %reduce-scatter.7.cloned.1.call-start = ((), (), s32[]{:S(2)}) async-start(), calls=%async_computation.16 | async-start | bytes 10485760 | tf_op jit(solution)/shard_map/reduce_scatter | solution.py:158
  668.0 67.5 %collective-permute-start.32 = (bf16[256,2048]{1,0:T(8,128)(2,1)}, bf16[256,2048]{1,0:T(8,128)(2,1)S(1)}, u32[]{:S(2)}, u32[]{:S(2)}) collective-permute-start(bf16[256,2048]{1,0:T(8,128)(2,1)} %get-tuple-element.174), channel_id=1, source_target_pairs={{0,1},{1,0},{2,3},{3,2},{4,5},{5,4},{6,7},{7,6},{8,9},{9,8},{10,11... | collective-permute-start | bytes 3145736 | tf_op jit(solution)/shard_map/ppermute | solution.py:45
  669.7 86.5 %collective-permute-start.33 = (bf16[256,2048]{1,0:T(8,128)(2,1)}, bf16[256,2048]{1,0:T(8,128)(2,1)S(1)}, u32[]{:S(2)}, u32[]{:S(2)}) collective-permute-start(bf16[256,2048]{1,0:T(8,128)(2,1)} %get-tuple-element.175), channel_id=1, source_target_pairs={{0,2},{1,3},{2,0},{3,1},{4,6},{5,7},{6,4},{7,5},{8,10},{9,11},{10,... | collective-permute-start | bytes 3145736 | tf_op jit(solution)/shard_map/ppermute | solution.py:45
  690.7 65.5 %collective-permute-start.34 = (bf16[256,2048]{1,0:T(8,128)(2,1)}, bf16[256,2048]{1,0:T(8,128)(2,1)S(1)}, u32[]{:S(2)}, u32[]{:S(2)}) collective-permute-start(bf16[256,2048]{1,0:T(8,128)(2,1)} %get-tuple-element.176), channel_id=1, source_target_pairs={{0,3},{1,2},{2,1},{3,0},{4,7},{5,6},{6,5},{7,4},{8,11},{9,10},{10,... | collective-permute-start | bytes 3145736 | tf_op jit(solution)/shard_map/ppermute | solution.py:45
  857.8 57.3 %reduce-scatter.9.cloned.1.call-start = ((), (), s32[]{:S(2)}) async-start(), calls=%async_computation.17 | async-start | bytes 2359296 | tf_op jit(solution)/shard_map/reduce_scatter | solution.py:777
  952.1 260.1 %reduce-scatter.11.cloned.1.call-start = ((), (), s32[]{:S(2)}) async-start(), calls=%async_computation.18 | async-start | bytes 7077888 | tf_op jit(solution)/shard_map/reduce_scatter | solution.py:777
  961.0 92.8 %collective-permute-start.40 = (bf16[512,2048]{1,0:T(8,128)(2,1)}, bf16[512,2048]{1,0:T(8,128)(2,1)}, u32[]{:S(2)}, u32[]{:S(2)}) collective-permute-start(bf16[512,2048]{1,0:T(8,128)(2,1)} %get-tuple-element.204), channel_id=1, source_target_pairs={{0,2},{1,3},{2,0},{3,1},{4,6},{5,7},{6,4},{7,5},{8,10},{9,11},{10,... | collective-permute-start | bytes 6291464 | tf_op jit(solution)/shard_map/ppermute | solution.py:45
  962.8 91.1 %collective-permute-start.41 = (bf16[512,2048]{1,0:T(8,128)(2,1)}, bf16[512,2048]{1,0:T(8,128)(2,1)}, u32[]{:S(2)}, u32[]{:S(2)}) collective-permute-start(bf16[512,2048]{1,0:T(8,128)(2,1)} %get-tuple-element.205), channel_id=1, source_target_pairs={{0,3},{1,2},{2,1},{3,0},{4,7},{5,6},{6,5},{7,4},{8,11},{9,10},{10,... | collective-permute-start | bytes 6291464 | tf_op jit(solution)/shard_map/ppermute | solution.py:45
  1012.5 118.2 %collective-permute-start.51 = (bf16[256,2048]{1,0:T(8,128)(2,1)S(1)}, bf16[256,2048]{1,0:T(8,128)(2,1)}, u32[]{:S(2)}, u32[]{:S(2)}) collective-permute-start(bf16[256,2048]{1,0:T(8,128)(2,1)S(1)} %constant_dynamic-slice_fusion.2), channel_id=1, source_target_pairs={{0,8},{4,12},{8,0},{12,4},{16,24},{20,28},{24,16},{28,20},{1,9},{5... | collective-permute-start | bytes 3145736 | tf_op jit(solution)/shard_map/ppermute | solution.py:45
  1060.7 85.9 %collective-permute-start.42 = (bf16[256,2048]{1,0:T(8,128)(2,1)}, bf16[256,2048]{1,0:T(8,128)(2,1)}, u32[]{:S(2)}, u32[]{:S(2)}) collective-permute-start(bf16[256,2048]{1,0:T(8,128)(2,1)} %pad_maximum_fusion.6), channel_id=1, source_target_pairs={{0,8},{4,12},{8,0},{12,4},{16,24},{20,28},{24,16},{28,20},{1,9},{5... | collective-permute-start | bytes 3145736 | tf_op jit(solution)/shard_map/ppermute | solution.py:45
  1063.8 66.0 %collective-permute-start.52 = (bf16[256,1024]{1,0:T(8,128)(2,1)S(1)}, bf16[256,1024]{1,0:T(8,128)(2,1)S(1)}, u32[]{:S(2)}, u32[]{:S(2)}) collective-permute-start(bf16[256,1024]{1,0:T(8,128)(2,1)S(1)} %constant_dynamic-slice_fusion.1), channel_id=1, source_target_pairs={{0,8},{4,12},{8,0},{12,4},{16,24},{20,28},{24,16},{28,20},{1,9},{5... | collective-permute-start | bytes 1572872 | tf_op jit(solution)/shard_map/ppermute | solution.py:45
  (112 other events, 1937.1 us)
Sparse Core Ops, SparseCore 0:
  10.2 67.4 all-gather.5
  97.5 50.8 all-gather.7
  244.8 56.7 all-gather.9
  323.3 56.8 all-gather.11
  381.6 56.8 all-gather.13
  577.5 66.1 reduce-scatter.4
  663.5 115.6 reduce-scatter.6
  878.5 36.5 reduce-scatter.8
  1010.9 117.1 reduce-scatter.10

commit v4 on v3

--- a/solution.py
+++ b/solution.py
@@ -16,6 +16,7 @@
 LOG2E = math.log2(math.e)
 MASKED = -1e30
 PAIR = 2
+FSDP, TENSOR = "fsdp", "tensor"
 BF16 = jnp.bfloat16
 F32 = jnp.float32
 
@@ -50,14 +51,14 @@
 
 
 def spread_pieces(value, direct=True):
-    count = lax.axis_size("tensor")
+    count = lax.axis_size(TENSOR)
     if direct or count != 4:
-        return [value] + [swap(value, "tensor", k) for k in range(1, count)]
+        return [value] + [swap(value, TENSOR, k) for k in range(1, count)]
     half = value.shape[0] // 2
-    one = swap(value, "tensor", 1)
-    two = swap(value, "tensor", 2)
-    low = swap(two[:half], "tensor", 1)
-    high = swap(one[half:], "tensor", 2)
+    one = swap(value, TENSOR, 1)
+    two = swap(value, TENSOR, 2)
+    low = swap(two[:half], TENSOR, 1)
+    high = swap(one[half:], TENSOR, 2)
     return [value, one, two, low, high]
 
 
@@ -74,9 +75,9 @@
 
 
 def collect(parts, direct=True, token=None):
-    count = lax.axis_size("tensor")
+    count = lax.axis_size(TENSOR)
     if direct or count != 4:
-        blocks = [swap(parts[k].astype(BF16), "tensor", k) for k in range(1, count)]
+        blocks = [swap(parts[k].astype(BF16), TENSOR, k) for k in range(1, count)]
         if token is not None:
             blocks = after(blocks, token)
         total = parts[0]
@@ -85,21 +86,21 @@
         return total
     half = parts[0].shape[0] // 2
     far = parts[3].astype(BF16)
-    low = swap(far[:half], "tensor", 1).astype(F32)
-    high = swap(far[half:], "tensor", 2).astype(F32)
+    low = swap(far[:half], TENSOR, 1).astype(F32)
+    high = swap(far[half:], TENSOR, 2).astype(F32)
     one = jnp.concatenate([parts[1][:half], parts[1][half:] + high], axis=0)
     two = jnp.concatenate([parts[2][:half] + low, parts[2][half:]], axis=0)
-    one = swap(one.astype(BF16), "tensor", 1).astype(F32)
-    two = swap(two.astype(BF16), "tensor", 2).astype(F32)
+    one = swap(one.astype(BF16), TENSOR, 1).astype(F32)
+    two = swap(two.astype(BF16), TENSOR, 2).astype(F32)
     return parts[0] + one + two
 
 
 def peer_swaps(parts):
-    return [swap(part, "tensor", k) for k, part in enumerate(parts) if k]
+    return [swap(part, TENSOR, k) for k, part in enumerate(parts) if k]
 
 
 def pair_join(value, micros):
-    other = swap(value, "fsdp", PAIR)
+    other = swap(value, FSDP, PAIR)
     size = value.shape[0] // micros
     parts = [v[m * size : (m + 1) * size] for m in range(micros) for v in (value, other)]
     return jnp.concatenate(parts, axis=0)
@@ -117,7 +118,7 @@
 
 
 def paired(values):
-    count = lax.axis_size("fsdp")
+    count = lax.axis_size(FSDP)
     size = values.shape[-1] // count
     order = paired_order(count)
     parts = [lax.slice_in_dim(values, f * size, (f + 1) * size, axis=-1) for f in order]
@@ -125,7 +126,7 @@
 
 
 def pair_groups():
-    count = lax.axis_size("fsdp")
+    count = lax.axis_size(FSDP)
     return [[f for f in range(count) if bool(f & PAIR) == side] for side in (False, True)]
 
 
@@ -147,7 +148,7 @@
 def gather_half(shard):
     return lax.all_gather(
         shard,
-        "fsdp",
+        FSDP,
         axis=0,
         tiled=True,
         axis_index_groups=pair_groups(),
@@ -156,14 +157,14 @@
 
 def scatter_half(grad):
     return lax.psum_scatter(
-        grad, "fsdp", scatter_dimension=0, tiled=True, axis_index_groups=pair_groups()
+        grad, FSDP, scatter_dimension=0, tiled=True, axis_index_groups=pair_groups()
     )
 
 
 def settle_half(part, side, pieces, token):
     rows = part.shape[0] // 2
     mine = lax.dynamic_slice_in_dim(part, side * rows, rows, 0)
-    other = swap(lax.dynamic_slice_in_dim(part, (1 - side) * rows, rows, 0), "fsdp", PAIR)
+    other = swap(lax.dynamic_slice_in_dim(part, (1 - side) * rows, rows, 0), FSDP, PAIR)
     low, high = order_pair(side, mine, after(other, token))
     half = part.shape[1] // pieces
     return [
@@ -216,11 +217,13 @@
     for qb in range(blocks):
         q_t = span_block(x_ref, qb * group, group, 0, HEAD_DIM)
 
-        def step(kb, carry):
+        def step(kb, carry, masked=True):
             top, total, acc = carry
-            keys = key_ref[pl.ds(pl.multiple_of(kb * block, block), block), :]
+            first = pl.multiple_of(kb * block, block) if masked else kb * block
+            keys = key_ref[pl.ds(first, block), :]
             scores = dot(keys, q_t, 1, 0) * coef
-            scores = jnp.where(allowed_mask(kb, qb, block, prefix), scores, MASKED)
+            if masked:
+                scores = jnp.where(allowed_mask(kb, qb, block, prefix), scores, MASKED)
             new_top = jnp.maximum(top, jnp.max(scores, axis=0, keepdims=True))
             probs = jnp.exp2(scores - new_top)
             shrink = jnp.exp2(top - new_top)
@@ -229,15 +232,15 @@
             acc = shrink * acc + dot(v_t, probs.astype(BF16), 1, 0)
             return new_top, total, acc
 
+        carry = (
+            jnp.full((1, block), MASKED, F32),
+            jnp.zeros((1, block), F32),
+            jnp.zeros((HEAD_DIM, block), F32),
+        )
+        for kb in range(qb):
+            carry = step(kb, carry, False)
         top, total, acc = lax.fori_loop(
-            0,
-            key_count(qb, block, prefix, blocks),
-            step,
-            (
-                jnp.full((1, block), MASKED, F32),
-                jnp.zeros((1, block), F32),
-                jnp.zeros((HEAD_DIM, block), F32),
-            ),
+            qb, key_count(qb, block, prefix, blocks), step, carry
         )
         out = (acc / total).astype(BF16)
         for i in range(group):
@@ -267,10 +270,11 @@
         delta = jnp.sum(do_t.astype(F32) * o_t.astype(F32), axis=0, keepdims=True)
         lse = lse_ref[0, :, qb * block : (qb + 1) * block]
 
-        def step(kb, dq):
-            rows = pl.ds(pl.multiple_of(kb * block, block), block)
+        def step(kb, dq, masked=True):
+            rows = pl.ds(pl.multiple_of(kb * block, block) if masked else kb * block, block)
             scores = dot(key_ref[rows, :], q_t, 1, 0) * coef
-            scores = jnp.where(allowed_mask(kb, qb, block, prefix), scores, MASKED)
+            if masked:
+                scores = jnp.where(allowed_mask(kb, qb, block, prefix), scores, MASKED)
             probs = jnp.exp2(scores - lse)
             grad_probs = dot(val_ref[rows, :], do_t, 1, 0)
             grad_scores = (probs * (grad_probs - delta)).astype(BF16)
@@ -279,12 +283,10 @@
             k_t = span_block(x_ref, kb * group, group, HEAD_DIM, 2 * HEAD_DIM)
             return dq + dot(k_t, grad_scores, 1, 0)
 
-        dq = lax.fori_loop(
-            0,
-            key_count(qb, block, prefix, blocks),
-            step,
-            jnp.zeros((HEAD_DIM, block), F32),
-        )
+        dq = jnp.zeros((HEAD_DIM, block), F32)
+        for kb in range(qb):
+            dq = step(kb, dq, False)
+        dq = lax.fori_loop(qb, key_count(qb, block, prefix, blocks), step, dq)
         dq = (dq * scale).astype(BF16)
         for i in range(group):
             dx_ref[qb * group + i, 0, :HEAD_DIM, :] = dq[:, i * span_len : (i + 1) * span_len]
@@ -323,8 +325,6 @@
             out_specs=[pair_spec(out_shape), lse_spec(tokens)],
             scratch_shapes=[pltpu.VMEM((tokens, HEAD_DIM), BF16)],
         ),
-        compiler_params=pltpu.CompilerParams(dimension_semantics=("arbitrary",)),
-        name="attend_forward",
     )(prefix, packed)
 
 
@@ -355,8 +355,6 @@
                 acc,
             ],
         ),
-        compiler_params=pltpu.CompilerParams(dimension_semantics=("arbitrary",)),
-        name="attend_back",
     )(prefix, packed, out, grad_out, lse)
 
 
@@ -395,7 +393,6 @@
             jax.ShapeDtypeStruct((count, units), F32),
             jax.ShapeDtypeStruct((count, units), BF16),
         ],
-        name="ffn_forward",
     )(rows, w_gate, w_up)
 
 
@@ -423,7 +420,6 @@
         ],
         out_specs=[col_tile(count, tile)] * 2,
         out_shape=[jax.ShapeDtypeStruct((count, units), BF16)] * 2,
-        name="ffn_back",
     )(grad_rows, w_down, gate, up)
 
 
@@ -457,7 +453,6 @@
         out_shape=[
             jax.ShapeDtypeStruct((rows, width), BF16 if k else F32) for k in range(peers)
         ],
-        name="to_peers",
     )(*lefts, *rights)
 
 
@@ -497,8 +492,20 @@
         + [row_block(tile, width)] * (1 + len(blocks)),
         out_specs=[row_block(tile, width)] * 3,
         out_shape=[jax.ShapeDtypeStruct((rows, width), kind) for kind in (F32, F32, BF16)],
-        name="norm_rows",
     )(inputs, gain, own, *blocks)
+
+
+def join_kernel(near_ref, far_ref, out_ref):
+    rows = near_ref.shape[0]
+    out_ref[:rows, :] = near_ref[...]
+    out_ref[rows:, :] = far_ref[...]
+
+
+def join(near, far):
+    rows, width = near.shape
+    return pl.pallas_call(
+        join_kernel, out_shape=jax.ShapeDtypeStruct((2 * rows, width), near.dtype)
+    )(near, far)
 
 
 def peer_sum_kernel(*refs):
@@ -522,7 +529,6 @@
         ],
         out_specs=[row_block(tile, width)] * 2,
         out_shape=[jax.ShapeDtypeStruct((rows, width), kind) for kind in (F32, BF16)],
-        name="peer_sum",
     )(*pieces, *pieces)
 
 
@@ -556,7 +562,6 @@
             jax.ShapeDtypeStruct((1, width), F32),
         ],
         scratch_shapes=[pltpu.VMEM((tile, width), F32)],
-        name="norm_grad",
     )(grads, gain, near, far, res)
 
 
@@ -607,7 +612,6 @@
         + [whole(cos_tab.shape)] * 2,
         out_specs=[pl.BlockSpec((2,) + out[1:], lambda n: (n, 0, 0, 0))] * micros,
         out_shape=[jax.ShapeDtypeStruct(out, BF16)] * micros,
-        name="project",
     )(*pieces, weights, weights, weights, cos_tab, sin_tab)
 
 
@@ -642,7 +646,6 @@
         + [col_tile(rows, tile)] * len(kinds),
         out_shape=[jax.ShapeDtypeStruct((seqs * span, cols), BF16)]
         + [jax.ShapeDtypeStruct((rows, width), kind) for kind in kinds],
-        name="mix_out",
     )(packed, weights)
 
 
@@ -671,43 +674,39 @@
         in_specs=[whole(p.shape) for p in pieces] + [col_tile(width, tile)],
         out_specs=pl.BlockSpec((tile // HEAD_DIM, seqs, HEAD_DIM, span), lambda n: (n, 0, 0, 0)),
         out_shape=jax.ShapeDtypeStruct((heads, seqs, HEAD_DIM, span), BF16),
-        name="mix_back",
     )(*pieces, weights)
 
 
-def unturn_kernel(blocks, *refs):
-    packed, (cos_ref, sin_ref, out_ref) = refs[:-3], refs[-3:]
-    _, seqs, _, span = packed[0].shape
-    plain = pl.program_id(0) >= 2 * blocks
-    for m, ref in enumerate(packed):
-        for k in range(seqs):
-            cos_tab = jnp.where(plain, 1.0, cos_ref[m, :, k * span : (k + 1) * span])
-            sin_tab = jnp.where(plain, 0.0, -sin_ref[m, :, k * span : (k + 1) * span])
+def unturn_kernel(ref, cos_ref, sin_ref, *refs):
+    out_ref = refs[-1]
+    heads, seqs, _, span = ref.shape
+    plain = pl.program_id(0) >= 2
+    for k in range(seqs):
+        cos_tab = jnp.where(plain, 1.0, cos_ref[:, k * span : (k + 1) * span])
+        sin_tab = jnp.where(plain, 0.0, -sin_ref[:, k * span : (k + 1) * span])
+        for h in range(0, heads, 2):
             pair = jnp.concatenate(
-                [turn(ref[h, k].astype(F32), cos_tab, sin_tab) for h in range(2)], axis=0
+                [turn(ref[h + i, k].astype(F32), cos_tab, sin_tab) for i in range(2)], axis=0
             )
-            first = (m * seqs + k) * span
-            out_ref[first : first + span, :] = pair.T.astype(BF16)
-
-
-def unturn(packed, cos_tab, sin_tab):
-    heads, seqs, _, span = packed[0].shape
-    blocks = heads // 2
-    rows = len(packed) * seqs * span
-    return pl.pallas_call(
-        functools.partial(unturn_kernel, blocks),
-        grid=(3 * blocks,),
-        in_specs=[
-            pl.BlockSpec(
-                (2, seqs, HEAD_DIM, span), lambda n: (n % blocks, 0, n // blocks, 0)
+            out_ref[k * span : (k + 1) * span, h * HEAD_DIM : (h + 2) * HEAD_DIM] = pair.T.astype(
+                BF16
             )
-        ]
-        * len(packed)
-        + [whole(cos_tab.shape)] * 2,
-        out_specs=col_tile(rows, 2 * HEAD_DIM),
-        out_shape=jax.ShapeDtypeStruct((rows, 3 * heads * HEAD_DIM), BF16),
-        name="unturn",
-    )(*packed, cos_tab, sin_tab)
+
+
+def unturn(packed, micro, micros, cos_tab, sin_tab, into):
+    heads, seqs, _, span = packed.shape
+    rows = seqs * span
+    extra = [] if into is None else [into]
+    return pl.pallas_call(
+        unturn_kernel,
+        grid=(3,),
+        in_specs=[pl.BlockSpec((heads, seqs, HEAD_DIM, span), lambda n: (0, 0, n, 0))]
+        + [whole(cos_tab.shape)] * 2
+        + [pl.BlockSpec(memory_space=pl.ANY) for _ in extra],
+        out_specs=pl.BlockSpec((rows, heads * HEAD_DIM), lambda n: (micro, n)),
+        out_shape=jax.ShapeDtypeStruct((micros * rows, 3 * heads * HEAD_DIM), BF16),
+        input_output_aliases={3: 0} if extra else {},
+    )(packed, cos_tab, sin_tab, *extra)
 
 
 class HeadSplit:
@@ -723,11 +722,11 @@
             self.head_groups, self.heads_per, -1, self.seq_groups, self.seqs_per, width, span
         ).transpose(3, 0, 2, 1, 4, 5, 6)
         packed = packed.reshape(self.seq_groups * self.head_groups, -1, width, span)
-        return lax.all_to_all(packed, "fsdp", split_axis=0, concat_axis=0, tiled=True)
+        return lax.all_to_all(packed, FSDP, split_axis=0, concat_axis=0, tiled=True)
 
     def to_spans(self, packed):
         width, span = packed.shape[2:]
-        packed = lax.all_to_all(packed, "fsdp", split_axis=0, concat_axis=0, tiled=True)
+        packed = lax.all_to_all(packed, FSDP, split_axis=0, concat_axis=0, tiled=True)
         packed = packed.reshape(
             self.seq_groups, self.head_groups, -1, self.heads_per, self.seqs_per, width, span
         ).transpose(1, 3, 2, 0, 4, 5, 6)
@@ -756,27 +755,27 @@
     w_down,
 ):
     micro_count, seq_dev, span_len, model_width = inputs.shape
-    n_tensor = lax.axis_size("tensor")
-    n_fsdp = lax.axis_size("fsdp")
+    n_tensor = lax.axis_size(TENSOR)
+    n_fsdp = lax.axis_size(FSDP)
     seq_mb = seq_dev * n_tensor
     seq_len = span_len * n_fsdp
     own_rows = seq_dev * span_len
     head_cols = w_query.shape[1]
     head_count = head_cols // HEAD_DIM
     ff_cols = w_gate.shape[1]
-    fsdp_index = lax.axis_index("fsdp")
-    tensor_index = lax.axis_index("tensor")
+    fsdp_index = lax.axis_index(FSDP)
+    tensor_index = lax.axis_index(TENSOR)
     query_index = fsdp_index * span_len + jnp.arange(span_len, dtype=jnp.int32)
     split = HeadSplit(n_fsdp, head_count, seq_mb)
     micros = range(micro_count)
 
     def gather(shard):
-        return lax.all_gather(shard, "fsdp", axis=0, tiled=True)
+        return lax.all_gather(shard, FSDP, axis=0, tiled=True)
 
     def scatter(grad):
-        return lax.psum_scatter(grad, "fsdp", scatter_dimension=0, tiled=True).astype(F32)
-
-    gains = lax.all_gather(jnp.stack([attn_gain, mlp_gain]), "fsdp", axis=1, tiled=True)
+        return lax.psum_scatter(grad, FSDP, scatter_dimension=0, tiled=True).astype(F32)
+
+    gains = lax.all_gather(jnp.stack([attn_gain, mlp_gain]), FSDP, axis=1, tiled=True)
     gain_attn = gains[0].astype(F32)
     gain_mlp = gains[1].astype(F32)
     full_qkv = gather(jnp.concatenate([w_query, w_key, w_value], axis=1))
@@ -830,7 +829,7 @@
     normed_rows = gather_rows(whole_blocks(after(normed_pieces, stack)), micro_count)
     grad_pair = after(grad_pair, stack)
     grad_blocks = spread(grad_pair)
-    ffn_other = swap(after(ffn_far, packed[-1]), "fsdp", PAIR)
+    ffn_other = swap(after(ffn_far, packed[-1]), FSDP, PAIR)
     attn_out, attn_lse = [None] * micro_count, [None] * micro_count
     done = full_out
     for m in reversed(micros):
@@ -860,10 +859,10 @@
         branch.append(part)
         resid.append(res)
         normed_mlp.append(normed)
-        others.append(swap(normed, "fsdp", PAIR))
+        others.append(swap(normed, FSDP, PAIR))
     for m in micros:
         other = after(others[m], joined) if m else others[m]
-        joined.append(jnp.concatenate([normed_mlp[m], other], axis=0))
+        joined.append(join(normed_mlp[m], other))
     full_up = gather_half(after(shards[1], joined))
     full_down = gather_half(shards[2])
     mlp_rows, first = [], None
@@ -898,7 +897,7 @@
         blocks = peer_swaps(normed_part[m])
         blocks = after(blocks, near_far[-1][0] if m else gu_grad)
         near, far = peer_sum(normed_part[m][0], blocks)
-        near_far.append((near, swap(far, "fsdp", PAIR)))
+        near_far.append((near, swap(far, FSDP, PAIR)))
     low = None
     for m in micros:
         near, far = near_far[m]
@@ -929,13 +928,15 @@
     mlp_part = collect(mlp_blocks, token=packed_grads[0])
     near = [mlp_part[2 * m * own_rows : (2 * m + 1) * own_rows] for m in micros]
     far = [mlp_part[(2 * m + 1) * own_rows : (2 * m + 2) * own_rows] for m in micros]
-    far = swap(jnp.concatenate(far, axis=0).astype(BF16), "fsdp", PAIR)
-    grad_qkv = unturn(grad_raw, cos_all, sin_all)
+    far = swap(jnp.concatenate(far, axis=0).astype(BF16), FSDP, PAIR)
+    grad_qkv = None
+    for m in reversed(micros):
+        grad_qkv = unturn(grad_raw[m], m, micro_count, cos_all[m], sin_all[m], grad_qkv)
     qkv_grad = dot(normed_rows, grad_qkv, 0, 0).astype(BF16)
     own_gate, own_up = settle_half(part_gu, side, 2, qkv_grad)
     (own_down,) = settle_half(part_down, side, 1, qkv_grad)
     part = to_peers([after(grad_qkv, qkv_grad)], [full_qkv], micro_count, n_tensor)
-    grad_normed = collect(part)
+    grad_normed = collect(part, False)
     far = after(far, part).astype(F32)
     mlp_out = paired(jnp.concatenate(near, axis=0) + far)
     branch = jnp.concatenate(branch, axis=0)
@@ -959,8 +960,8 @@
     part, attn_gain_sum = norm_back(grad_normed, unit_attn, scale_attn, gain_attn)
     input_grad = (jnp.concatenate(grad_resid, axis=0) + part).reshape(inputs.shape)
 
-    stat_sum = tree_sum(stats, "fsdp")
-    gain_sum = tree_sum(tree_sum(jnp.stack([attn_gain_sum, mlp_gain_sum]), "tensor"), "fsdp")
+    stat_sum = tree_sum(stats, FSDP)
+    gain_sum = tree_sum(tree_sum(jnp.stack([attn_gain_sum, mlp_gain_sum]), TENSOR), FSDP)
     row_share = model_width // n_fsdp
     own_gain = lax.dynamic_slice_in_dim(gain_sum, fsdp_index * row_share, row_share, 1)
     counts = ((seq_len - own_prefix) * model_width).astype(F32)
@@ -983,32 +984,32 @@
 
 def solution(mesh):
     in_specs = (
-        P(None, "tensor", "fsdp", None),
-        P(None, "tensor", "fsdp", None),
+        P(None, TENSOR, FSDP, None),
+        P(None, TENSOR, FSDP, None),
         P(),
-        P(None, None, "fsdp"),
-        P("fsdp"),
-        P("fsdp", "tensor"),
-        P("fsdp", "tensor"),
-        P("fsdp", "tensor"),
-        P("fsdp", "tensor"),
-        P("fsdp"),
-        P("fsdp", "tensor"),
-        P("fsdp", "tensor"),
-        P("fsdp", "tensor"),
+        P(None, None, FSDP),
+        P(FSDP),
+        P(FSDP, TENSOR),
+        P(FSDP, TENSOR),
+        P(FSDP, TENSOR),
+        P(FSDP, TENSOR),
+        P(FSDP),
+        P(FSDP, TENSOR),
+        P(FSDP, TENSOR),
+        P(FSDP, TENSOR),
     )
     out_specs = (
-        P(None, "tensor", "fsdp", None),
-        P(None, "tensor", "fsdp", None),
-        P("fsdp"),
-        P("fsdp", "tensor"),
-        P("fsdp", "tensor"),
-        P("fsdp", "tensor"),
-        P("fsdp", "tensor"),
-        P("fsdp"),
-        P("fsdp", "tensor"),
-        P("fsdp", "tensor"),
-        P("fsdp", "tensor"),
-        P(None, "tensor", None),
+        P(None, TENSOR, FSDP, None),
+        P(None, TENSOR, FSDP, None),
+        P(FSDP),
+        P(FSDP, TENSOR),
+        P(FSDP, TENSOR),
+        P(FSDP, TENSOR),
+        P(FSDP, TENSOR),
+        P(FSDP),
+        P(FSDP, TENSOR),
+        P(FSDP, TENSOR),
+        P(FSDP, TENSOR),
+        P(None, TENSOR, None),
     )
     return jax.shard_map(layer, mesh=mesh, in_specs=in_specs, out_specs=out_specs, check_vma=False)

time: 1230 us -> 1190 us (0.967)
  waiting for transfers between devices: 699 us -> 656 us
    all_to_all x6, waiting for transfers between devices: 130 us -> 105 us  [the longest x3 73.8 us: to_heads(): return lax.all_to_all(packed, FSDP, split_axis=0, concat_axis=0, tiled=True)]
    ppermute x56 -> x57, waiting for transfers between devices: 551 us -> 538 us  [swap(): return lax.ppermute(value, axis, [(a, a ^ distance) for a in range(count)])]
    ppermute x56 -> x57, starting transfers between devices: 59.3 us -> 69.9 us  [swap(): return lax.ppermute(value, axis, [(a, a ^ distance) for a in range(count)])]
    unnamed x182 -> x191, local copies, waits for them, and re-layouts: 48.6 us -> 39.7 us
  transfers between devices with their start and end apart: 71 -> 72, of which waited for: 42 -> 39; matrix products, arithmetic and copies ran while one was open for 12% -> 12% of each run, Pallas kernels for 19% -> 19%
where the time goes in v4:
time: 1190 us; the launch traced here: 1180 us
  waiting for transfers between devices  656 us (55%)
  Pallas kernels  240 us (20%)
  starting transfers between devices  94.6 us (8%)
  local copies, waits for them, and re-layouts  61.7 us (5%)
  matrix products  54.1 us (5%)
  other arithmetic  42.3 us (4%)
  between operations  15.3 us (1%)
  blocking collectives  13.5 us (1%)
    ppermute x57, waiting for transfers between devices, swap(): return lax.ppermute(value, axis, [(a, a ^ distance) for a in range(count)])  538 us
    all_to_all x3, waiting for transfers between devices, to_heads(): return lax.all_to_all(packed, FSDP, split_axis=0, concat_axis=0, tiled=True)  73.8 us
    ppermute x57, starting transfers between devices, swap(): return lax.ppermute(value, axis, [(a, a ^ distance) for a in range(count)])  69.9 us
    pallas_call x4, Pallas kernels, to_peers(): pl.pallas_call(functools.partial(to_peers_kernel, terms, micros), grid=(w...  54.2 us
    dot_general x4, matrix products, dot(): lax.dot_general(left, right, (((left_dim,), (right_dim,)), ((), ())), pre...  54.1 us
    unnamed x191, local copies, waits for them, and re-layouts  39.7 us
    pallas_call x2, Pallas kernels, attend_back(): pl.pallas_call(backward_kernel, out_shape=jax.ShapeDtypeStruct(grad_shape...  37.2 us
    pallas_call x2, Pallas kernels, attend_forward(): pl.pallas_call(forward_kernel, out_shape=(jax.ShapeDtypeStruct(out_shape,...  36.2 us
  transfers between devices with their start and end apart: 72, of which 39 were waited for; matrix products, arithmetic and copies ran while one was open for 12% of the time, Pallas kernels for 19%

profile of v4, /device:TPU:0, one launch (start us, length us, event | category | flops | bytes accessed | tf_op | source)
XLA Modules:
  0.0 1176.8 jit_solution(1278591359473771671)
XLA Ops:
  28.2 21.7 %collective-permute-done.1.refs_2_ = bf16[256,2048]{1,0:T(8,128)(2,1)S(1)} collective-permute-done((bf16[256,2048]{1,0:T(8,128)(2,1)S(1)}, bf16[256,2048]{1,0:T(8,128)(2,1)S(1)}, u32[]{:S(2)}, u32[]{:S(2)}) %collective-permute-start.1) | collective-permute-done | bytes 1048608 | tf_op jit(solution)/shard_map/ppermute | solution.py:46
  95.8 53.8 %all-to-all-done.1.x_ref = bf16[8,4,192,128]{3,2,1,0:T(8,128)(2,1)S(1)} async-done(((bf16[8,4,192,128]{3,2,1,0:T(8,128)(2,1)}), bf16[8,4,192,128]{3,2,1,0:T(8,128)(2,1)S(1)}, u32[]{:S(2)}, u32[]{:S(2)}) %all-to-all-start.1) | async-done | bytes 1572896 | tf_op jit(solution)/shard_map/all_to_all | solution.py:725
  159.1 17.7 %shard_map.221 = (bf16[8,4,64,128]{3,2,1,0:T(8,128)(2,1)}, f32[4,1,1024]{2,1,0:T(1,128)}) custom-call(s32[4]{0:T(128)} %get-tuple-element.273.prefix_ref, bf16[8,4,192,128]{3,2,1,0:T(8,128)(2,1)} %copy-done.6), custom_call_target="tpu_custom_call" | custom-call | tf_op jit(solution)/shard_map/pallas_call | solution.py:315
  176.8 14.2 %all-to-all-done.x_ref = bf16[8,4,192,128]{3,2,1,0:T(8,128)(2,1)S(1)} async-done(((bf16[8,4,192,128]{3,2,1,0:T(8,128)(2,1)}), bf16[8,4,192,128]{3,2,1,0:T(8,128)(2,1)S(1)}, u32[]{:S(2)}, u32[]{:S(2)}) %all-to-all-start) | async-done | bytes 1572896 | tf_op jit(solution)/shard_map/all_to_all | solution.py:725
  192.2 18.5 %shard_map.222 = (bf16[8,4,64,128]{3,2,1,0:T(8,128)(2,1)}, f32[4,1,1024]{2,1,0:T(1,128)}) custom-call(s32[4]{0:T(128)} %get-tuple-element.272.prefix_ref, bf16[8,4,192,128]{3,2,1,0:T(8,128)(2,1)} %copy-done.5), custom_call_target="tpu_custom_call" | custom-call | tf_op jit(solution)/shard_map/pallas_call | solution.py:315
  220.4 22.6 %all-to-all-done.2.x_ref = bf16[8,8,64,128]{3,2,1,0:T(8,128)(2,1)S(1)} async-done(((bf16[8,8,64,128]{3,2,1,0:T(8,128)(2,1)}), bf16[8,8,64,128]{3,2,1,0:T(8,128)(2,1)S(1)}, u32[]{:S(2)}, u32[]{:S(2)}) %all-to-all-start.2) | async-done | bytes 1048608 | tf_op jit(solution)/shard_map/all_to_all | solution.py:729
  323.5 39.4 %collective-permute-done.21 = bf16[256,2048]{1,0:T(8,128)(2,1)S(1)} collective-permute-done((bf16[256,2048]{1,0:T(8,128)(2,1)S(1)}, bf16[256,2048]{1,0:T(8,128)(2,1)S(1)}, u32[]{:S(2)}, u32[]{:S(2)}) %collective-permute-start.21) | collective-permute-done | bytes 1048608 | tf_op jit(solution)/shard_map/ppermute | solution.py:46
  372.3 106.0 %collective-permute-done.12 = bf16[256,2048]{1,0:T(8,128)(2,1)} collective-permute-done((bf16[256,2048]{1,0:T(8,128)(2,1)}, bf16[256,2048]{1,0:T(8,128)(2,1)}, u32[]{:S(2)}, u32[]{:S(2)}) %collective-permute-start.12) | collective-permute-done | bytes 1048608 | tf_op jit(solution)/shard_map/ppermute | solution.py:46
  497.0 19.0 %collective-permute-done.13 = bf16[128,2048]{1,0:T(8,128)(2,1)S(1)} collective-permute-done((bf16[128,2048]{1,0:T(8,128)(2,1)S(1)}, bf16[128,2048]{1,0:T(8,128)(2,1)S(1)}, u32[]{:S(2)}, u32[]{:S(2)}) %collective-permute-start.13) | collective-permute-done | bytes 524320 | tf_op jit(solution)/shard_map/ppermute | solution.py:46
  530.5 13.9 %shard_map.228 = (f32[1024,1024]{1,0:T(8,128)}, f32[1024,1024]{1,0:T(8,128)}, bf16[1024,1024]{1,0:T(8,128)(2,1)}) custom-call(bf16[1024,2048]{1,0:T(8,128)(2,1)} %copy-done.15, bf16[2048,1024]{1,0:T(8,128)(2,1)} %all-gather.10.cloned.1.call-done.wg_ref.refs_2_, bf16[2048,1024]{1,0:T(8,128)(2,1)} %all-gather.12.cloned.1.call-done.wu_ref.refs_3_), custom_call_target="tpu_custom_call" | custom-call | tf_op jit(solution)/shard_map/pallas_call | solution.py:386
  544.5 14.1 %shard_map.229 = (f32[1024,1024]{1,0:T(8,128)}, f32[1024,1024]{1,0:T(8,128)}, bf16[1024,1024]{1,0:T(8,128)(2,1)}) custom-call(bf16[1024,2048]{1,0:T(8,128)(2,1)} %constant_dynamic-update-slice_fusion.7.x_ref, bf16[2048,1024]{1,0:T(8,128)(2,1)} %all-gather.10.cloned.1.call-done.wg_ref.refs_2_, bf16[2048,1024]{1,0:T(8,128)(2,1)} %all-gather.12.cloned.1.call-done.wu_ref.refs_3_), custom_call_target="tpu_custom_call" | custom-call | tf_op jit(solution)/shard_map/pallas_call | solution.py:386
  587.9 14.0 %shard_map.231 = (f32[256,2048]{1,0:T(8,128)}, bf16[256,2048]{1,0:T(8,128)(2,1)}, bf16[256,2048]{1,0:T(8,128)(2,1)}, bf16[256,2048]{1,0:T(8,128)(2,1)}) custom-call(bf16[1024,1024]{1,0:T(8,128)(2,1)} %get-tuple-element.162.refs_0_, bf16[1024,1024]{1,0:T(8,128)(2,1)} %get-tuple-element.163.refs_1_, ...), custom_call_target="tpu_custom_call" | custom-call | tf_op jit(solution)/shard_map/pallas_call | solution.py:447
  613.1 13.9 %shard_map.233 = (f32[256,2048]{1,0:T(8,128)}, bf16[256,2048]{1,0:T(8,128)(2,1)}, bf16[256,2048]{1,0:T(8,128)(2,1)}, bf16[256,2048]{1,0:T(8,128)(2,1)}) custom-call(bf16[1024,1024]{1,0:T(8,128)(2,1)} %get-tuple-element.171.refs_0_, bf16[1024,1024]{1,0:T(8,128)(2,1)} %get-tuple-element.172.refs_1_, ...), custom_call_target="tpu_custom_call" | custom-call | tf_op jit(solution)/shard_map/pallas_call | solution.py:447
  627.1 26.0 %fusion.11 = bf16[2048,2048]{1,0:T(8,128)(2,1)} fusion(bf16[1024,1024]{1,0:T(8,128)(2,1)} %get-tuple-element.172.refs_1_, bf16[1024,1024]{1,0:T(8,128)(2,1)} %get-tuple-element.171.refs_0_, bf16[1024,1024]{1,0:T(8,128)(2,1)} %get-tuple-element.163.refs_1_, bf16[1024,1024]{1,0:T(8,128)(2,1)S(1)} %copy-done.46, ...), kind=kOutput, calls=%fused_computation.13 | convolution fusion | flops 17234395136 | bytes 25165824 | tf_op jit(solution)/shard_map/dot_general | solution.py:25
  659.3 21.1 %collective-permute-done.25.refs_1_.refs_5_ = bf16[256,2048]{1,0:T(8,128)(2,1)} collective-permute-done((bf16[256,2048]{1,0:T(8,128)(2,1)S(1)}, bf16[256,2048]{1,0:T(8,128)(2,1)}, u32[]{:S(2)}, u32[]{:S(2)}) %collective-permute-start.25) | collective-permute-done | bytes 1048608 | tf_op jit(solution)/shard_map/ppermute | solution.py:46
  681.4 22.6 %collective-permute-done.26.refs_2_.refs_6_ = bf16[256,2048]{1,0:T(8,128)(2,1)} collective-permute-done((bf16[256,2048]{1,0:T(8,128)(2,1)}, bf16[256,2048]{1,0:T(8,128)(2,1)}, u32[]{:S(2)}, u32[]{:S(2)}) %collective-permute-start.26) | collective-permute-done | bytes 1048608 | tf_op jit(solution)/shard_map/ppermute | solution.py:46
  707.4 17.8 %collective-permute-done.32.refs_1_.refs_5_ = bf16[256,2048]{1,0:T(8,128)(2,1)S(1)} collective-permute-done((bf16[256,2048]{1,0:T(8,128)(2,1)}, bf16[256,2048]{1,0:T(8,128)(2,1)S(1)}, u32[]{:S(2)}, u32[]{:S(2)}) %collective-permute-start.32) | collective-permute-done | bytes 1048608 | tf_op jit(solution)/shard_map/ppermute | solution.py:46
  725.3 19.9 %collective-permute-done.33.refs_2_.refs_6_ = bf16[256,2048]{1,0:T(8,128)(2,1)S(1)} collective-permute-done((bf16[256,2048]{1,0:T(8,128)(2,1)}, bf16[256,2048]{1,0:T(8,128)(2,1)S(1)}, u32[]{:S(2)}, u32[]{:S(2)}) %collective-permute-start.33) | collective-permute-done | bytes 1048608 | tf_op jit(solution)/shard_map/ppermute | solution.py:46
  750.9 26.9 %collective-permute-done.28.far_ref = bf16[128,2048]{1,0:T(8,128)(2,1)} collective-permute-done((bf16[128,2048]{1,0:T(8,128)(2,1)}, bf16[128,2048]{1,0:T(8,128)(2,1)}, u32[]{:S(2)}, u32[]{:S(2)}) %collective-permute-start.28) | collective-permute-done | bytes 524320 | tf_op jit(solution)/shard_map/ppermute | solution.py:46
  873.8 18.3 %shard_map.241 = bf16[8,4,192,128]{3,2,1,0:T(8,128)(2,1)} custom-call(s32[4]{0:T(128)} %get-tuple-element.273.prefix_ref, bf16[8,4,192,128]{3,2,1,0:T(8,128)(2,1)} %copy-done.6, bf16[8,4,64,128]{3,2,1,0:T(8,128)(2,1)} %get-tuple-element.128.o_ref, bf16[8,8,64,128]{3,2,1,0:T(8,128)(2,1)} %copy-done.8, f32[4,1,1024]{2,1,0:T(1,128)} %get-tuple-element.125.lse_ref), custom_call_target="tpu_custom_call" | custom-call | tf_op jit(solution)/shard_map/pallas_call | solution.py:338
  908.4 19.0 %shard_map.240 = bf16[8,4,192,128]{3,2,1,0:T(8,128)(2,1)} custom-call(s32[4]{0:T(128)} %get-tuple-element.272.prefix_ref, bf16[8,4,192,128]{3,2,1,0:T(8,128)(2,1)} %copy-done.5, bf16[8,4,64,128]{3,2,1,0:T(8,128)(2,1)} %get-tuple-element.127.o_ref, bf16[8,8,64,128]{3,2,1,0:T(8,128)(2,1)} %copy-done.8, f32[4,1,1024]{2,1,0:T(1,128)} %get-tuple-element.144.lse_ref), custom_call_target="tpu_custom_call" | custom-call | tf_op jit(solution)/shard_map/pallas_call | solution.py:338
  953.3 41.8 %collective-permute-done.40 = bf16[512,2048]{1,0:T(8,128)(2,1)} collective-permute-done((bf16[512,2048]{1,0:T(8,128)(2,1)}, bf16[512,2048]{1,0:T(8,128)(2,1)}, u32[]{:S(2)}, u32[]{:S(2)}) %collective-permute-start.40) | collective-permute-done | bytes 2097184 | tf_op jit(solution)/shard_map/ppermute | solution.py:46
  1026.4 64.5 %collective-permute-done.53 = bf16[256,1024]{1,0:T(8,128)(2,1)S(1)} collective-permute-done((bf16[256,1024]{1,0:T(8,128)(2,1)S(1)}, bf16[256,1024]{1,0:T(8,128)(2,1)S(1)}, u32[]{:S(2)}, u32[]{:S(2)}) %collective-permute-start.53) | collective-permute-done | bytes 524320 | tf_op jit(solution)/shard_map/ppermute | solution.py:46
  1124.7 18.1 %collective-permute-done.46 = bf16[256,2048]{1,0:T(8,128)(2,1)S(1)} collective-permute-done((bf16[256,2048]{1,0:T(8,128)(2,1)S(1)}, bf16[256,2048]{1,0:T(8,128)(2,1)S(1)}, u32[]{:S(2)}, u32[]{:S(2)}) %collective-permute-start.46) | collective-permute-done | bytes 1048608 | tf_op jit(solution)/shard_map/ppermute | solution.py:46
  (442 shorter events, 496.8 us)
Async XLA Ops:
  7.2 70.5 %all-gather.6.cloned.1.call-start = ((), (), s32[]{:S(2)}) async-start(), calls=%async_computation.10 | async-start | bytes 7077888 | tf_op jit(solution)/shard_map/all_gather | solution.py:773
  95.0 64.1 %all-gather.8.cloned.1.call-start = ((), (), s32[]{:S(2)}) async-start(), calls=%async_computation.11 | async-start | bytes 2359296 | tf_op jit(solution)/shard_map/all_gather | solution.py:773
  156.5 60.1 %collective-permute-start.15 = (bf16[256,3072]{1,0:T(8,128)(2,1)S(1)}, bf16[256,3072]{1,0:T(8,128)(2,1)}, u32[]{:S(2)}, u32[]{:S(2)}) collective-permute-start(bf16[256,3072]{1,0:T(8,128)(2,1)S(1)} %pad_maximum_fusion.1), channel_id=1, source_target_pairs={{0,8},{4,12},{8,0},{12,4},{16,24},{20,28},{24,16},{28,20},{1,9},{5... | collective-permute-start | bytes 4718600 | tf_op jit(solution)/shard_map/ppermute | solution.py:46
  216.5 314.0 %all-gather.10.cloned.1.call-start = ((), (), s32[]{:S(2)}) async-start(), calls=%async_computation.12 | async-start | bytes 5242880 | tf_op jit(solution)/shard_map/all_gather | solution.py:149
  243.0 287.5 %all-gather.12.cloned.1.call-start = ((), (), s32[]{:S(2)}) async-start(), calls=%async_computation.13 | async-start | bytes 5242880 | tf_op jit(solution)/shard_map/all_gather | solution.py:149
  323.1 252.4 %all-gather.14.cloned.1.call-start = ((), (), s32[]{:S(2)}) async-start(), calls=%async_computation.14 | async-start | bytes 5242880 | tf_op jit(solution)/shard_map/all_gather | solution.py:149
  363.1 118.6 %collective-permute-start.24 = (bf16[512,2048]{1,0:T(8,128)(2,1)S(1)}, bf16[512,2048]{1,0:T(8,128)(2,1)}, u32[]{:S(2)}, u32[]{:S(2)}) collective-permute-start(bf16[512,2048]{1,0:T(8,128)(2,1)S(1)} %pad_maximum_fusion), channel_id=1, source_target_pairs={{0,3},{1,2},{2,1},{3,0},{4,7},{5,6},{6,5},{7,4},{8,11},{9,10},{10,... | collective-permute-start | bytes 6291464 | tf_op jit(solution)/shard_map/ppermute | solution.py:46
  365.8 117.3 %collective-permute-start.23 = (bf16[512,2048]{1,0:T(8,128)(2,1)S(1)}, bf16[512,2048]{1,0:T(8,128)(2,1)}, u32[]{:S(2)}, u32[]{:S(2)}) collective-permute-start(bf16[512,2048]{1,0:T(8,128)(2,1)S(1)} %pad_maximum_fusion), channel_id=1, source_target_pairs={{0,2},{1,3},{2,0},{3,1},{4,6},{5,7},{6,4},{7,5},{8,10},{9,11},{10,... | collective-permute-start | bytes 6291464 | tf_op jit(solution)/shard_map/ppermute | solution.py:46
  366.3 116.8 %collective-permute-start.22 = (bf16[512,2048]{1,0:T(8,128)(2,1)S(1)}, bf16[512,2048]{1,0:T(8,128)(2,1)}, u32[]{:S(2)}, u32[]{:S(2)}) collective-permute-start(bf16[512,2048]{1,0:T(8,128)(2,1)S(1)} %pad_maximum_fusion), channel_id=1, source_target_pairs={{0,1},{1,0},{2,3},{3,2},{4,5},{5,4},{6,7},{7,6},{8,9},{9,8},{10,11... | collective-permute-start | bytes 6291464 | tf_op jit(solution)/shard_map/ppermute | solution.py:46
  366.7 111.7 %collective-permute-start.12 = (bf16[256,2048]{1,0:T(8,128)(2,1)}, bf16[256,2048]{1,0:T(8,128)(2,1)}, u32[]{:S(2)}, u32[]{:S(2)}) collective-permute-start(bf16[256,2048]{1,0:T(8,128)(2,1)} %shard_map.226), channel_id=1, source_target_pairs={{0,2},{1,3},{2,0},{3,1},{4,6},{5,7},{6,4},{7,5},{8,10},{9,11},{10,... | collective-permute-start | bytes 3145736 | tf_op jit(solution)/shard_map/ppermute | solution.py:46
  368.4 110.1 %collective-permute-start.11 = (bf16[256,2048]{1,0:T(8,128)(2,1)}, bf16[256,2048]{1,0:T(8,128)(2,1)}, u32[]{:S(2)}, u32[]{:S(2)}) collective-permute-start(bf16[256,2048]{1,0:T(8,128)(2,1)} %shard_map.226), channel_id=1, source_target_pairs={{0,1},{1,0},{2,3},{3,2},{4,5},{5,4},{6,7},{7,6},{8,9},{9,8},{10,11... | collective-permute-start | bytes 3145736 | tf_op jit(solution)/shard_map/ppermute | solution.py:46
  370.9 282.1 %reduce-scatter.5.cloned.1.call-start = ((), (), s32[]{:S(2)}) async-start(), calls=%async_computation.15 | async-start | bytes 5242880 | tf_op jit(solution)/shard_map/reduce_scatter | solution.py:159
  575.3 291.7 %reduce-scatter.7.cloned.1.call-start = ((), (), s32[]{:S(2)}) async-start(), calls=%async_computation.16 | async-start | bytes 10485760 | tf_op jit(solution)/shard_map/reduce_scatter | solution.py:159
  657.7 67.5 %collective-permute-start.32 = (bf16[256,2048]{1,0:T(8,128)(2,1)}, bf16[256,2048]{1,0:T(8,128)(2,1)S(1)}, u32[]{:S(2)}, u32[]{:S(2)}) collective-permute-start(bf16[256,2048]{1,0:T(8,128)(2,1)} %get-tuple-element.174), channel_id=1, source_target_pairs={{0,1},{1,0},{2,3},{3,2},{4,5},{5,4},{6,7},{7,6},{8,9},{9,8},{10,11... | collective-permute-start | bytes 3145736 | tf_op jit(solution)/shard_map/ppermute | solution.py:46
  658.6 86.5 %collective-permute-start.33 = (bf16[256,2048]{1,0:T(8,128)(2,1)}, bf16[256,2048]{1,0:T(8,128)(2,1)S(1)}, u32[]{:S(2)}, u32[]{:S(2)}) collective-permute-start(bf16[256,2048]{1,0:T(8,128)(2,1)} %get-tuple-element.175), channel_id=1, source_target_pairs={{0,2},{1,3},{2,0},{3,1},{4,6},{5,7},{6,4},{7,5},{8,10},{9,11},{10,... | collective-permute-start | bytes 3145736 | tf_op jit(solution)/shard_map/ppermute | solution.py:46
  680.4 64.8 %collective-permute-start.34 = (bf16[256,2048]{1,0:T(8,128)(2,1)}, bf16[256,2048]{1,0:T(8,128)(2,1)S(1)}, u32[]{:S(2)}, u32[]{:S(2)}) collective-permute-start(bf16[256,2048]{1,0:T(8,128)(2,1)} %get-tuple-element.176), channel_id=1, source_target_pairs={{0,3},{1,2},{2,1},{3,0},{4,7},{5,6},{6,5},{7,4},{8,11},{9,10},{10,... | collective-permute-start | bytes 3145736 | tf_op jit(solution)/shard_map/ppermute | solution.py:46
  846.3 60.3 %reduce-scatter.9.cloned.1.call-start = ((), (), s32[]{:S(2)}) async-start(), calls=%async_computation.17 | async-start | bytes 2359296 | tf_op jit(solution)/shard_map/reduce_scatter | solution.py:776
  903.9 91.1 %collective-permute-start.40 = (bf16[512,2048]{1,0:T(8,128)(2,1)}, bf16[512,2048]{1,0:T(8,128)(2,1)}, u32[]{:S(2)}, u32[]{:S(2)}) collective-permute-start(bf16[512,2048]{1,0:T(8,128)(2,1)} %get-tuple-element.204), channel_id=1, source_target_pairs={{0,2},{1,3},{2,0},{3,1},{4,6},{5,7},{6,4},{7,5},{8,10},{9,11},{10,... | collective-permute-start | bytes 6291464 | tf_op jit(solution)/shard_map/ppermute | solution.py:46
  904.6 92.1 %collective-permute-start.41 = (bf16[512,2048]{1,0:T(8,128)(2,1)}, bf16[512,2048]{1,0:T(8,128)(2,1)}, u32[]{:S(2)}, u32[]{:S(2)}) collective-permute-start(bf16[512,2048]{1,0:T(8,128)(2,1)} %get-tuple-element.205), channel_id=1, source_target_pairs={{0,3},{1,2},{2,1},{3,0},{4,7},{5,6},{6,5},{7,4},{8,11},{9,10},{10,... | collective-permute-start | bytes 6291464 | tf_op jit(solution)/shard_map/ppermute | solution.py:46
  935.5 69.7 %all-to-all-start.4 = ((bf16[8,4,192,128]{3,2,1,0:T(8,128)(2,1)}), bf16[8,4,192,128]{3,2,1,0:T(8,128)(2,1)}, u32[]{:S(2)}, u32[]{:S(2)}) async-start(bf16[8,4,192,128]{3,2,1,0:T(8,128)(2,1)} %shard_map.240), calls=%async_computation.7 | async-start | bytes 3145728 | tf_op jit(solution)/shard_map/all_to_all | solution.py:729
  939.8 228.0 %reduce-scatter.11.cloned.1.call-start = ((), (), s32[]{:S(2)}) async-start(), calls=%async_computation.18 | async-start | bytes 7077888 | tf_op jit(solution)/shard_map/reduce_scatter | solution.py:776
  951.4 140.3 %collective-permute-start.52 = (bf16[256,2048]{1,0:T(8,128)(2,1)}, bf16[256,2048]{1,0:T(8,128)(2,1)}, u32[]{:S(2)}, u32[]{:S(2)}) collective-permute-start(bf16[256,2048]{1,0:T(8,128)(2,1)} %constant_dynamic-slice_fusion.2), channel_id=1, source_target_pairs={{0,8},{4,12},{8,0},{12,4},{16,24},{20,28},{24,16},{28,20},{1,9},{5... | collective-permute-start | bytes 3145736 | tf_op jit(solution)/shard_map/ppermute | solution.py:46
  1023.1 84.3 %collective-permute-start.42 = (bf16[256,2048]{1,0:T(8,128)(2,1)}, bf16[256,2048]{1,0:T(8,128)(2,1)}, u32[]{:S(2)}, u32[]{:S(2)}) collective-permute-start(bf16[256,2048]{1,0:T(8,128)(2,1)} %pad_maximum_fusion.6), channel_id=1, source_target_pairs={{0,8},{4,12},{8,0},{12,4},{16,24},{20,28},{24,16},{28,20},{1,9},{5... | collective-permute-start | bytes 3145736 | tf_op jit(solution)/shard_map/ppermute | solution.py:46
  1024.8 66.1 %collective-permute-start.53 = (bf16[256,1024]{1,0:T(8,128)(2,1)S(1)}, bf16[256,1024]{1,0:T(8,128)(2,1)S(1)}, u32[]{:S(2)}, u32[]{:S(2)}) collective-permute-start(bf16[256,1024]{1,0:T(8,128)(2,1)S(1)} %constant_dynamic-slice_fusion.1), channel_id=1, source_target_pairs={{0,8},{4,12},{8,0},{12,4},{16,24},{20,28},{24,16},{28,20},{1,9},{5... | collective-permute-start | bytes 1572872 | tf_op jit(solution)/shard_map/ppermute | solution.py:46
  (118 other events, 1985.6 us)
Sparse Core Ops, SparseCore 0:
  10.2 67.4 all-gather.5
  97.5 50.8 all-gather.7
  243.2 56.8 all-gather.9
  323.3 56.8 all-gather.11
  381.6 56.8 all-gather.13
  575.4 65.5 reduce-scatter.4
  653.2 114.7 reduce-scatter.6
  867.1 37.6 reduce-scatter.8
  1020.7 100.3 reduce-scatter.10

commit v5 on v4

--- a/solution.py
+++ b/solution.py
@@ -173,14 +173,6 @@
         ).astype(F32)
         for i in range(pieces)
     ]
-
-
-def tree_sum(value, axis):
-    step = 1
-    while step < lax.axis_size(axis):
-        value = value + swap(value, axis, step)
-        step *= 2
-    return value
 
 
 def span_block(ref, first, count, lo, hi):
@@ -868,10 +860,9 @@
     mlp_rows, first = [], None
     for m in micros:
         blocks = spread(joined[m] if first is None else after(joined[m], first), False)
-        if first is None:
-            first = blocks[1:3]
-            grad_rows = gather_rows(after(grad_blocks, first), micro_count)
+        first = blocks[1:3]
         mlp_rows.append(gather_rows(blocks, 1))
+    grad_rows = gather_rows(after(grad_blocks, first), micro_count)
 
     hidden, gate_val, up_val = [], [], []
     for m in micros:
@@ -937,7 +928,7 @@
     (own_down,) = settle_half(part_down, side, 1, qkv_grad)
     part = to_peers([after(grad_qkv, qkv_grad)], [full_qkv], micro_count, n_tensor)
     grad_normed = collect(part, False)
-    far = after(far, part).astype(F32)
+    far = after(far, grad_normed).astype(F32)
     mlp_out = paired(jnp.concatenate(near, axis=0) + far)
     branch = jnp.concatenate(branch, axis=0)
     result = jnp.concatenate(resid, axis=0) + mlp_out
@@ -960,10 +951,19 @@
     part, attn_gain_sum = norm_back(grad_normed, unit_attn, scale_attn, gain_attn)
     input_grad = (jnp.concatenate(grad_resid, axis=0) + part).reshape(inputs.shape)
 
-    stat_sum = tree_sum(stats, FSDP)
-    gain_sum = tree_sum(tree_sum(jnp.stack([attn_gain_sum, mlp_gain_sum]), TENSOR), FSDP)
+    gain_cols = jnp.stack([attn_gain_sum, mlp_gain_sum], axis=0).reshape(2, n_fsdp, -1)
     row_share = model_width // n_fsdp
-    own_gain = lax.dynamic_slice_in_dim(gain_sum, fsdp_index * row_share, row_share, 1)
+    stat_row = jnp.broadcast_to(stats.reshape(1, -1), (n_fsdp, stats.size))
+    pad = -stats.size % 128
+    small = jnp.concatenate(
+        [gain_cols[0], gain_cols[1], stat_row, jnp.zeros((n_fsdp, pad), F32)], axis=1
+    )
+    small = lax.all_to_all(small, FSDP, split_axis=0, concat_axis=0, tiled=True)
+    small = jnp.sum(small, axis=0)
+    own_gain = small[: 2 * row_share]
+    own_gain = sum([own_gain] + [swap(own_gain, TENSOR, k) for k in range(1, n_tensor)])
+    own_gain = own_gain.reshape(2, row_share)
+    stat_sum = small[2 * row_share : 2 * row_share + stats.size].reshape(stats.shape)
     counts = ((seq_len - own_prefix) * model_width).astype(F32)
     rms_stats = jnp.sqrt(stat_sum / counts[..., None] + stat_eps)
     return (

time: 1190 us -> 1140 us (0.958)
  waiting for transfers between devices: 656 us -> 598 us
  local copies, waits for them, and re-layouts: 61.7 us -> 75.1 us
    ppermute x57 -> x52, waiting for transfers between devices: 538 us -> 454 us  [swap(): return lax.ppermute(value, axis, [(a, a ^ distance) for a in range(count)])]
    all_to_all x3, waiting for transfers between devices: 30.7 us -> 51.3 us  [to_spans(): lax.all_to_all(packed, FSDP, split_axis=0, concat_axis=0, tiled=True)]
    unnamed x191 -> x190, local copies, waits for them, and re-layouts: 39.7 us -> 51.1 us
    ppermute x57 -> x52, starting transfers between devices: 69.9 us -> 63.2 us  [swap(): return lax.ppermute(value, axis, [(a, a ^ distance) for a in range(count)])]
  transfers between devices with their start and end apart: 72 -> 68, of which waited for: 39 -> 38; matrix products, arithmetic and copies ran while one was open for 12% -> 13% of each run, Pallas kernels for 19% -> 20%
where the time goes in v5:
time: 1140 us; the launch traced here: 1130 us
  waiting for transfers between devices  598 us (52%)
  Pallas kernels  239 us (21%)
  starting transfers between devices  91.3 us (8%)
  local copies, waits for them, and re-layouts  75.1 us (7%)
  matrix products  54 us (5%)
  other arithmetic  38.9 us (3%)
  between operations  15.5 us (1%)
  blocking collectives  13.5 us (1%)
    ppermute x52, waiting for transfers between devices, swap(): return lax.ppermute(value, axis, [(a, a ^ distance) for a in range(count)])  454 us
    all_to_all x3, waiting for transfers between devices, to_heads(): return lax.all_to_all(packed, FSDP, split_axis=0, concat_axis=0, tiled=True)  73.8 us
    ppermute x52, starting transfers between devices, swap(): return lax.ppermute(value, axis, [(a, a ^ distance) for a in range(count)])  63.2 us
    dot_general x4, matrix products, dot(): lax.dot_general(left, right, (((left_dim,), (right_dim,)), ((), ())), pre...  54 us
    pallas_call x4, Pallas kernels, to_peers(): pl.pallas_call(functools.partial(to_peers_kernel, terms, micros), grid=(w...  53.9 us
    all_to_all x3, waiting for transfers between devices, to_spans(): lax.all_to_all(packed, FSDP, split_axis=0, concat_axis=0, tiled=True)  51.3 us
    unnamed x190, local copies, waits for them, and re-layouts  51.1 us
    pallas_call x2, Pallas kernels, attend_back(): pl.pallas_call(backward_kernel, out_shape=jax.ShapeDtypeStruct(grad_shape...  37.3 us
  transfers between devices with their start and end apart: 68, of which 38 were waited for; matrix products, arithmetic and copies ran while one was open for 13% of the time, Pallas kernels for 20%

profile of v5, /device:TPU:0, one launch (start us, length us, event | category | flops | bytes accessed | tf_op | source)
XLA Modules:
  0.0 1125.5 jit_solution(6189745412293221291)
XLA Ops:
  28.2 21.7 %collective-permute-done.1.refs_2_ = bf16[256,2048]{1,0:T(8,128)(2,1)S(1)} collective-permute-done((bf16[256,2048]{1,0:T(8,128)(2,1)S(1)}, bf16[256,2048]{1,0:T(8,128)(2,1)S(1)}, u32[]{:S(2)}, u32[]{:S(2)}) %collective-permute-start.1) | collective-permute-done | bytes 1048608 | tf_op jit(solution)/shard_map/ppermute | solution.py:46
  95.8 53.8 %all-to-all-done.1.x_ref = bf16[8,4,192,128]{3,2,1,0:T(8,128)(2,1)S(1)} async-done(((bf16[8,4,192,128]{3,2,1,0:T(8,128)(2,1)}), bf16[8,4,192,128]{3,2,1,0:T(8,128)(2,1)S(1)}, u32[]{:S(2)}, u32[]{:S(2)}) %all-to-all-start.1) | async-done | bytes 1572896 | tf_op jit(solution)/shard_map/all_to_all | solution.py:717
  159.1 17.7 %shard_map.221 = (bf16[8,4,64,128]{3,2,1,0:T(8,128)(2,1)}, f32[4,1,1024]{2,1,0:T(1,128)}) custom-call(s32[4]{0:T(128)} %get-tuple-element.285.prefix_ref, bf16[8,4,192,128]{3,2,1,0:T(8,128)(2,1)} %copy-done.5), custom_call_target="tpu_custom_call" | custom-call | tf_op jit(solution)/shard_map/pallas_call | solution.py:307
  176.8 14.2 %all-to-all-done.x_ref = bf16[8,4,192,128]{3,2,1,0:T(8,128)(2,1)S(1)} async-done(((bf16[8,4,192,128]{3,2,1,0:T(8,128)(2,1)}), bf16[8,4,192,128]{3,2,1,0:T(8,128)(2,1)S(1)}, u32[]{:S(2)}, u32[]{:S(2)}) %all-to-all-start) | async-done | bytes 1572896 | tf_op jit(solution)/shard_map/all_to_all | solution.py:717
  192.2 18.5 %shard_map.222 = (bf16[8,4,64,128]{3,2,1,0:T(8,128)(2,1)}, f32[4,1,1024]{2,1,0:T(1,128)}) custom-call(s32[4]{0:T(128)} %get-tuple-element.284.prefix_ref, bf16[8,4,192,128]{3,2,1,0:T(8,128)(2,1)} %copy-done.4), custom_call_target="tpu_custom_call" | custom-call | tf_op jit(solution)/shard_map/pallas_call | solution.py:307
  220.4 22.6 %all-to-all-done.2.x_ref = bf16[8,8,64,128]{3,2,1,0:T(8,128)(2,1)S(1)} async-done(((bf16[8,8,64,128]{3,2,1,0:T(8,128)(2,1)}), bf16[8,8,64,128]{3,2,1,0:T(8,128)(2,1)S(1)}, u32[]{:S(2)}, u32[]{:S(2)}) %all-to-all-start.2) | async-done | bytes 1048608 | tf_op jit(solution)/shard_map/all_to_all | solution.py:721
  327.4 35.6 %collective-permute-done.21 = bf16[256,2048]{1,0:T(8,128)(2,1)S(1)} collective-permute-done((bf16[256,2048]{1,0:T(8,128)(2,1)S(1)}, bf16[256,2048]{1,0:T(8,128)(2,1)S(1)}, u32[]{:S(2)}, u32[]{:S(2)}) %collective-permute-start.21) | collective-permute-done | bytes 1048608 | tf_op jit(solution)/shard_map/ppermute | solution.py:46
  374.3 93.1 %collective-permute-done.13 = bf16[128,2048]{1,0:T(8,128)(2,1)} collective-permute-done((bf16[128,2048]{1,0:T(8,128)(2,1)}, bf16[128,2048]{1,0:T(8,128)(2,1)}, u32[]{:S(2)}, u32[]{:S(2)}) %collective-permute-start.13) | collective-permute-done | bytes 524320 | tf_op jit(solution)/shard_map/ppermute | solution.py:46
  472.8 17.8 %collective-permute-done.18 = bf16[256,2048]{1,0:T(8,128)(2,1)S(1)} collective-permute-done((bf16[256,2048]{1,0:T(8,128)(2,1)S(1)}, bf16[256,2048]{1,0:T(8,128)(2,1)S(1)}, u32[]{:S(2)}, u32[]{:S(2)}) %collective-permute-start.18) | collective-permute-done | bytes 1048608 | tf_op jit(solution)/shard_map/ppermute | solution.py:46
  515.5 13.9 %shard_map.228 = (f32[1024,1024]{1,0:T(8,128)}, f32[1024,1024]{1,0:T(8,128)}, bf16[1024,1024]{1,0:T(8,128)(2,1)}) custom-call(bf16[1024,2048]{1,0:T(8,128)(2,1)} %copy-done.12, bf16[2048,1024]{1,0:T(8,128)(2,1)} %all-gather.10.cloned.1.call-done.wg_ref.refs_2_, bf16[2048,1024]{1,0:T(8,128)(2,1)} %all-gather.12.cloned.1.call-done.wu_ref.refs_3_), custom_call_target="tpu_custom_call" | custom-call | tf_op jit(solution)/shard_map/pallas_call | solution.py:378
  529.5 14.1 %shard_map.229 = (f32[1024,1024]{1,0:T(8,128)}, f32[1024,1024]{1,0:T(8,128)}, bf16[1024,1024]{1,0:T(8,128)(2,1)}) custom-call(bf16[1024,2048]{1,0:T(8,128)(2,1)} %constant_dynamic-update-slice_fusion.7.x_ref, bf16[2048,1024]{1,0:T(8,128)(2,1)} %all-gather.10.cloned.1.call-done.wg_ref.refs_2_, bf16[2048,1024]{1,0:T(8,128)(2,1)} %all-gather.12.cloned.1.call-done.wu_ref.refs_3_), custom_call_target="tpu_custom_call" | custom-call | tf_op jit(solution)/shard_map/pallas_call | solution.py:378
  598.1 13.9 %shard_map.233 = (f32[256,2048]{1,0:T(8,128)}, bf16[256,2048]{1,0:T(8,128)(2,1)}, bf16[256,2048]{1,0:T(8,128)(2,1)}, bf16[256,2048]{1,0:T(8,128)(2,1)}) custom-call(bf16[1024,1024]{1,0:T(8,128)(2,1)} %get-tuple-element.171.refs_0_, bf16[1024,1024]{1,0:T(8,128)(2,1)} %get-tuple-element.172.refs_1_, ...), custom_call_target="tpu_custom_call" | custom-call | tf_op jit(solution)/shard_map/pallas_call | solution.py:439
  612.0 25.9 %fusion.11 = bf16[2048,2048]{1,0:T(8,128)(2,1)} fusion(bf16[1024,1024]{1,0:T(8,128)(2,1)} %get-tuple-element.172.refs_1_, bf16[1024,1024]{1,0:T(8,128)(2,1)} %get-tuple-element.171.refs_0_, bf16[1024,1024]{1,0:T(8,128)(2,1)} %get-tuple-element.163.refs_1_, bf16[1024,1024]{1,0:T(8,128)(2,1)S(1)} %copy-done.46, ...), kind=kOutput, calls=%fused_computation.13 | convolution fusion | flops 17234395136 | bytes 25165824 | tf_op jit(solution)/shard_map/dot_general | solution.py:25
  644.3 21.0 %collective-permute-done.25.refs_1_.refs_5_ = bf16[256,2048]{1,0:T(8,128)(2,1)} collective-permute-done((bf16[256,2048]{1,0:T(8,128)(2,1)S(1)}, bf16[256,2048]{1,0:T(8,128)(2,1)}, u32[]{:S(2)}, u32[]{:S(2)}) %collective-permute-start.25) | collective-permute-done | bytes 1048608 | tf_op jit(solution)/shard_map/ppermute | solution.py:46
  666.4 21.6 %collective-permute-done.26.refs_2_.refs_6_ = bf16[256,2048]{1,0:T(8,128)(2,1)} collective-permute-done((bf16[256,2048]{1,0:T(8,128)(2,1)}, bf16[256,2048]{1,0:T(8,128)(2,1)}, u32[]{:S(2)}, u32[]{:S(2)}) %collective-permute-start.26) | collective-permute-done | bytes 1048608 | tf_op jit(solution)/shard_map/ppermute | solution.py:46
  691.5 18.7 %collective-permute-done.32.refs_1_.refs_5_ = bf16[256,2048]{1,0:T(8,128)(2,1)S(1)} collective-permute-done((bf16[256,2048]{1,0:T(8,128)(2,1)}, bf16[256,2048]{1,0:T(8,128)(2,1)S(1)}, u32[]{:S(2)}, u32[]{:S(2)}) %collective-permute-start.32) | collective-permute-done | bytes 1048608 | tf_op jit(solution)/shard_map/ppermute | solution.py:46
  710.2 18.2 %collective-permute-done.33.refs_2_.refs_6_ = bf16[256,2048]{1,0:T(8,128)(2,1)S(1)} collective-permute-done((bf16[256,2048]{1,0:T(8,128)(2,1)}, bf16[256,2048]{1,0:T(8,128)(2,1)S(1)}, u32[]{:S(2)}, u32[]{:S(2)}) %collective-permute-start.33) | collective-permute-done | bytes 1048608 | tf_op jit(solution)/shard_map/ppermute | solution.py:46
  734.0 27.1 %collective-permute-done.28.far_ref = bf16[128,2048]{1,0:T(8,128)(2,1)} collective-permute-done((bf16[128,2048]{1,0:T(8,128)(2,1)}, bf16[128,2048]{1,0:T(8,128)(2,1)}, u32[]{:S(2)}, u32[]{:S(2)}) %collective-permute-start.28) | collective-permute-done | bytes 524320 | tf_op jit(solution)/shard_map/ppermute | solution.py:46
  835.9 14.0 %shard_map.239 = (f32[512,2048]{1,0:T(8,128)}, bf16[512,2048]{1,0:T(8,128)(2,1)}, bf16[512,2048]{1,0:T(8,128)(2,1)}, bf16[512,2048]{1,0:T(8,128)(2,1)}) custom-call(bf16[2048,1024]{1,0:T(8,128)(2,1)} %copy-done.10, bf16[2048,1024]{1,0:T(8,128)(2,1)} %all-gather.14.cloned.1.call-done.wd_ref.refs_1_), custom_call_target="tpu_custom_call" | custom-call | tf_op jit(solution)/shard_map/pallas_call | solution.py:439
  856.6 18.3 %shard_map.241 = bf16[8,4,192,128]{3,2,1,0:T(8,128)(2,1)} custom-call(s32[4]{0:T(128)} %get-tuple-element.285.prefix_ref, bf16[8,4,192,128]{3,2,1,0:T(8,128)(2,1)} %copy-done.5, bf16[8,4,64,128]{3,2,1,0:T(8,128)(2,1)} %get-tuple-element.128.o_ref, bf16[8,8,64,128]{3,2,1,0:T(8,128)(2,1)} %copy-done.7, f32[4,1,1024]{2,1,0:T(1,128)} %get-tuple-element.125.lse_ref), custom_call_target="tpu_custom_call" | custom-call | tf_op jit(solution)/shard_map/pallas_call | solution.py:330
  889.5 19.0 %shard_map.240 = bf16[8,4,192,128]{3,2,1,0:T(8,128)(2,1)} custom-call(s32[4]{0:T(128)} %get-tuple-element.284.prefix_ref, bf16[8,4,192,128]{3,2,1,0:T(8,128)(2,1)} %copy-done.4, bf16[8,4,64,128]{3,2,1,0:T(8,128)(2,1)} %get-tuple-element.127.o_ref, bf16[8,8,64,128]{3,2,1,0:T(8,128)(2,1)} %copy-done.7, f32[4,1,1024]{2,1,0:T(1,128)} %get-tuple-element.144.lse_ref), custom_call_target="tpu_custom_call" | custom-call | tf_op jit(solution)/shard_map/pallas_call | solution.py:330
  941.3 19.0 %all-to-all-done.4.ref = bf16[8,4,192,128]{3,2,1,0:T(8,128)(2,1)} async-done(((bf16[8,4,192,128]{3,2,1,0:T(8,128)(2,1)}), bf16[8,4,192,128]{3,2,1,0:T(8,128)(2,1)}, u32[]{:S(2)}, u32[]{:S(2)}) %all-to-all-start.4) | async-done | bytes 1572896 | tf_op jit(solution)/shard_map/all_to_all | solution.py:721
  980.1 45.2 %collective-permute-done.40 = bf16[512,2048]{1,0:T(8,128)(2,1)} collective-permute-done((bf16[512,2048]{1,0:T(8,128)(2,1)}, bf16[512,2048]{1,0:T(8,128)(2,1)}, u32[]{:S(2)}, u32[]{:S(2)}) %collective-permute-start.40) | collective-permute-done | bytes 2097184 | tf_op jit(solution)/shard_map/ppermute | solution.py:46
  1069.8 15.7 %collective-permute-done.46 = bf16[256,2048]{1,0:T(8,128)(2,1)S(1)} collective-permute-done((bf16[256,2048]{1,0:T(8,128)(2,1)S(1)}, bf16[256,2048]{1,0:T(8,128)(2,1)S(1)}, u32[]{:S(2)}, u32[]{:S(2)}) %collective-permute-start.46) | collective-permute-done | bytes 1048608 | tf_op jit(solution)/shard_map/ppermute | solution.py:46
  (439 shorter events, 509.4 us)
Async XLA Ops:
  7.2 70.5 %all-gather.6.cloned.1.call-start = ((), (), s32[]{:S(2)}) async-start(), calls=%async_computation.11 | async-start | bytes 7077888 | tf_op jit(solution)/shard_map/all_gather | solution.py:765
  91.4 58.2 %all-to-all-start.1 = ((bf16[8,4,192,128]{3,2,1,0:T(8,128)(2,1)}), bf16[8,4,192,128]{3,2,1,0:T(8,128)(2,1)S(1)}, u32[]{:S(2)}, u32[]{:S(2)}) async-start(bf16[8,4,192,128]{3,2,1,0:T(8,128)(2,1)} %get-tuple-element.123), calls=%async_computation.1 | async-start | bytes 3145728 | tf_op jit(solution)/shard_map/all_to_all | solution.py:717
  95.0 64.1 %all-gather.8.cloned.1.call-start = ((), (), s32[]{:S(2)}) async-start(), calls=%async_computation.12 | async-start | bytes 2359296 | tf_op jit(solution)/shard_map/all_gather | solution.py:765
  156.5 60.1 %collective-permute-start.15 = (bf16[256,3072]{1,0:T(8,128)(2,1)S(1)}, bf16[256,3072]{1,0:T(8,128)(2,1)}, u32[]{:S(2)}, u32[]{:S(2)}) collective-permute-start(bf16[256,3072]{1,0:T(8,128)(2,1)S(1)} %pad_maximum_fusion.1), channel_id=1, source_target_pairs={{0,8},{4,12},{8,0},{12,4},{16,24},{20,28},{24,16},{28,20},{1,9},{5... | collective-permute-start | bytes 4718600 | tf_op jit(solution)/shard_map/ppermute | solution.py:46
  216.5 299.0 %all-gather.10.cloned.1.call-start = ((), (), s32[]{:S(2)}) async-start(), calls=%async_computation.13 | async-start | bytes 5242880 | tf_op jit(solution)/shard_map/all_gather | solution.py:149
  243.1 272.5 %all-gather.12.cloned.1.call-start = ((), (), s32[]{:S(2)}) async-start(), calls=%async_computation.14 | async-start | bytes 5242880 | tf_op jit(solution)/shard_map/all_gather | solution.py:149
  323.2 237.5 %all-gather.14.cloned.1.call-start = ((), (), s32[]{:S(2)}) async-start(), calls=%async_computation.15 | async-start | bytes 5242880 | tf_op jit(solution)/shard_map/all_gather | solution.py:149
  363.2 129.1 %collective-permute-start.24 = (bf16[512,2048]{1,0:T(8,128)(2,1)S(1)}, bf16[512,2048]{1,0:T(8,128)(2,1)}, u32[]{:S(2)}, u32[]{:S(2)}) collective-permute-start(bf16[512,2048]{1,0:T(8,128)(2,1)S(1)} %pad_maximum_fusion), channel_id=1, source_target_pairs={{0,3},{1,2},{2,1},{3,0},{4,7},{5,6},{6,5},{7,4},{8,11},{9,10},{10,... | collective-permute-start | bytes 6291464 | tf_op jit(solution)/shard_map/ppermute | solution.py:46
  365.9 126.4 %collective-permute-start.23 = (bf16[512,2048]{1,0:T(8,128)(2,1)S(1)}, bf16[512,2048]{1,0:T(8,128)(2,1)}, u32[]{:S(2)}, u32[]{:S(2)}) collective-permute-start(bf16[512,2048]{1,0:T(8,128)(2,1)S(1)} %pad_maximum_fusion), channel_id=1, source_target_pairs={{0,2},{1,3},{2,0},{3,1},{4,6},{5,7},{6,4},{7,5},{8,10},{9,11},{10,... | collective-permute-start | bytes 6291464 | tf_op jit(solution)/shard_map/ppermute | solution.py:46
  366.4 125.9 %collective-permute-start.22 = (bf16[512,2048]{1,0:T(8,128)(2,1)S(1)}, bf16[512,2048]{1,0:T(8,128)(2,1)}, u32[]{:S(2)}, u32[]{:S(2)}) collective-permute-start(bf16[512,2048]{1,0:T(8,128)(2,1)S(1)} %pad_maximum_fusion), channel_id=1, source_target_pairs={{0,1},{1,0},{2,3},{3,2},{4,5},{5,4},{6,7},{7,6},{8,9},{9,8},{10,11... | collective-permute-start | bytes 6291464 | tf_op jit(solution)/shard_map/ppermute | solution.py:46
  367.7 99.7 %collective-permute-start.13 = (bf16[128,2048]{1,0:T(8,128)(2,1)}, bf16[128,2048]{1,0:T(8,128)(2,1)}, u32[]{:S(2)}, u32[]{:S(2)}) collective-permute-start(bf16[128,2048]{1,0:T(8,128)(2,1)} %slice.301), channel_id=1, source_target_pairs={{0,1},{1,0},{2,3},{3,2},{4,5},{5,4},{6,7},{7,6},{8,9},{9,8},{10,11... | collective-permute-start | bytes 1572872 | tf_op jit(solution)/shard_map/ppermute | solution.py:46
  370.2 97.6 %collective-permute-start.14 = (bf16[128,2048]{1,0:T(8,128)(2,1)}, bf16[128,2048]{1,0:T(8,128)(2,1)}, u32[]{:S(2)}, u32[]{:S(2)}) collective-permute-start(bf16[128,2048]{1,0:T(8,128)(2,1)} %slice.302), channel_id=1, source_target_pairs={{0,2},{1,3},{2,0},{3,1},{4,6},{5,7},{6,4},{7,5},{8,10},{9,11},{10,... | collective-permute-start | bytes 1572872 | tf_op jit(solution)/shard_map/ppermute | solution.py:46
  372.8 265.2 %reduce-scatter.5.cloned.1.call-start = ((), (), s32[]{:S(2)}) async-start(), calls=%async_computation.16 | async-start | bytes 5242880 | tf_op jit(solution)/shard_map/reduce_scatter | solution.py:159
  560.2 289.6 %reduce-scatter.7.cloned.1.call-start = ((), (), s32[]{:S(2)}) async-start(), calls=%async_computation.17 | async-start | bytes 10485760 | tf_op jit(solution)/shard_map/reduce_scatter | solution.py:159
  642.6 67.5 %collective-permute-start.32 = (bf16[256,2048]{1,0:T(8,128)(2,1)}, bf16[256,2048]{1,0:T(8,128)(2,1)S(1)}, u32[]{:S(2)}, u32[]{:S(2)}) collective-permute-start(bf16[256,2048]{1,0:T(8,128)(2,1)} %get-tuple-element.174), channel_id=1, source_target_pairs={{0,1},{1,0},{2,3},{3,2},{4,5},{5,4},{6,7},{7,6},{8,9},{9,8},{10,11... | collective-permute-start | bytes 3145736 | tf_op jit(solution)/shard_map/ppermute | solution.py:46
  642.7 85.8 %collective-permute-start.33 = (bf16[256,2048]{1,0:T(8,128)(2,1)}, bf16[256,2048]{1,0:T(8,128)(2,1)S(1)}, u32[]{:S(2)}, u32[]{:S(2)}) collective-permute-start(bf16[256,2048]{1,0:T(8,128)(2,1)} %get-tuple-element.175), channel_id=1, source_target_pairs={{0,2},{1,3},{2,0},{3,1},{4,6},{5,7},{6,4},{7,5},{8,10},{9,11},{10,... | collective-permute-start | bytes 3145736 | tf_op jit(solution)/shard_map/ppermute | solution.py:46
  665.3 63.1 %collective-permute-start.34 = (bf16[256,2048]{1,0:T(8,128)(2,1)}, bf16[256,2048]{1,0:T(8,128)(2,1)S(1)}, u32[]{:S(2)}, u32[]{:S(2)}) collective-permute-start(bf16[256,2048]{1,0:T(8,128)(2,1)} %get-tuple-element.176), channel_id=1, source_target_pairs={{0,3},{1,2},{2,1},{3,0},{4,7},{5,6},{6,5},{7,4},{8,11},{9,10},{10,... | collective-permute-start | bytes 3145736 | tf_op jit(solution)/shard_map/ppermute | solution.py:46
  829.2 58.6 %reduce-scatter.9.cloned.1.call-start = ((), (), s32[]{:S(2)}) async-start(), calls=%async_computation.18 | async-start | bytes 2359296 | tf_op jit(solution)/shard_map/reduce_scatter | solution.py:768
  922.5 193.8 %reduce-scatter.11.cloned.1.call-start = ((), (), s32[]{:S(2)}) async-start(), calls=%async_computation.19 | async-start | bytes 7077888 | tf_op jit(solution)/shard_map/reduce_scatter | solution.py:768
  932.5 92.8 %collective-permute-start.40 = (bf16[512,2048]{1,0:T(8,128)(2,1)}, bf16[512,2048]{1,0:T(8,128)(2,1)}, u32[]{:S(2)}, u32[]{:S(2)}) collective-permute-start(bf16[512,2048]{1,0:T(8,128)(2,1)} %get-tuple-element.204), channel_id=1, source_target_pairs={{0,2},{1,3},{2,0},{3,1},{4,6},{5,7},{6,4},{7,5},{8,10},{9,11},{10,... | collective-permute-start | bytes 6291464 | tf_op jit(solution)/shard_map/ppermute | solution.py:46
  934.0 91.3 %collective-permute-start.41 = (bf16[512,2048]{1,0:T(8,128)(2,1)}, bf16[512,2048]{1,0:T(8,128)(2,1)}, u32[]{:S(2)}, u32[]{:S(2)}) collective-permute-start(bf16[512,2048]{1,0:T(8,128)(2,1)} %get-tuple-element.205), channel_id=1, source_target_pairs={{0,3},{1,2},{2,1},{3,0},{4,7},{5,6},{6,5},{7,4},{8,11},{9,10},{10,... | collective-permute-start | bytes 6291464 | tf_op jit(solution)/shard_map/ppermute | solution.py:46
  935.6 99.8 %collective-permute-start.51 = (bf16[256,1024]{1,0:T(8,128)(2,1)}, bf16[256,1024]{1,0:T(8,128)(2,1)}, u32[]{:S(2)}, u32[]{:S(2)}) collective-permute-start(bf16[256,1024]{1,0:T(8,128)(2,1)} %constant_dynamic-slice_fusion), channel_id=1, source_target_pairs={{0,8},{4,12},{8,0},{12,4},{16,24},{20,28},{24,16},{28,20},{1,9},{5... | collective-permute-start | bytes 1572872 | tf_op jit(solution)/shard_map/ppermute | solution.py:46
  976.9 58.5 %collective-permute-start.50 = (bf16[256,2048]{1,0:T(8,128)(2,1)S(1)}, bf16[256,2048]{1,0:T(8,128)(2,1)S(1)}, u32[]{:S(2)}, u32[]{:S(2)}) collective-permute-start(bf16[256,2048]{1,0:T(8,128)(2,1)S(1)} %constant_dynamic-slice_fusion.1), channel_id=1, source_target_pairs={{0,8},{4,12},{8,0},{12,4},{16,24},{20,28},{24,16},{28,20},{1,9},{5... | collective-permute-start | bytes 3145736 | tf_op jit(solution)/shard_map/ppermute | solution.py:46
  1032.3 57.3 %collective-permute-start.42 = (bf16[256,2048]{1,0:T(8,128)(2,1)}, bf16[256,2048]{1,0:T(8,128)(2,1)}, u32[]{:S(2)}, u32[]{:S(2)}) collective-permute-start(bf16[256,2048]{1,0:T(8,128)(2,1)} %pad_maximum_fusion.6), channel_id=1, source_target_pairs={{0,8},{4,12},{8,0},{12,4},{16,24},{20,28},{24,16},{28,20},{1,9},{5... | collective-permute-start | bytes 3145736 | tf_op jit(solution)/shard_map/ppermute | solution.py:46
  (114 other events, 2117.1 us)
Sparse Core Ops, SparseCore 0:
  10.2 67.4 all-gather.5
  97.5 50.8 all-gather.7
  243.2 56.8 all-gather.9
  323.3 56.8 all-gather.11
  381.6 56.8 all-gather.13
  560.3 65.6 reduce-scatter.4
  638.1 114.9 reduce-scatter.6
  850.0 37.7 reduce-scatter.8
  975.7 108.5 reduce-scatter.10
